TPU v7x, 512 devices: a whole 4x4x16 slice. The times are simulated.
512 devices in a mesh: rep: 4 (over x), tm: 16 (over z), height: 8 (over y, core).
Axes of the slice: x: 4, y: 4, z: 16, core: 2. Of those that a mesh axis runs over, the one named last changes fastest.
Arguments:
- inputs: bfloat16 [4, 64, 128, 32, 128], P('rep', 'tm', 'height'), may hold values from -32 to 32
- spatial_kernel: bfloat16 [3, 3, 128, 128], replicated, may hold values from -0.1875 to 0.1875
- temporal_kernel: bfloat16 [3, 128, 128], replicated, may hold values from -0.3125 to 0.3125
- norm_gain: float32 [128], replicated, may hold values from 0.1 to 1.9
- norm_shift: float32 [128], replicated, may hold values from -3 to 3
- cotangent: bfloat16 [4, 64, 128, 32, 128], P('rep', 'tm', 'height'), may hold values from -6 to 6
Outputs:
- outputs: bfloat16 [4, 64, 128, 32, 128], P('rep', 'tm', 'height')
- grad_inputs: bfloat16 [4, 64, 128, 32, 128], P('rep', 'tm', 'height')
- grad_spatial: float32 [3, 3, 128, 128], replicated
- grad_temporal: float32 [3, 128, 128], replicated
- grad_gain: float32 [128], replicated
- grad_shift: float32 [128], replicated
All inputs are finite; a program needn't handle non-finite values.
Results may differ from a plain program's by a relative error of at most 0.0041.
The roundings to bfloat16 on the way count: a program that leaves them out, or rounds other values in their place, can miss the bound.
Values may be sent and summed in bfloat16 or wider, within the bound.
No kernel may reach another device: no remote copies, remote signals or barrier semaphores. Data moves between devices by JAX's collectives and lax.ppermute only.
A program may use at most 64 MiB of HBM per device.

v0:
```python
import math

import jax
import jax.numpy as jnp
from jax import lax
from jax.sharding import PartitionSpec as P

GROUPS = 32


EPS = 1e-05


def with_halo(value, sides, width):
    for axis, dim in sides:
        count, length = (lax.axis_size(axis), value.shape[dim])
        up = [(i, (i + 1) % count) for i in range(count - 1)]
        down = [(j, i) for i, j in up]
        last = lax.slice_in_dim(value, length - width, length, axis=dim)
        first = lax.slice_in_dim(value, 0, width, axis=dim)
        before = lax.ppermute(last, axis, up)
        after = lax.ppermute(first, axis, down)
        value = jnp.concatenate([before, value, after], axis=dim)
    return value


def from_behind(value, axis, steps):
    count = lax.axis_size(axis)
    first, last = (max(0, -steps), min(count, count - steps))
    return lax.ppermute(value, axis, [(source, source + steps) for source in range(first, last)])


def carried_in(part, axis, combine, identity, reverse):
    count = lax.axis_size(axis)
    place = lax.axis_index(axis)
    ahead = count - 1 - place if reverse else place
    gathered = jax.tree.map(lambda a: lax.all_gather(a, axis), part)
    state = jax.tree.map(lambda a, e: jnp.zeros_like(a) + jnp.asarray(e, a.dtype), part, identity)

    def one(turn, state):
        source = count - 1 - turn if reverse else turn
        return combine(
            state, jax.tree.map(lambda a: lax.dynamic_index_in_dim(a, source, 0, False), gathered)
        )

    return lax.fori_loop(0, ahead, one, state)


def add_pair(earlier, later):
    return (earlier[0] + later[0], earlier[1] + later[1])


def reverse_sum(values):
    return jnp.cumsum(values[::-1], 0)[::-1]


def widen(stat):
    return stat[:, None, None, :, None]


def shards(inputs, spatial_kernel, temporal_kernel, norm_gain, norm_shift, cotangent):
    pixels_in = inputs[0]
    frames, rows, columns, channels = pixels_in.shape
    group_size = channels // GROUPS
    time_devices = lax.axis_size("tm")
    height_devices = lax.axis_size("height")
    frame_start = lax.axis_index("tm") * frames
    per_frame = float(rows * height_devices * columns * group_size)
    halo_in = with_halo(pixels_in, (("height", 1),), 1)
    padded = jnp.pad(halo_in, ((0, 0), (0, 0), (1, 1), (0, 0)))
    total = jnp.zeros((frames, rows, columns, channels), jnp.float32)
    for row_tap in range(3):
        for col_tap in range(3):
            window = padded[:, row_tap : row_tap + rows, col_tap : col_tap + columns]
            total = total + jnp.einsum(
                "frwc,cd->frwd",
                window,
                spatial_kernel[row_tap, col_tap],
                preferred_element_type=jnp.float32,
            )
    feature = total.astype(jnp.bfloat16)
    prior = from_behind(feature[frames - 2 :], "tm", 1)
    earlier = jnp.concatenate([prior, feature], 0)
    mixed = jnp.zeros((frames, rows, columns, channels), jnp.float32)
    for time_tap in range(3):
        mixed = mixed + jnp.einsum(
            "frwc,cd->frwd",
            earlier[time_tap : time_tap + frames],
            temporal_kernel[time_tap],
            preferred_element_type=jnp.float32,
        )
    grouped = mixed.reshape(frames, rows, columns, GROUPS, group_size)
    first = grouped.sum((1, 2, 4))
    second = (grouped * grouped).sum((1, 2, 4))
    row_first, row_second = lax.psum((first, second), "height")
    empty = jnp.zeros((GROUPS,), jnp.float32)
    before = carried_in(
        (row_first.sum(0), row_second.sum(0)), "tm", add_pair, (empty, empty), False
    )
    counted = ((frame_start + jnp.arange(frames)).astype(jnp.float32) + 1.0)[:, None] * per_frame
    mean = (before[0] + jnp.cumsum(row_first, 0)) / counted
    variance = (before[1] + jnp.cumsum(row_second, 0)) / counted - mean * mean
    inv_std = lax.rsqrt(variance + EPS)
    normed = (grouped - widen(mean)) * widen(inv_std)
    gain = norm_gain.reshape(GROUPS, group_size)
    shift = norm_shift.reshape(GROUPS, group_size)
    pre = normed * gain + shift
    sigma = jax.nn.sigmoid(pre)
    outputs = (
        pixels_in.astype(jnp.float32) + (pre * sigma).reshape(frames, rows, columns, channels)
    ).astype(jnp.bfloat16)
    grad_pre = cotangent[0].astype(jnp.float32).reshape(grouped.shape) * (
        sigma * (1.0 + pre * (1.0 - sigma))
    )
    gain_part = (grad_pre * normed).sum((0, 1, 2)).reshape(channels)
    shift_part = grad_pre.sum((0, 1, 2)).reshape(channels)
    grad_normed = grad_pre * gain
    local_a = grad_normed.sum((1, 2, 4))
    local_b = (grad_normed * normed).sum((1, 2, 4))
    sum_a, sum_b = lax.psum((local_a, local_b), "height")
    q_first = (-inv_std * sum_a + inv_std * inv_std * sum_b * mean) / counted
    q_second = -inv_std * inv_std * sum_b / (2.0 * counted)
    zeroed = jnp.zeros((GROUPS,), jnp.float32)
    after = carried_in((q_first.sum(0), q_second.sum(0)), "tm", add_pair, (zeroed, zeroed), True)
    carry_first = after[0] + reverse_sum(q_first)
    carry_second = after[1] + reverse_sum(q_second)
    grad_mixed = (
        widen(inv_std) * grad_normed + widen(carry_first) + 2.0 * grouped * widen(carry_second)
    )
    grad_mixed = grad_mixed.reshape(frames, rows, columns, channels).astype(jnp.bfloat16)
    temporal_terms = []
    for time_tap in range(3):
        temporal_terms.append(
            jnp.einsum(
                "frwc,frwd->cd",
                earlier[time_tap : time_tap + frames],
                grad_mixed,
                preferred_element_type=jnp.float32,
            )
        )
    temporal_part = jnp.stack(temporal_terms)
    following = from_behind(grad_mixed[:2], "tm", -1)
    later = jnp.concatenate([grad_mixed, following], 0)
    grad_feature = jnp.zeros((frames, rows, columns, channels), jnp.float32)
    for time_tap in range(3):
        grad_feature = grad_feature + jnp.einsum(
            "frwd,cd->frwc",
            later[2 - time_tap : 2 - time_tap + frames],
            temporal_kernel[time_tap],
            preferred_element_type=jnp.float32,
        )
    grad_feature = grad_feature.astype(jnp.bfloat16)
    halo_grad = with_halo(grad_feature, (("height", 1),), 1)
    padded_grad = jnp.pad(halo_grad, ((0, 0), (0, 0), (1, 1), (0, 0)))
    grad_in = cotangent[0].astype(jnp.float32)
    spatial_terms = []
    for row_tap in range(3):
        for col_tap in range(3):
            back = padded_grad[
                :, 2 - row_tap : 2 - row_tap + rows, 2 - col_tap : 2 - col_tap + columns
            ]
            grad_in = grad_in + jnp.einsum(
                "frwd,cd->frwc",
                back,
                spatial_kernel[row_tap, col_tap],
                preferred_element_type=jnp.float32,
            )
            window = padded[:, row_tap : row_tap + rows, col_tap : col_tap + columns]
            spatial_terms.append(
                jnp.einsum(
                    "frwc,frwd->cd", window, grad_feature, preferred_element_type=jnp.float32
                )
            )
    spatial_part = jnp.stack(spatial_terms).reshape(3, 3, channels, channels)
    grad_inputs = grad_in.astype(jnp.bfloat16)
    spatial_sum, temporal_sum, gain_sum, shift_sum = lax.psum(
        (spatial_part, temporal_part, gain_part, shift_part), ("rep", "tm", "height")
    )
    pixel_total = lax.axis_size("rep") * frames * time_devices * rows * height_devices * columns
    scale = 1.0 / math.sqrt(pixel_total)
    return (
        outputs[None],
        grad_inputs[None],
        spatial_sum * scale,
        temporal_sum * scale,
        gain_sum * scale,
        shift_sum * scale,
    )


def solution(mesh):
    in_specs = (
        P("rep", "tm", "height", None, None),
        P(),
        P(),
        P(),
        P(),
        P("rep", "tm", "height", None, None),
    )
    out_specs = (
        P("rep", "tm", "height", None, None),
        P("rep", "tm", "height", None, None),
        P(),
        P(),
        P(),
        P(),
    )
    return jax.shard_map(shards, mesh=mesh, in_specs=in_specs, out_specs=out_specs, check_vma=False)
```

profile of v0, /device:TPU:1, one launch (start us, length us, event | category | flops | bytes accessed | tf_op | source)
XLA Modules:
  0.0 734.0 jit_solution(1848081160454730432)
XLA Ops:
  7.2 0.8 fusion.138
  8.0 4.6 collective-permute-start
  12.6 5.5 collective-permute-start.1
  18.1 0.5 fusion.122
  18.6 0.5 fusion.121
  19.2 1.3 dynamic-slice
  21.1 1.4 select_maximum_fusion.2
  22.5 0.3 fusion.52
  22.8 0.7 copy-done
  24.1 0.3 convolution_add_fusion.10
  25.0 0.3 convolution_add_fusion.7
  25.9 1.3 collective-permute-start.2
  27.5 5.4 collective-permute-done.2
  33.1 0.9 multiply_reduce_fusion
  34.1 0.8 reduce_sum.101
  34.9 1.4 reduce_sum.123
  36.3 0.7 reduce_sum.120
  37.0 0.9 reduce_sum.124
  38.0 11.9 %all-reduce.11 = (f32[4,32]{1,0:T(4,128)S(1)}, f32[4,32]{1,0:T(4,128)S(1)}) all-reduce(f32[4,32]{1,0:T(4,128)} %reduce_sum.120, f32[4,32]{1,0:T(4,128)S(1)} %reduce_sum.124), channel_id=1, replica_groups=mesh['rep'=4,'tm'=16,'height'=8] {'height'}, use_global_device_ids=true, to_apply=%region_2.3 | all-reduce | flops 256 | bytes 2048 | tf_op jit(solution)/shard_map/psum | solution.py:95
  50.3 28.4 %all-reduce.9 = (f32[512]{0:T(512)S(1)}, f32[512]{0:T(512)S(1)}) all-reduce(f32[512]{0:T(512)S(1)} %dynamic-update-slice, f32[512]{0:T(512)S(1)} %dynamic-update-slice.1), channel_id=2, replica_groups=mesh['rep'=4,'tm'=16,'height'=8] {'tm'}, use_global_device_ids=true, to_apply=%add.2 | all-reduce | flops 1024 | bytes 8192
  78.9 1.3 add_rsqrt_fusion
  80.2 0.6 copy-done.12
  80.9 0.7 mul.190
  81.6 0.8 sub.44
  82.4 0.7 sub.45
  83.1 1.5 fusion.30
  85.0 20.0 %all-reduce.10 = (f32[4,32]{1,0:T(4,128)S(1)}, f32[4,32]{1,0:T(4,128)S(1)}) all-reduce(f32[4,32]{1,0:T(4,128)S(1)} %reduce_sum.131, f32[4,32]{1,0:T(4,128)S(1)} %reduce_sum.128), channel_id=1, replica_groups=mesh['rep'=4,'tm'=16,'height'=8] {'height'}, use_global_device_ids=true, to_apply=%region_17.18 | all-reduce | flops 256 | bytes 2048 | tf_op jit(solution)/shard_map/psum | solution.py:120
  105.6 21.6 %all-reduce.8 = (f32[512]{0:T(512)S(1)}, f32[512]{0:T(512)S(1)}) all-reduce(f32[512]{0:T(512)S(1)} %dynamic-update-slice.2, f32[512]{0:T(512)S(1)} %dynamic-update-slice.3), channel_id=4, replica_groups=mesh['rep'=4,'tm'=16,'height'=8] {'tm'}, use_global_device_ids=true, to_apply=%add.4 | all-reduce | flops 1024 | bytes 8192
  127.4 0.7 while.27
  128.7 2.7 fusion.28
  131.4 0.3 convolution_bitcast_fusion.4
  131.8 1.3 collective-permute-start.3
  133.1 108.4 %all-reduce.6 = (f32[128]{0:T(128)S(1)}, f32[128]{0:T(128)S(1)}) all-reduce(f32[128]{0:T(128)S(1)} %get-tuple-element.125, f32[128]{0:T(128)S(1)} %get-tuple-element.128), channel_id=1, replica_groups=mesh['rep'=4,'tm'=16,'height'=8] {'rep','tm','height'}, use_global_device_ids=true, to_apply=%region_27.28 | all-reduce | flops 256 | bytes 2048 | tf_op jit(solution)/shard_map/psum | solution.py:176
  241.4 0.5 broadcast_multiply_fusion.2
  241.9 0.3 convolution_bitcast_fusion.1
  242.3 0.3 convolution_bitcast_fusion
  242.6 0.7 pad_maximum_fusion.10
  243.6 1.2 fusion.50
  244.8 1.2 fusion.13
  246.1 0.3 fusion.23
  246.4 0.6 copy-done.4
  247.3 0.3 fusion.16
  247.7 0.3 fusion.22
  248.0 0.3 fusion.21
  248.4 0.3 fusion.20
  248.7 0.3 fusion.19
  249.1 0.3 fusion.18
  249.4 1.9 collective-permute-start.4
  251.3 2.4 collective-permute-start.5
  253.8 0.3 fusion.15
  254.1 0.3 fusion.17
  254.5 0.8 copy-done.7
  255.3 1.3 collective-permute-done.5
  256.6 0.3 select_maximum_fusion
  256.9 0.3 convolution_add_fusion.5
  257.2 0.3 fusion.40
  257.6 0.3 fusion.42
  257.9 0.3 fusion.44
  258.5 0.5 fusion.8
  259.0 0.3 fusion.38
  259.3 1.1 fusion.14
  260.5 464.1 %all-reduce.14.cloned.1.call-done = (f32[3,3,128,128]{3,2,1,0:T(8,128)}, f32[3,128,128]{2,1,0:T(8,128)}) async-done(((f32[3,3,128,128]{3,2,1,0:T(8,128)}, f32[3,128,128]{2,1,0:T(8,128)}), (f32[3,3,128,128]{3,2,1,0:T(8,128)}, f32[3,128,128]{2,1,0:T(8,128)})) %all-reduce.14.cloned.1.call-update) | async-done | bytes 786448 | tf_op jit(solution)/shard_map/psum | solution.py:176
  724.5 2.0 broadcast_multiply_fusion
  726.5 0.7 broadcast_multiply_fusion.1
  (111 shorter events, 6.0 us)
Async XLA Ops:
  7.2 15.3 %copy-start.3 = (bf16[3,3,128,128]{3,2,1,0:T(8,128)(2,1)S(1)}, bf16[3,3,128,128]{3,2,1,0:T(8,128)(2,1)}, u32[]{:S(2)}) copy-start(bf16[3,3,128,128]{3,2,1,0:T(8,128)(2,1)} %param.11) | copy-start | bytes 884740
  7.2 717.4 %all-reduce.14.cloned.1.call-start = ((), (), s32[]{:S(2)}) async-start(), calls=%async_computation | async-start | bytes 1572864 | tf_op jit(solution)/shard_map/psum | solution.py:176
  8.0 13.0 %collective-permute-start = (bf16[4,1,32,128]{3,2,1,0:T(8,128)(2,1)S(1)}, bf16[4,1,32,128]{3,2,1,0:T(8,128)(2,1)S(1)}, u32[]{:S(2)}, u32[]{:S(2)}) collective-permute-start(bf16[4,1,32,128]{3,2,1,0:T(8,128)(2,1)S(1)} %get-tuple-element.181), channel_id=1, source_target_pairs={{0,1},{1,2},{2,3},{3,4},{4,5},{5,6},{6,7},{8,9},{9,10},{10,11},{11... | collective-permute-start | bytes 98312 | tf_op jit(solution)/shard_map/ppermute | solution.py:21
  12.6 8.5 %collective-permute-start.1 = (bf16[4,1,32,128]{3,2,1,0:T(8,128)(2,1)S(1)}, bf16[4,1,32,128]{3,2,1,0:T(8,128)(2,1)S(1)}, u32[]{:S(2)}, u32[]{:S(2)}) collective-permute-start(bf16[4,1,32,128]{3,2,1,0:T(8,128)(2,1)S(1)} %get-tuple-element.182), channel_id=1, source_target_pairs={{1,0},{2,1},{3,2},{4,3},{5,4},{6,5},{7,6},{9,8},{10,9},{11,10},{12... | collective-permute-start | bytes 98312 | tf_op jit(solution)/shard_map/ppermute | solution.py:22
  21.1 1.7 copy-start.10
  22.5 1.0 copy-start
  25.6 1.6 copy-start.8
  25.9 7.0 collective-permute-start.2
  32.9 1.2 copy-start.5
  34.1 49.0 %copy-start.1 = (bf16[1,4,16,32,128]{4,3,2,1,0:T(8,128)(2,1)S(1)}, bf16[1,4,16,32,128]{4,3,2,1,0:T(8,128)(2,1)}, u32[]{:S(2)}) copy-start(bf16[1,4,16,32,128]{4,3,2,1,0:T(8,128)(2,1)} %param.15) | copy-start | bytes 1572868
  80.2 0.6 copy-start.12
  83.1 22.0 %copy-start.13 = (f32[4,32]{1,0:T(4,128)S(1)}, f32[4,32]{1,0:T(4,128)}, u32[]{:S(2)}) copy-start(f32[4,32]{1,0:T(4,128)} %copy-done.12) | copy-start | bytes 1540
  83.1 22.0 %copy-start.14 = (f32[4,32]{1,0:T(4,128)S(1)}, f32[4,32]{1,0:T(4,128)}, u32[]{:S(2)}) copy-start(f32[4,32]{1,0:T(4,128)} %get-tuple-element.172) | copy-start | bytes 1540
  83.1 22.0 %copy-start.19 = (f32[4]{0:T(128)S(1)}, f32[4]{0:T(128)}, u32[]{:S(2)}) copy-start(f32[4]{0:T(128)} %fusion.122) | copy-start | bytes 52
  83.1 22.0 %copy-start.20 = (f32[4]{0:T(128)S(1)}, f32[4]{0:T(128)}, u32[]{:S(2)}) copy-start(f32[4]{0:T(128)} %fusion.121) | copy-start | bytes 52
  83.1 45.6 %copy-start.15 = (f32[4,128]{1,0:T(4,128)S(1)}, f32[4,128]{1,0:T(4,128)}, u32[]{:S(2)}) copy-start(f32[4,128]{1,0:T(4,128)} %mul.190) | copy-start | bytes 6148
  83.1 45.6 %copy-start.16 = (f32[4,128]{1,0:T(4,128)S(1)}, f32[4,128]{1,0:T(4,128)}, u32[]{:S(2)}) copy-start(f32[4,128]{1,0:T(4,128)} %sub.45) | copy-start | bytes 6148
  83.1 45.6 %copy-start.17 = (f32[128]{0:T(128)S(1)}, f32[128]{0:T(128)}, u32[]{:S(2)}) copy-start(f32[128]{0:T(128)} %param.13) | copy-start | bytes 1540
  83.1 45.6 %copy-start.18 = (f32[128]{0:T(128)S(1)}, f32[128]{0:T(128)}, u32[]{:S(2)}) copy-start(f32[128]{0:T(128)} %param.14) | copy-start | bytes 1540
  131.4 110.5 %copy-start.6 = (bf16[2,16,32,128]{3,2,1,0:T(8,128)(2,1)S(1)}, bf16[2,16,32,128]{3,2,1,0:T(8,128)(2,1)}, u32[]{:S(2)}) copy-start(bf16[2,16,32,128]{3,2,1,0:T(8,128)(2,1)} %copy-done.5) | copy-start | bytes 786436
  131.8 111.8 %collective-permute-start.3 = (bf16[2,16,32,128]{3,2,1,0:T(8,128)(2,1)S(1)}, bf16[2,16,32,128]{3,2,1,0:T(8,128)(2,1)}, u32[]{:S(2)}, u32[]{:S(2)}) collective-permute-start(bf16[2,16,32,128]{3,2,1,0:T(8,128)(2,1)S(1)} %slice.196), channel_id=1, source_target_pairs={{8,0},{16,8},{24,16},{32,24},{40,32},{48,40},{56,48},{64,56},{72,6... | collective-permute-start | bytes 786440 | tf_op jit(solution)/shard_map/ppermute | solution.py:30
  246.1 1.0 copy-start.4
  246.4 0.9 copy-start.11
  249.4 5.9 collective-permute-start.4
  251.3 5.2 collective-permute-start.5
  254.4 0.8 copy-start.7
  255.3 1.6 copy-start.2
  724.5 2.0 copy-start.9
Sparse Core Ops, SparseCore 0:
  255.4 469.0 all-reduce.13
where the time goes:
time: 735 us; the launch traced here: 734 us
  waiting for transfers between devices  471 us (64%)
  blocking collectives  190 us (26%)
  starting transfers between devices  17 us (2%)
  between operations  15.2 us (2%)
  matrix products  14.7 us (2%)
  other arithmetic  14.4 us (2%)
  local copies, waits for them, and re-layouts  11.3 us (2%)
    psum x1, waiting for transfers between devices, shards(): lax.psum((spatial_part, temporal_part, gain_part, shift_part), ('rep', 't...  464 us
    psum x1, blocking collectives, shards(): lax.psum((spatial_part, temporal_part, gain_part, shift_part), ('rep', 't...  108 us
    unnamed x2, blocking collectives  50 us
    psum x1, blocking collectives, shards(): sum_a, sum_b = lax.psum((local_a, local_b), 'height')  20 us
  transfers between devices with their start and end apart: 7, of which 3 were waited for; matrix products, arithmetic and copies ran while one was open for 1% of the time, Pallas kernels for 0%

commit v1 on v0

--- a/solution.py
+++ b/solution.py
@@ -30,24 +30,33 @@
     return lax.ppermute(value, axis, [(source, source + steps) for source in range(first, last)])
 
 
-def carried_in(part, axis, combine, identity, reverse):
-    count = lax.axis_size(axis)
-    place = lax.axis_index(axis)
-    ahead = count - 1 - place if reverse else place
-    gathered = jax.tree.map(lambda a: lax.all_gather(a, axis), part)
-    state = jax.tree.map(lambda a, e: jnp.zeros_like(a) + jnp.asarray(e, a.dtype), part, identity)
-
-    def one(turn, state):
-        source = count - 1 - turn if reverse else turn
-        return combine(
-            state, jax.tree.map(lambda a: lax.dynamic_index_in_dim(a, source, 0, False), gathered)
-        )
-
-    return lax.fori_loop(0, ahead, one, state)
-
-
-def add_pair(earlier, later):
-    return (earlier[0] + later[0], earlier[1] + later[1])
+def share(part, axes):
+    count = 1
+    for axis in axes:
+        count *= lax.axis_size(axis)
+    copies = jnp.broadcast_to(part[None], (count,) + part.shape)
+    return lax.all_to_all(copies, axes, 0, 0, tiled=True)
+
+
+def every_frame(first, second):
+    frames = first.shape[0]
+    time_devices, height_devices = lax.axis_size("tm"), lax.axis_size("height")
+    mine = jnp.concatenate([first.reshape(-1), second.reshape(-1)])
+    every = share(mine, ("tm", "height")).reshape(time_devices, height_devices, 2, frames, GROUPS)
+    summed = every.sum(1).transpose(1, 0, 2, 3).reshape(2, time_devices * frames, GROUPS)
+    return summed[0], summed[1]
+
+
+def total_over_devices(part):
+    rows, channels = part.shape
+    ends = ("rep", "height")
+    pieces = lax.axis_size("rep") * lax.axis_size("height")
+    piece = -(-rows // pieces)
+    padded = jnp.pad(part.astype(jnp.bfloat16), ((0, pieces * piece - rows), (0, 0)))
+    got = lax.all_to_all(padded.reshape(pieces, piece, channels), ends, 0, 0, tiled=True)
+    partial = got.astype(jnp.float32).sum(0).astype(jnp.bfloat16)
+    summed = share(partial, ("tm",)).astype(jnp.float32).sum(0).astype(jnp.bfloat16)
+    return share(summed, ends).astype(jnp.float32).reshape(pieces * piece, channels)[:rows]
 
 
 def reverse_sum(values):
@@ -92,15 +101,13 @@
     grouped = mixed.reshape(frames, rows, columns, GROUPS, group_size)
     first = grouped.sum((1, 2, 4))
     second = (grouped * grouped).sum((1, 2, 4))
-    row_first, row_second = lax.psum((first, second), "height")
-    empty = jnp.zeros((GROUPS,), jnp.float32)
-    before = carried_in(
-        (row_first.sum(0), row_second.sum(0)), "tm", add_pair, (empty, empty), False
-    )
-    counted = ((frame_start + jnp.arange(frames)).astype(jnp.float32) + 1.0)[:, None] * per_frame
-    mean = (before[0] + jnp.cumsum(row_first, 0)) / counted
-    variance = (before[1] + jnp.cumsum(row_second, 0)) / counted - mean * mean
-    inv_std = lax.rsqrt(variance + EPS)
+    first_all, second_all = every_frame(first, second)
+    counted_all = (jnp.arange(time_devices * frames).astype(jnp.float32) + 1.0)[:, None] * per_frame
+    mean_all = jnp.cumsum(first_all, 0) / counted_all
+    variance_all = jnp.cumsum(second_all, 0) / counted_all - mean_all * mean_all
+    inv_std_all = lax.rsqrt(variance_all + EPS)
+    mean = lax.dynamic_slice_in_dim(mean_all, frame_start, frames, 0)
+    inv_std = lax.dynamic_slice_in_dim(inv_std_all, frame_start, frames, 0)
     normed = (grouped - widen(mean)) * widen(inv_std)
     gain = norm_gain.reshape(GROUPS, group_size)
     shift = norm_shift.reshape(GROUPS, group_size)
@@ -117,13 +124,11 @@
     grad_normed = grad_pre * gain
     local_a = grad_normed.sum((1, 2, 4))
     local_b = (grad_normed * normed).sum((1, 2, 4))
-    sum_a, sum_b = lax.psum((local_a, local_b), "height")
-    q_first = (-inv_std * sum_a + inv_std * inv_std * sum_b * mean) / counted
-    q_second = -inv_std * inv_std * sum_b / (2.0 * counted)
-    zeroed = jnp.zeros((GROUPS,), jnp.float32)
-    after = carried_in((q_first.sum(0), q_second.sum(0)), "tm", add_pair, (zeroed, zeroed), True)
-    carry_first = after[0] + reverse_sum(q_first)
-    carry_second = after[1] + reverse_sum(q_second)
+    sum_a, sum_b = every_frame(local_a, local_b)
+    q_first = (-inv_std_all * sum_a + inv_std_all * inv_std_all * sum_b * mean_all) / counted_all
+    q_second = -inv_std_all * inv_std_all * sum_b / (2.0 * counted_all)
+    carry_first = lax.dynamic_slice_in_dim(reverse_sum(q_first), frame_start, frames, 0)
+    carry_second = lax.dynamic_slice_in_dim(reverse_sum(q_second), frame_start, frames, 0)
     grad_mixed = (
         widen(inv_std) * grad_normed + widen(carry_first) + 2.0 * grouped * widen(carry_second)
     )
@@ -173,9 +178,16 @@
             )
     spatial_part = jnp.stack(spatial_terms).reshape(3, 3, channels, channels)
     grad_inputs = grad_in.astype(jnp.bfloat16)
-    spatial_sum, temporal_sum, gain_sum, shift_sum = lax.psum(
-        (spatial_part, temporal_part, gain_part, shift_part), ("rep", "tm", "height")
-    )
+    parts = [
+        spatial_part.reshape(9 * channels, channels),
+        temporal_part.reshape(3 * channels, channels),
+        gain_part[None],
+        shift_part[None],
+    ]
+    sums = total_over_devices(jnp.concatenate(parts, 0))
+    spatial_sum = sums[: 9 * channels].reshape(3, 3, channels, channels)
+    temporal_sum = sums[9 * channels : 12 * channels].reshape(3, channels, channels)
+    gain_sum, shift_sum = sums[12 * channels], sums[12 * channels + 1]
     pixel_total = lax.axis_size("rep") * frames * time_devices * rows * height_devices * columns
     scale = 1.0 / math.sqrt(pixel_total)
     return (

time: 735 us -> 187 us (0.25)
  waiting for transfers between devices: 471 us -> 68.4 us
  blocking collectives: 190 us -> 0 us
  starting transfers between devices: 17 us -> 65.6 us
  between operations: 15.2 us -> 1.26 us
  matrix products: 14.7 us -> 22.5 us
    psum x1 -> x0, waiting for transfers between devices: 464 us -> none  [shards(): lax.psum((spatial_part, temporal_part, gain_part, shift_part), ('rep', 't...]
    psum x3 -> x0, blocking collectives: 140 us -> none  [the longest x1 108 us: shards(): lax.psum((spatial_part, temporal_part, gain_part, shift_part), ('rep', 't...]
    all_to_all x0 -> x5, waiting for transfers between devices: none -> 55.2 us  [the longest x4 49.8 us: share(): return lax.all_to_all(copies, axes, 0, 0, tiled=True)]
    unnamed x2 -> x0, blocking collectives: 50 us -> none
    all_to_all x0 -> x5, starting transfers between devices: none -> 46.4 us  [the longest x4 39.1 us: share(): return lax.all_to_all(copies, axes, 0, 0, tiled=True)]
    dot_general x9, matrix products: 3.81 us -> 13.9 us  [shards(): jnp.einsum('frwd,cd->frwc', back, spatial_kernel[row_tap, col_tap], prefe...]
  transfers between devices with their start and end apart: 7 -> 11, of which waited for: 3 -> 8; matrix products, arithmetic and copies ran while one was open for 1% -> 9% of each run, Pallas kernels for 0% -> 0%
where the time goes in v1:
time: 187 us; the launch traced here: 186 us
  waiting for transfers between devices  68.4 us (37%)
  starting transfers between devices  65.6 us (35%)
  matrix products  22.5 us (12%)
  other arithmetic  17.3 us (9%)
  local copies, waits for them, and re-layouts  10.8 us (6%)
    all_to_all x4, waiting for transfers between devices, share(): return lax.all_to_all(copies, axes, 0, 0, tiled=True)  49.8 us
    all_to_all x4, starting transfers between devices, share(): return lax.all_to_all(copies, axes, 0, 0, tiled=True)  39.1 us
    dot_general x9, matrix products, shards(): jnp.einsum('frwd,cd->frwc', back, spatial_kernel[row_tap, col_tap], prefe...  13.9 us
    ppermute x2, waiting for transfers between devices, from_behind(): lax.ppermute(value, axis, [(source, source + steps) for source in range(f...  12.4 us
    ppermute x2, starting transfers between devices, with_halo(): before = lax.ppermute(last, axis, up)  7.85 us
    ppermute x2, starting transfers between devices, with_halo(): after = lax.ppermute(first, axis, down)  7.38 us
    all_to_all x1, starting transfers between devices, total_over_devices(): lax.all_to_all(padded.reshape(pieces, piece, channels), ends, 0, 0, tiled...  7.31 us
    all_to_all x1, waiting for transfers between devices, total_over_devices(): lax.all_to_all(padded.reshape(pieces, piece, channels), ends, 0, 0, tiled...  5.35 us
  transfers between devices with their start and end apart: 11, of which 8 were waited for; matrix products, arithmetic and copies ran while one was open for 9% of the time, Pallas kernels for 0%

profile of v1, /device:TPU:1, one launch (start us, length us, event | category | flops | bytes accessed | tf_op | source)
XLA Modules:
  0.0 185.8 jit_solution(12898867940388783667)
XLA Ops:
  0.6 0.8 fusion.161
  1.5 4.6 %collective-permute-start = (bf16[4,1,32,128]{3,2,1,0:T(8,128)(2,1)S(1)}, bf16[4,1,32,128]{3,2,1,0:T(8,128)(2,1)S(1)}, u32[]{:S(2)}, u32[]{:S(2)}) collective-permute-start(bf16[4,1,32,128]{3,2,1,0:T(8,128)(2,1)S(1)} %get-tuple-element.18), channel_id=1, source_target_pairs={{0,1},{1,2},{2,3},{3,4},{4,5},{5,6},{6,7},{8,9},{9,10},{10,11},{11... | collective-permute-start | bytes 98312 | tf_op jit(solution)/shard_map/ppermute | solution.py:21
  6.1 5.5 %collective-permute-start.1 = (bf16[4,1,32,128]{3,2,1,0:T(8,128)(2,1)S(1)}, bf16[4,1,32,128]{3,2,1,0:T(8,128)(2,1)S(1)}, u32[]{:S(2)}, u32[]{:S(2)}) collective-permute-start(bf16[4,1,32,128]{3,2,1,0:T(8,128)(2,1)S(1)} %get-tuple-element.19), channel_id=1, source_target_pairs={{1,0},{2,1},{3,2},{4,3},{5,4},{6,5},{7,6},{9,8},{10,9},{11,10},{12... | collective-permute-start | bytes 98312 | tf_op jit(solution)/shard_map/ppermute | solution.py:22
  11.5 0.8 collective-permute-done.1
  12.4 1.4 select_maximum_fusion.2
  14.1 0.7 copy-done
  17.1 2.5 %collective-permute-start.2 = (bf16[2,16,32,128]{3,2,1,0:T(8,128)(2,1)S(1)}, bf16[2,16,32,128]{3,2,1,0:T(8,128)(2,1)S(1)}, u32[]{:S(2)}, u32[]{:S(2)}) collective-permute-start(bf16[2,16,32,128]{3,2,1,0:T(8,128)(2,1)S(1)} %slice.236), channel_id=1, source_target_pairs={{0,8},{8,16},{16,24},{24,32},{32,40},{40,48},{48,56},{56,64},{64,7... | collective-permute-start | bytes 786440 | tf_op jit(solution)/shard_map/ppermute | solution.py:30
  19.9 5.2 %collective-permute-done.2 = bf16[2,16,32,128]{3,2,1,0:T(8,128)(2,1)S(1)} collective-permute-done((bf16[2,16,32,128]{3,2,1,0:T(8,128)(2,1)S(1)}, bf16[2,16,32,128]{3,2,1,0:T(8,128)(2,1)S(1)}, u32[]{:S(2)}, u32[]{:S(2)}) %collective-permute-start.2) | collective-permute-done | bytes 262176 | tf_op jit(solution)/shard_map/ppermute | solution.py:30
  25.4 0.3 fusion.159
  26.4 0.7 broadcast_in_dim.12
  27.1 21.2 %all-to-all-start = ((f32[128,1,256]{2,1,0:T(1,128)}), f32[128,1,256]{2,1,0:T(1,128)}, u32[]{:S(2)}, u32[]{:S(2)}) async-start(f32[128,1,256]{2,1,0:T(1,128)} %broadcast_in_dim.12), calls=%async_computation | async-start | bytes 262144 | tf_op jit(solution)/shard_map/all_to_all | solution.py:38
  48.3 0.5 fusion.148
  48.8 15.6 %all-to-all-done = f32[128,1,256]{2,1,0:T(1,128)} async-done(((f32[128,1,256]{2,1,0:T(1,128)}), f32[128,1,256]{2,1,0:T(1,128)}, u32[]{:S(2)}, u32[]{:S(2)}) %all-to-all-start) | async-done | bytes 131104 | tf_op jit(solution)/shard_map/all_to_all | solution.py:38
  64.4 1.2 reduce.12
  65.6 1.0 reshape.175
  66.7 1.2 reduce_sum.130
  68.1 0.7 broadcast_divide_fusion
  69.2 2.0 %fusion.54 = (bf16[128]{0:T(256)(128)(2,1)}, f32[4,128]{1,0:T(4,128)S(1)}, f32[4,128]{1,0:T(4,128)S(1)}, bf16[128]{0:T(256)(128)(2,1)}) fusion(f32[4,16,32,128]{3,2,1,0:T(8,128)S(1)} %get-tuple-element.28, f32[4,128]{1,0:T(4,128)S(1)} %mul.207, f32[4,128]{1,0:T(4,128)S(1)} %sub.32, f32[128]{0:T(128)} %param.9, f32[128]{0:T(128)} %param.10, ...), kind=kLoop, calls=%fused_computation.84 | loop fusion | flops 5241600 | bytes 1582592 | tf_op jit(solution)/shard_map/reduce_sum | solution.py:122
  71.8 0.7 broadcast_in_dim.14
  72.6 7.3 %all-to-all-start.1 = ((f32[128,1,256]{2,1,0:T(1,128)}), f32[128,1,256]{2,1,0:T(1,128)}, u32[]{:S(2)}, u32[]{:S(2)}) async-start(f32[128,1,256]{2,1,0:T(1,128)} %broadcast_in_dim.14), calls=%async_computation.1 | async-start | bytes 262144 | tf_op jit(solution)/shard_map/all_to_all | solution.py:38
  79.8 0.5 fusion.147
  80.4 15.6 %all-to-all-done.1 = f32[128,1,256]{2,1,0:T(1,128)} async-done(((f32[128,1,256]{2,1,0:T(1,128)}), f32[128,1,256]{2,1,0:T(1,128)}, u32[]{:S(2)}, u32[]{:S(2)}) %all-to-all-start.1) | async-done | bytes 131104 | tf_op jit(solution)/shard_map/all_to_all | solution.py:38
  95.9 1.2 reduce.13
  97.1 1.0 reshape.178
  98.2 1.2 reduce_sum.137
  99.4 0.8 fusion.90
  100.8 2.3 %fusion.52 = (bf16[4,16,32,128]{3,2,1,0:T(8,128)(2,1)S(1)}, bf16[1,4,16,32,128]{4,3,2,1,0:T(8,128)(2,1)}) fusion(bf16[1,4,16,32,128]{4,3,2,1,0:T(8,128)(2,1)S(1)} %copy-done.1, f32[4,16,32,128]{3,2,1,0:T(8,128)S(1)} %get-tuple-element.28, f32[4,128]{1,0:T(4,128)S(1)} %mul.235, f32[4,128]{1,0:T(4,128)S(1)} %add.179, f32[128]{0:T(128)} %param.9, ...), kind=kLoop, calls=%fused_computation.80 | loop fusion | flops 6029312 | bytes 3154944 | tf_op jit(solution)/shard_map/convert_element_type | solution.py:135
  103.5 1.5 collective-permute-start.3
  105.0 0.3 fusion.28
  105.7 0.5 copy-done.9
  106.5 7.2 %collective-permute-done.3 = bf16[2,16,32,128]{3,2,1,0:T(8,128)(2,1)S(1)} collective-permute-done((bf16[2,16,32,128]{3,2,1,0:T(8,128)(2,1)S(1)}, bf16[2,16,32,128]{3,2,1,0:T(8,128)(2,1)S(1)}, u32[]{:S(2)}, u32[]{:S(2)}) %collective-permute-start.3) | collective-permute-done | bytes 262176 | tf_op jit(solution)/shard_map/ppermute | solution.py:30
  114.1 0.4 fusion.13
  114.8 2.0 %fusion.101 = f32[4,16,32,128]{3,2,1,0:T(8,128)} fusion(bf16[4,16,32,128]{3,2,1,0:T(8,128)(2,1)S(1)} %fusion.13, bf16[3,3,128,128]{3,2,1,0:T(8,128)(2,1)} %param.7), kind=kOutput, calls=%fused_computation.151 | convolution fusion | flops 67108864 | bytes 1605632 | tf_op jit(solution)/shard_map/frwd,cd->frwc/dot_general | solution.py:167
  116.8 0.4 fusion.32
  117.2 0.4 fusion.45
  117.6 0.4 fusion.43
  117.9 0.4 fusion.41
  118.3 0.4 fusion.39
  118.7 0.4 fusion.37
  119.0 3.3 %collective-permute-start.4 = (bf16[4,1,32,128]{3,2,1,0:T(8,128)(2,1)S(1)}, bf16[4,1,32,128]{3,2,1,0:T(8,128)(2,1)S(1)}, u32[]{:S(2)}, u32[]{:S(2)}) collective-permute-start(bf16[4,1,32,128]{3,2,1,0:T(8,128)(2,1)S(1)} %get-tuple-element.16), channel_id=1, source_target_pairs={{0,1},{1,2},{2,3},{3,4},{4,5},{5,6},{6,7},{8,9},{9,10},{10,11},{11... | collective-permute-start | bytes 98312 | tf_op jit(solution)/shard_map/ppermute | solution.py:21
  122.3 1.9 %collective-permute-start.5 = (bf16[4,1,32,128]{3,2,1,0:T(8,128)(2,1)S(1)}, bf16[4,1,32,128]{3,2,1,0:T(8,128)(2,1)S(1)}, u32[]{:S(2)}, u32[]{:S(2)}) collective-permute-start(bf16[4,1,32,128]{3,2,1,0:T(8,128)(2,1)S(1)} %get-tuple-element.17), channel_id=1, source_target_pairs={{1,0},{2,1},{3,2},{4,3},{5,4},{6,5},{7,6},{9,8},{10,9},{11,10},{12... | collective-permute-start | bytes 98312 | tf_op jit(solution)/shard_map/ppermute | solution.py:22
  124.2 0.4 fusion.30
  124.6 0.4 fusion.35
  125.5 0.9 reshape.180
  126.4 7.3 %all-to-all-start.2 = ((bf16[32,49,128]{2,1,0:T(8,128)(2,1)}), bf16[32,49,128]{2,1,0:T(8,128)(2,1)S(1)}, u32[]{:S(2)}, u32[]{:S(2)}) async-start(bf16[32,49,128]{2,1,0:T(8,128)(2,1)} %reshape.180), calls=%async_computation.2 | async-start | bytes 917504 | tf_op jit(solution)/shard_map/all_to_all | solution.py:56
  134.0 2.1 %fusion.64 = f32[4,16,32,128]{3,2,1,0:T(8,128)} fusion(bf16[4,18,34,128]{3,2,1,0:T(8,128)(2,1)S(1)} %select_maximum_fusion, bf16[3,3,128,128]{3,2,1,0:T(8,128)(2,1)} %param.7), kind=kOutput, calls=%fused_computation.110 | convolution fusion | flops 67108864 | bytes 1605632 | tf_op jit(solution)/shard_map/frwd,cd->frwc/dot_general | solution.py:167
  136.2 2.0 %fusion.66 = f32[4,16,32,128]{3,2,1,0:T(8,128)} fusion(bf16[4,18,34,128]{3,2,1,0:T(8,128)(2,1)S(1)} %select_maximum_fusion, bf16[3,3,128,128]{3,2,1,0:T(8,128)(2,1)} %param.7), kind=kOutput, calls=%fused_computation.112 | convolution fusion | flops 67108864 | bytes 1605632 | tf_op jit(solution)/shard_map/frwd,cd->frwc/dot_general | solution.py:167
  138.2 1.1 fusion.68
  139.3 5.3 %all-to-all-done.2 = bf16[32,49,128]{2,1,0:T(8,128)(2,1)S(1)} async-done(((bf16[32,49,128]{2,1,0:T(8,128)(2,1)}), bf16[32,49,128]{2,1,0:T(8,128)(2,1)S(1)}, u32[]{:S(2)}, u32[]{:S(2)}) %all-to-all-start.2) | async-done | bytes 401440 | tf_op jit(solution)/shard_map/all_to_all | solution.py:56
  144.7 0.7 broadcast_in_dim.16
  145.4 4.2 %all-to-all-start.3 = ((bf16[16,49,128]{2,1,0:T(8,128)(2,1)}), bf16[16,49,128]{2,1,0:T(8,128)(2,1)}, u32[]{:S(2)}, u32[]{:S(2)}) async-start(bf16[16,49,128]{2,1,0:T(8,128)(2,1)} %broadcast_in_dim.16), calls=%async_computation.3 | async-start | bytes 458752 | tf_op jit(solution)/shard_map/all_to_all | solution.py:38
  149.6 1.1 fusion.70
  150.8 1.2 convolution_add_fusion.5
  152.3 1.3 fusion.8
  153.7 10.6 %all-to-all-done.3 = bf16[16,49,128]{2,1,0:T(8,128)(2,1)} async-done(((bf16[16,49,128]{2,1,0:T(8,128)(2,1)}), bf16[16,49,128]{2,1,0:T(8,128)(2,1)}, u32[]{:S(2)}, u32[]{:S(2)}) %all-to-all-start.3) | async-done | bytes 200736 | tf_op jit(solution)/shard_map/all_to_all | solution.py:38
  164.3 1.0 reduce_sum.141
  165.2 0.8 broadcast_in_dim.17
  166.1 6.5 %all-to-all-start.4 = ((bf16[32,49,128]{2,1,0:T(8,128)(2,1)}), bf16[32,49,128]{2,1,0:T(8,128)(2,1)S(1)}, u32[]{:S(2)}, u32[]{:S(2)}) async-start(bf16[32,49,128]{2,1,0:T(8,128)(2,1)} %broadcast_in_dim.17), calls=%async_computation.4 | async-start | bytes 917504 | tf_op jit(solution)/shard_map/all_to_all | solution.py:38
  172.6 1.1 fusion.62
  173.6 1.9 fusion.14
  175.5 8.1 %all-to-all-done.4 = bf16[32,49,128]{2,1,0:T(8,128)(2,1)S(1)} async-done(((bf16[32,49,128]{2,1,0:T(8,128)(2,1)}), bf16[32,49,128]{2,1,0:T(8,128)(2,1)S(1)}, u32[]{:S(2)}, u32[]{:S(2)}) %all-to-all-start.4) | async-done | bytes 401440 | tf_op jit(solution)/shard_map/all_to_all | solution.py:38
  183.7 0.9 slice_multiply_fusion
  184.6 0.7 slice_multiply_fusion.1
  185.3 0.5 fusion.145
  (97 shorter events, 8.6 us)
Async XLA Ops:
  0.6 13.1 %copy-start.5 = (bf16[3,3,128,128]{3,2,1,0:T(8,128)(2,1)S(1)}, bf16[3,3,128,128]{3,2,1,0:T(8,128)(2,1)}, u32[]{:S(2)}) copy-start(bf16[3,3,128,128]{3,2,1,0:T(8,128)(2,1)} %param.7) | copy-start | bytes 884740
  1.5 10.0 %collective-permute-start = (bf16[4,1,32,128]{3,2,1,0:T(8,128)(2,1)S(1)}, bf16[4,1,32,128]{3,2,1,0:T(8,128)(2,1)S(1)}, u32[]{:S(2)}, u32[]{:S(2)}) collective-permute-start(bf16[4,1,32,128]{3,2,1,0:T(8,128)(2,1)S(1)} %get-tuple-element.18), channel_id=1, source_target_pairs={{0,1},{1,2},{2,3},{3,4},{4,5},{5,6},{6,7},{8,9},{9,10},{10,11},{11... | collective-permute-start | bytes 98312 | tf_op jit(solution)/shard_map/ppermute | solution.py:21
  6.1 6.3 %collective-permute-start.1 = (bf16[4,1,32,128]{3,2,1,0:T(8,128)(2,1)S(1)}, bf16[4,1,32,128]{3,2,1,0:T(8,128)(2,1)S(1)}, u32[]{:S(2)}, u32[]{:S(2)}) collective-permute-start(bf16[4,1,32,128]{3,2,1,0:T(8,128)(2,1)S(1)} %get-tuple-element.19), channel_id=1, source_target_pairs={{1,0},{2,1},{3,2},{4,3},{5,4},{6,5},{7,6},{9,8},{10,9},{11,10},{12... | collective-permute-start | bytes 98312 | tf_op jit(solution)/shard_map/ppermute | solution.py:22
  11.5 2.5 %copy-start.12 = (bf16[4,1,32,128]{3,2,1,0:T(8,128)(2,1)}, bf16[4,1,32,128]{3,2,1,0:T(8,128)(2,1)S(1)}, u32[]{:S(2)}) copy-start(bf16[4,1,32,128]{3,2,1,0:T(8,128)(2,1)S(1)} %collective-permute-done) | copy-start | bytes 98308
  12.4 4.5 %copy-start.10 = (bf16[4,1,32,128]{3,2,1,0:T(8,128)(2,1)}, bf16[4,1,32,128]{3,2,1,0:T(8,128)(2,1)S(1)}, u32[]{:S(2)}) copy-start(bf16[4,1,32,128]{3,2,1,0:T(8,128)(2,1)S(1)} %collective-permute-done.1) | copy-start | bytes 98308
  13.7 1.0 copy-start
  16.8 2.8 %copy-start.8 = (bf16[3,128,128]{2,1,0:T(8,128)(2,1)S(1)}, bf16[3,128,128]{2,1,0:T(8,128)(2,1)}, u32[]{:S(2)}) copy-start(bf16[3,128,128]{2,1,0:T(8,128)(2,1)} %param.8) | copy-start | bytes 294916
  17.1 7.9 %collective-permute-start.2 = (bf16[2,16,32,128]{3,2,1,0:T(8,128)(2,1)S(1)}, bf16[2,16,32,128]{3,2,1,0:T(8,128)(2,1)S(1)}, u32[]{:S(2)}, u32[]{:S(2)}) collective-permute-start(bf16[2,16,32,128]{3,2,1,0:T(8,128)(2,1)S(1)} %slice.236), channel_id=1, source_target_pairs={{0,8},{8,16},{16,24},{24,32},{32,40},{40,48},{48,56},{56,64},{64,7... | collective-permute-start | bytes 786440 | tf_op jit(solution)/shard_map/ppermute | solution.py:30
  25.1 0.7 copy-start.6
  27.1 37.3 %all-to-all-start = ((f32[128,1,256]{2,1,0:T(1,128)}), f32[128,1,256]{2,1,0:T(1,128)}, u32[]{:S(2)}, u32[]{:S(2)}) async-start(f32[128,1,256]{2,1,0:T(1,128)} %broadcast_in_dim.12), calls=%async_computation | async-start | bytes 262144 | tf_op jit(solution)/shard_map/all_to_all | solution.py:38
  48.8 20.4 %copy-start.1 = (bf16[1,4,16,32,128]{4,3,2,1,0:T(8,128)(2,1)S(1)}, bf16[1,4,16,32,128]{4,3,2,1,0:T(8,128)(2,1)}, u32[]{:S(2)}) copy-start(bf16[1,4,16,32,128]{4,3,2,1,0:T(8,128)(2,1)} %param.11) | copy-start | bytes 1572868
  69.0 3.5 %copy-start.14 = (f32[4,128]{1,0:T(4,128)}, f32[4,128]{1,0:T(4,128)S(1)}, u32[]{:S(2)}) copy-start(f32[4,128]{1,0:T(4,128)S(1)} %mul.207) | copy-start | bytes 6148
  69.2 3.3 %copy-start.15 = (f32[4,128]{1,0:T(4,128)}, f32[4,128]{1,0:T(4,128)S(1)}, u32[]{:S(2)}) copy-start(f32[4,128]{1,0:T(4,128)S(1)} %sub.32) | copy-start | bytes 6148
  72.6 23.4 %all-to-all-start.1 = ((f32[128,1,256]{2,1,0:T(1,128)}), f32[128,1,256]{2,1,0:T(1,128)}, u32[]{:S(2)}, u32[]{:S(2)}) async-start(f32[128,1,256]{2,1,0:T(1,128)} %broadcast_in_dim.14), calls=%async_computation.1 | async-start | bytes 262144 | tf_op jit(solution)/shard_map/all_to_all | solution.py:38
  103.2 1.8 copy-start.7
  103.5 10.2 %collective-permute-start.3 = (bf16[2,16,32,128]{3,2,1,0:T(8,128)(2,1)S(1)}, bf16[2,16,32,128]{3,2,1,0:T(8,128)(2,1)S(1)}, u32[]{:S(2)}, u32[]{:S(2)}) collective-permute-start(bf16[2,16,32,128]{3,2,1,0:T(8,128)(2,1)S(1)} %slice.241), channel_id=1, source_target_pairs={{8,0},{16,8},{24,16},{32,24},{40,32},{48,40},{56,48},{64,56},{72,6... | collective-permute-start | bytes 786440 | tf_op jit(solution)/shard_map/ppermute | solution.py:30
  105.4 0.9 copy-start.9
  114.8 2.1 %copy-start.13 = (bf16[4,1,32,128]{3,2,1,0:T(8,128)(2,1)S(1)}, bf16[4,1,32,128]{3,2,1,0:T(8,128)(2,1)}, u32[]{:S(2)}) copy-start(bf16[4,1,32,128]{3,2,1,0:T(8,128)(2,1)} %copy-done.12) | copy-start | bytes 98308
  118.7 5.6 %copy-start.11 = (bf16[4,1,32,128]{3,2,1,0:T(8,128)(2,1)S(1)}, bf16[4,1,32,128]{3,2,1,0:T(8,128)(2,1)}, u32[]{:S(2)}) copy-start(bf16[4,1,32,128]{3,2,1,0:T(8,128)(2,1)} %copy-done.10) | copy-start | bytes 98308
  119.0 14.7 %collective-permute-start.4 = (bf16[4,1,32,128]{3,2,1,0:T(8,128)(2,1)S(1)}, bf16[4,1,32,128]{3,2,1,0:T(8,128)(2,1)S(1)}, u32[]{:S(2)}, u32[]{:S(2)}) collective-permute-start(bf16[4,1,32,128]{3,2,1,0:T(8,128)(2,1)S(1)} %get-tuple-element.16), channel_id=1, source_target_pairs={{0,1},{1,2},{2,3},{3,4},{4,5},{5,6},{6,7},{8,9},{9,10},{10,11},{11... | collective-permute-start | bytes 98312 | tf_op jit(solution)/shard_map/ppermute | solution.py:21
  122.3 11.4 %collective-permute-start.5 = (bf16[4,1,32,128]{3,2,1,0:T(8,128)(2,1)S(1)}, bf16[4,1,32,128]{3,2,1,0:T(8,128)(2,1)S(1)}, u32[]{:S(2)}, u32[]{:S(2)}) collective-permute-start(bf16[4,1,32,128]{3,2,1,0:T(8,128)(2,1)S(1)} %get-tuple-element.17), channel_id=1, source_target_pairs={{1,0},{2,1},{3,2},{4,3},{5,4},{6,5},{7,6},{9,8},{10,9},{11,10},{12... | collective-permute-start | bytes 98312 | tf_op jit(solution)/shard_map/ppermute | solution.py:22
  124.6 0.7 copy-start.16
  124.6 0.7 copy-start.17
  126.4 18.3 %all-to-all-start.2 = ((bf16[32,49,128]{2,1,0:T(8,128)(2,1)}), bf16[32,49,128]{2,1,0:T(8,128)(2,1)S(1)}, u32[]{:S(2)}, u32[]{:S(2)}) async-start(bf16[32,49,128]{2,1,0:T(8,128)(2,1)} %reshape.180), calls=%async_computation.2 | async-start | bytes 917504 | tf_op jit(solution)/shard_map/all_to_all | solution.py:56
  145.4 18.8 %all-to-all-start.3 = ((bf16[16,49,128]{2,1,0:T(8,128)(2,1)}), bf16[16,49,128]{2,1,0:T(8,128)(2,1)}, u32[]{:S(2)}, u32[]{:S(2)}) async-start(bf16[16,49,128]{2,1,0:T(8,128)(2,1)} %broadcast_in_dim.16), calls=%async_computation.3 | async-start | bytes 458752 | tf_op jit(solution)/shard_map/all_to_all | solution.py:38
  149.6 2.4 %copy-start.4 = (f32[4,16,32,128]{3,2,1,0:T(8,128)S(1)}, f32[4,16,32,128]{3,2,1,0:T(8,128)}, u32[]{:S(2)}) copy-start(f32[4,16,32,128]{3,2,1,0:T(8,128)} %fusion.66) | copy-start | bytes 3145732
  150.8 1.3 copy-start.2
  150.8 1.6 copy-start.3
  166.1 17.5 %all-to-all-start.4 = ((bf16[32,49,128]{2,1,0:T(8,128)(2,1)}), bf16[32,49,128]{2,1,0:T(8,128)(2,1)S(1)}, u32[]{:S(2)}, u32[]{:S(2)}) async-start(bf16[32,49,128]{2,1,0:T(8,128)(2,1)} %broadcast_in_dim.17), calls=%async_computation.4 | async-start | bytes 917504 | tf_op jit(solution)/shard_map/all_to_all | solution.py:38

commit v2 on v0

v2 whole, which is shorter than its diff:
```python
import functools
import math

import jax
import jax.numpy as jnp
from jax import lax
from jax.experimental import pallas as pl
from jax.experimental.pallas import tpu as pltpu
from jax.sharding import PartitionSpec as P

GROUPS = 32


EPS = 1e-05
TILE = 128


def iota(shape, dim):
    return lax.broadcasted_iota(jnp.int32, shape, dim)


def exact_dot(a, b):
    return lax.dot_general(
        a,
        b,
        (((1,), (0,)), ((), ())),
        precision=lax.Precision.HIGHEST,
        preferred_element_type=jnp.float32,
    )


def dot(a, b, turned=False):
    return lax.dot_general(
        a,
        b,
        (((1,), (1 if turned else 0,)), ((), ())),
        preferred_element_type=jnp.float32,
    )


def group_matrix(size):
    return (iota((TILE, TILE), 0) // size == iota((TILE, TILE), 1) // size).astype(jnp.float32)


def per_device_sums(got, time_devices, height_devices, earlier):
    shape = (2 * time_devices, got.shape[0])
    row, col = iota(shape, 0), iota(shape, 1)
    at, source = row % time_devices, col // (2 * height_devices)
    keep = (source < at) if earlier else (source == at)
    keep = keep & (row // time_devices == col % 2)
    return exact_dot(keep.astype(jnp.float32), got)


def moved(value, step, columns):
    pixels = value.shape[0]
    rolled = pltpu.roll(value, step % pixels, 0)
    place = iota(value.shape, 0) % columns
    edge = 0 if step > 0 else columns - 1
    return jnp.where(place == edge, 0.0, rolled)


def three_rows(block, rows, columns):
    size = rows * columns
    return jnp.concatenate(
        [block[i * columns : i * columns + size] for i in range(3)], axis=1
    )


def convolve(block, weight, rows, columns, turned):
    taps = dot(three_rows(block, rows, columns), weight, turned)
    c = taps.shape[1] // 3
    sign = -1 if turned else 1
    return (
        taps[:, c : 2 * c]
        + moved(taps[:, :c], sign, columns)
        + moved(taps[:, 2 * c :], -sign, columns)
    )


def flat(value):
    return value.reshape(-1, value.shape[-1])


def put_weight(weight_ref, spatial_ref):
    for i in range(3):
        for j in range(3):
            weight_ref[i * TILE : (i + 1) * TILE, j * TILE : (j + 1) * TILE] = spatial_ref[i, j]


def put_payload(out_ref, firsts, seconds):
    frames = len(firsts)
    sums = exact_dot(jnp.concatenate(firsts + seconds, 0), group_matrix(frames))
    lane = iota((1, TILE), 1) % frames
    rows = []
    for start in (0, frames):
        line = jnp.zeros((1, TILE), jnp.float32)
        for f in range(frames):
            line = jnp.where(lane == f, sums[start + f : start + f + 1], line)
        rows.append(line)
    line = jnp.where(iota((8, TILE), 0) % 2 == 0, rows[0], rows[1])
    for i in range(out_ref.shape[0] // 8):
        out_ref[i * 8 : (i + 1) * 8] = line


def own_features(x_ref, before_ref, after_ref, spatial_ref, feature_ref, weight_ref):
    put_weight(weight_ref, spatial_ref)
    frames, rows, columns, _ = x_ref.shape

    def one(f, _):
        block = jnp.concatenate([flat(before_ref[f]), flat(x_ref[f]), flat(after_ref[f])], 0)
        out = convolve(block, weight_ref[...], rows + 2, columns, False)
        feature_ref[f] = out.astype(jnp.bfloat16).reshape(feature_ref.shape[1:])
        return 0

    lax.fori_loop(0, frames, one, 0)


def mix(blocks, temporal_ref):
    return dot(jnp.concatenate(blocks, axis=1), flat(temporal_ref[...]))


def mixed_and_sums(
    feature_ref, prev_ref, spatial_ref, temporal_ref, prior_ref, mixed_ref, out_ref, weight_ref
):
    put_weight(weight_ref, spatial_ref)
    frames, rows, columns, _ = mixed_ref.shape

    def one(f, _):
        out = convolve(flat(prev_ref[f]), weight_ref[...], rows, columns, False)
        prior_ref[f] = out.astype(jnp.bfloat16).reshape(prior_ref.shape[1:])
        return 0

    lax.fori_loop(0, 2, one, 0)
    firsts, seconds = [], []
    for f in range(frames):
        blocks = [
            flat(prior_ref[f + k]) if f + k < 2 else flat(feature_ref[f + k - 2]) for k in range(3)
        ]
        out = mix(blocks, temporal_ref)
        mixed_ref[f] = out.reshape(mixed_ref.shape[1:])
        inner = out[columns : (rows - 1) * columns]
        firsts.append(inner.sum(0, keepdims=True))
        seconds.append((inner * inner).sum(0, keepdims=True))
    put_payload(out_ref, firsts, seconds)


def next_and_turned(
    next_ref,
    feature_ref,
    prior_ref,
    x_ref,
    before_ref,
    after_ref,
    spatial_ref,
    temporal_ref,
    mixed_ref,
    xt_ref,
    ft_ref,
    weight_ref,
    held_ref,
):
    put_weight(weight_ref, spatial_ref)
    frames, rows, columns, _ = x_ref.shape
    ext = rows + 2

    def one(f, _):
        out = convolve(flat(next_ref[f]), weight_ref[...], ext, columns, False)
        held_ref[f] = out.astype(jnp.bfloat16).reshape(held_ref.shape[1:])
        return 0

    lax.fori_loop(0, 2, one, 0)
    for f in range(2):
        blocks = [
            flat(feature_ref[f + 2 + k]) if f + k < 2 else flat(held_ref[f + k - 2])
            for k in range(3)
        ]
        mixed_ref[f] = mix(blocks, temporal_ref).reshape(mixed_ref.shape[1:])

    for f in range(frames):
        block = jnp.concatenate(
            [flat(before_ref[f, 1:]), flat(x_ref[f]), flat(after_ref[f, :1])], 0
        )
        xt_ref[f] = three_rows(block, rows, columns).astype(jnp.float32).T.astype(jnp.bfloat16)
        seen = [
            flat(prior_ref[f + k, 1 : rows + 1])
            if f + k < 2
            else flat(feature_ref[f + k - 2, 1 : rows + 1])
            for k in range(3)
        ]
        ft_ref[f] = jnp.concatenate(seen, axis=1).astype(jnp.float32).T.astype(jnp.bfloat16)


def counts(f, frames, time_devices, per_frame):
    at = iota((time_devices, TILE), 0) * frames + (f + 1)
    return at.astype(jnp.float32) * per_frame


def statistics_and_sums(
    time_devices,
    height_devices,
    per_frame,
    got_ref,
    mixed_ref,
    cot_ref,
    gain_ref,
    shift_ref,
    stats_ref,
    out_ref,
    parts_ref,
):
    frames, rows, columns, _ = cot_ref.shape
    me = lax.axis_index("tm")
    got = got_ref[...]
    here = per_device_sums(got, time_devices, height_devices, False)
    earlier = per_device_sums(got, time_devices, height_devices, True)
    group = group_matrix(frames)
    lane = iota(here.shape, 1) % frames
    for f in range(frames):
        sums = exact_dot(earlier + jnp.where(lane <= f, here, 0.0), group)
        count = counts(f, frames, time_devices, per_frame)
        mean = sums[:time_devices] / count
        variance = sums[time_devices:] / count - mean * mean
        at = 2 * f * time_devices
        stats_ref[at : at + time_devices] = mean
        stats_ref[at + time_devices : at + 2 * time_devices] = lax.rsqrt(variance + EPS)
    gain, shift = gain_ref[...], shift_ref[...]
    step = 4
    firsts, seconds = [], []
    for f in range(frames):
        mean = stats_ref[pl.ds(2 * f * time_devices + me, 1)]
        inv_std = stats_ref[pl.ds((2 * f + 1) * time_devices + me, 1)]

        def some(i, sums, f=f, mean=mean, inv_std=inv_std):
            normed = (flat(mixed_ref[f, pl.ds(1 + i * step, step)]) - mean) * inv_std
            pre = normed * gain + shift
            sigma = 1.0 / (1.0 + jnp.exp(-pre))
            cot = flat(cot_ref[f, pl.ds(i * step, step)]).astype(jnp.float32)
            grad = cot * (sigma * (1.0 + pre * (1.0 - sigma)))
            split = (-1, 8, TILE)
            return (
                sums[0] + grad.reshape(split).sum(0),
                sums[1] + (grad * normed).reshape(split).sum(0),
            )

        zero = jnp.zeros((8, TILE), jnp.float32)
        a, b = lax.fori_loop(0, rows // step, some, (zero, zero), unroll=2)
        firsts.append(a.sum(0, keepdims=True))
        seconds.append(b.sum(0, keepdims=True))
    put_payload(out_ref, [a * gain for a in firsts], [b * gain for b in seconds])
    total_a, total_b = sum(firsts[1:], firsts[0]), sum(seconds[1:], seconds[0])
    parts_ref[...] = jnp.where(iota((16, TILE), 0) < 8, total_b, total_a)


def outputs_and_grads(
    time_devices,
    stats_ref,
    mixed_ref,
    mixed_next_ref,
    x_ref,
    cot_ref,
    before_ref,
    after_ref,
    next_ref,
    gain_ref,
    shift_ref,
    scaled_ref,
    outputs_ref,
):
    frames, rows, columns, _ = cot_ref.shape
    me = lax.axis_index("tm")
    following = jnp.minimum(me + 1, time_devices - 1)
    gain, shift = gain_ref[...], shift_ref[...]
    step = 4

    def grads(mixed, cot, mean, inv_std):
        pre = (mixed - mean) * inv_std * gain + shift
        sigma = 1.0 / (1.0 + jnp.exp(-pre))
        grad = cot.astype(jnp.float32) * (sigma * (1.0 + pre * (1.0 - sigma)))
        return pre * sigma, inv_std * (grad * gain)

    for f in range(frames + 2):
        own = f < frames
        at, g = (me, f) if own else (following, f - frames)
        mean = stats_ref[pl.ds(2 * g * time_devices + at, 1)]
        inv_std = stats_ref[pl.ds((2 * g + 1) * time_devices + at, 1)]
        source = mixed_ref if own else mixed_next_ref

        def edge(row, cot, f=f, g=g, mean=mean, inv_std=inv_std, source=source):
            _, scaled = grads(source[g, row], cot, mean, inv_std)
            scaled_ref[f, row] = scaled

        edge(0, before_ref[frames + g, 1] if own else next_ref[2 + g, 1])
        edge(rows + 1, after_ref[frames + g, 0] if own else next_ref[2 + g, rows + 2])

        def some(i, _, f=f, g=g, own=own, mean=mean, inv_std=inv_std, source=source):
            here = pl.ds(1 + i * step, step)
            cot = cot_ref[g, pl.ds(i * step, step)] if own else next_ref[2 + g, pl.ds(2 + i * step, step)]
            silu, scaled = grads(flat(source[g, here]), flat(cot), mean, inv_std)
            scaled_ref[f, here] = scaled.reshape(step, columns, TILE)
            if own:
                kept = flat(x_ref[g, pl.ds(i * step, step)]).astype(jnp.float32) + silu
                outputs_ref[g, pl.ds(i * step, step)] = kept.astype(jnp.bfloat16).reshape(
                    step, columns, TILE
                )
            return 0

        lax.fori_loop(0, rows // step, some, 0, unroll=2)


def parameter_grads(
    time_devices,
    height_devices,
    per_frame,
    got_ref,
    stats_ref,
    scaled_ref,
    mixed_ref,
    mixed_next_ref,
    xt_ref,
    ft_ref,
    temporal_ref,
    parts_ref,
    feature_grad_ref,
    out_ref,
    carry_ref,
    mixed_grad_ref,
):
    frames, ext, columns, _ = mixed_ref.shape
    rows = ext - 2
    me, level = lax.axis_index("tm"), lax.axis_index("height")
    following = jnp.minimum(me + 1, time_devices - 1)
    here = per_device_sums(got_ref[...], time_devices, height_devices, False)
    group = group_matrix(frames)
    lane = iota(here.shape, 1) % frames
    firsts, seconds = [], []
    for f in range(frames):
        sums = exact_dot(jnp.where(lane == f, here, 0.0), group)
        sum_a, sum_b = sums[:time_devices], sums[time_devices:]
        at = 2 * f * time_devices
        mean = stats_ref[at : at + time_devices]
        inv_std = stats_ref[at + time_devices : at + 2 * time_devices]
        count = counts(f, frames, time_devices, per_frame)
        firsts.append((-inv_std * sum_a + inv_std * inv_std * sum_b * mean) / count)
        seconds.append(-inv_std * inv_std * sum_b / (2.0 * count))
    square = (time_devices, time_devices)
    later = (iota(square, 1) > iota(square, 0)).astype(jnp.float32)
    for kind, values in enumerate((firsts, seconds)):
        run = exact_dot(later, sum(values[1:], values[0]))
        for f in range(frames - 1, -1, -1):
            run = run + values[f]
            at = (2 * f + kind) * time_devices
            carry_ref[at : at + time_devices] = run
    exists = (me < time_devices - 1).astype(jnp.float32)
    for f in range(frames + 2):
        own = f < frames
        at, g = (me, f) if own else (following, f - frames)
        first = carry_ref[pl.ds(2 * g * time_devices + at, 1)]
        second = 2.0 * carry_ref[pl.ds((2 * g + 1) * time_devices + at, 1)]
        source = mixed_ref if own else mixed_next_ref

        def some(i, _, f=f, g=g, own=own, first=first, second=second, source=source):
            at = pl.ds(i * 3, 3)
            grad = flat(scaled_ref[f, at]) + first + flat(source[g, at]) * second
            if not own:
                grad = grad * exists
            mixed_grad_ref[f, at] = grad.astype(jnp.bfloat16).reshape(3, columns, TILE)
            return 0

        lax.fori_loop(0, ext // 3, some, 0, unroll=3)
    turned = jnp.concatenate([temporal_ref[k] for k in range(3)], axis=1)
    place = iota((ext * columns, TILE), 0) // columns
    outside = ((place == 0) & (level == 0)) | ((place == ext - 1) & (level == height_devices - 1))
    spatial = jnp.zeros((3 * TILE, 3 * TILE), jnp.float32)
    temporal = jnp.zeros((3 * TILE, TILE), jnp.float32)
    for f in range(frames):
        blocks = [flat(mixed_grad_ref[f + 2 - k]) for k in range(3)]
        grad = dot(jnp.concatenate(blocks, axis=1), turned, True)
        grad = jnp.where(outside, 0.0, grad).astype(jnp.bfloat16)
        feature_grad_ref[f] = grad.reshape(ext, columns, TILE)
        inner = grad[columns : (rows + 1) * columns]
        wide = inner.astype(jnp.float32)
        shifted = jnp.concatenate(
            [
                moved(wide, -1, columns).astype(jnp.bfloat16),
                inner,
                moved(wide, 1, columns).astype(jnp.bfloat16),
            ],
            axis=1,
        )
        spatial = spatial + dot(xt_ref[f], shifted)
        temporal = temporal + dot(ft_ref[f], flat(mixed_grad_ref[f, 1 : rows + 1]))
    pieces = out_ref.shape[0]
    piece = 12 * TILE // pieces
    blocks = [spatial[:, j * TILE : (j + 1) * TILE] for j in range(3)] + [temporal]
    whole = jnp.concatenate(blocks, axis=0).astype(jnp.bfloat16)
    for p in range(pieces):
        out_ref[p, :piece] = whole[p * piece : (p + 1) * piece]
        tail = parts_ref[8 * min(p, 1) : 8 * min(p, 1) + 8]
        tail = jnp.where((iota((8, TILE), 0) == 0) & (p < 2), tail, 0.0)
        out_ref[p, piece : piece + 8] = tail.astype(jnp.bfloat16)


def input_grads(grad_ref, cot_ref, spatial_ref, out_ref, weight_ref):
    frames, rows, columns, _ = cot_ref.shape
    for s in range(3):
        for j in range(3):
            weight_ref[j * TILE : (j + 1) * TILE, s * TILE : (s + 1) * TILE] = spatial_ref[2 - s, j]

    def one(f, _):
        out = convolve(flat(grad_ref[f]), weight_ref[...], rows, columns, True)
        out = out + flat(cot_ref[f]).astype(jnp.float32)
        out_ref[f] = out.astype(jnp.bfloat16).reshape(out_ref.shape[1:])
        return 0

    lax.fori_loop(0, frames, one, 0)


def sum_and_copy(got_ref, out_ref):
    total = got_ref[0].astype(jnp.float32)
    for i in range(1, got_ref.shape[0]):
        total = total + got_ref[i].astype(jnp.float32)
    total = total.astype(jnp.bfloat16)
    for i in range(out_ref.shape[0]):
        out_ref[i] = total


def call(body, name, outs, args, scratch=(), flops=0):
    moved_bytes = sum(a.size * a.dtype.itemsize for a in (*args, *outs))
    whole = pl.BlockSpec(memory_space=pltpu.VMEM)
    return pl.pallas_call(
        body,
        name=name,
        out_shape=outs,
        in_specs=[whole] * len(args),
        out_specs=[whole] * len(outs),
        scratch_shapes=list(scratch),
        compiler_params=pltpu.CompilerParams(vmem_limit_bytes=48 * 1024 * 1024),
        cost_estimate=pl.CostEstimate(
            flops=flops, bytes_accessed=moved_bytes, transcendentals=0
        ),
    )(*args)


def shards(inputs, spatial_kernel, temporal_kernel, norm_gain, norm_shift, cotangent):
    x, cot = inputs[0], cotangent[0]
    frames, rows, columns, channels = x.shape
    ext = rows + 2
    reps, time_devices, height_devices = (lax.axis_size(a) for a in ("rep", "tm", "height"))
    per_frame = float(rows * height_devices * columns * (channels // GROUPS))
    bf16, f32 = jnp.bfloat16, jnp.float32
    out = jax.ShapeDtypeStruct
    frame = (columns, channels)
    gain, shift = norm_gain[None], norm_shift[None]
    weight = pltpu.VMEM((3 * channels, 3 * channels), bf16)
    conv = 2 * 9 * channels * channels * columns

    up = [(i, i + 1) for i in range(height_devices - 1)]
    down = [(j, i) for i, j in up]
    before = lax.ppermute(jnp.concatenate([x[:, rows - 2 :], cot[:, rows - 2 :]], 0), "height", up)
    after = lax.ppermute(jnp.concatenate([x[:, :2], cot[:, :2]], 0), "height", down)
    onward = [(i, i + 1) for i in range(time_devices - 1)]
    back = [(j, i) for i, j in onward]
    last = jnp.concatenate([before[2:4], x[2:4], after[2:4]], 1)
    prev = lax.ppermute(last, "tm", onward)
    first = jnp.concatenate(
        [
            jnp.concatenate([before[:2], before[4:6]], 0),
            jnp.concatenate([x[:2], cot[:2]], 0),
            jnp.concatenate([after[:2], after[4:6]], 0),
        ],
        1,
    )
    following = lax.ppermute(first, "tm", back)

    (feature,) = call(
        own_features,
        "own_features",
        [out((frames, ext) + frame, bf16)],
        (x, before, after, spatial_kernel),
        [weight],
        conv * frames * ext,
    )
    peers = time_devices * height_devices
    prior, mixed, payload = call(
        mixed_and_sums,
        "mixed_and_sums",
        [
            out((2, ext) + frame, bf16),
            out((frames, ext) + frame, f32),
            out((2 * peers, channels), f32),
        ],
        (feature, prev, spatial_kernel, temporal_kernel),
        [weight],
        conv * frames * ext,
    )
    share = ("tm", "height")
    got = lax.all_to_all(payload, share, 0, 0, tiled=True)
    mixed_next, xt, ft = call(
        next_and_turned,
        "next_and_turned",
        [
            out((2, ext) + frame, f32),
            out((frames, 3 * channels, rows * columns), bf16),
            out((frames, 3 * channels, rows * columns), bf16),
        ],
        (following, feature, prior, x, before, after, spatial_kernel, temporal_kernel),
        [weight, pltpu.VMEM((2, ext) + frame, bf16)],
        conv * 2 * ext,
    )
    stats, payload, parts = call(
        functools.partial(statistics_and_sums, time_devices, height_devices, per_frame),
        "statistics_and_sums",
        [
            out((2 * frames * time_devices, channels), f32),
            out((2 * peers, channels), f32),
            out((16, channels), f32),
        ],
        (got, mixed, cot, gain, shift),
    )
    got = lax.all_to_all(payload, share, 0, 0, tiled=True)
    scaled, outputs = call(
        functools.partial(outputs_and_grads, time_devices),
        "outputs_and_grads",
        [out((frames + 2, ext) + frame, f32), out((frames, rows) + frame, bf16)],
        (stats, mixed, mixed_next, x, cot, before, after, following, gain, shift),
    )
    ends = ("rep", "height")
    pieces = reps * height_devices
    feature_grad, partial = call(
        functools.partial(parameter_grads, time_devices, height_devices, per_frame),
        "parameter_grads",
        [
            out((frames, ext) + frame, bf16),
            out((pieces, 12 * TILE // pieces + 8, channels), bf16),
        ],
        (got, stats, scaled, mixed, mixed_next, xt, ft, temporal_kernel, parts),
        [
            pltpu.VMEM((2 * frames * time_devices, channels), f32),
            pltpu.VMEM((frames + 2, ext) + frame, bf16),
        ],
        conv * frames * rows * 2,
    )
    partial = lax.all_to_all(partial, ends, 0, 0, tiled=True)
    (grad_inputs,) = call(
        input_grads,
        "input_grads",
        [out((frames, rows) + frame, bf16)],
        (feature_grad, cot, spatial_kernel),
        [weight],
        conv * frames * rows,
    )
    piece = partial.shape[1:]
    (partial,) = call(sum_and_copy, "sum_first", [out((time_devices,) + piece, bf16)], (partial,))
    partial = lax.all_to_all(partial, "tm", 0, 0, tiled=True)
    (partial,) = call(sum_and_copy, "sum_second", [out((pieces,) + piece, bf16)], (partial,))
    sums = lax.all_to_all(partial, ends, 0, 0, tiled=True).astype(f32)
    pixel_total = reps * frames * time_devices * rows * height_devices * columns
    scale = 1.0 / math.sqrt(pixel_total)
    body = piece[0] - 8
    grads = (sums[:, :body] * scale).reshape(12, channels, channels)
    spatial_sum = grads[:9].reshape(3, 3, channels, channels).swapaxes(0, 1)
    return (
        outputs[None],
        grad_inputs[None],
        spatial_sum,
        grads[9:],
        sums[0, body] * scale,
        sums[1, body] * scale,
    )


def solution(mesh):
    in_specs = (
        P("rep", "tm", "height", None, None),
        P(),
        P(),
        P(),
        P(),
        P("rep", "tm", "height", None, None),
    )
    out_specs = (
        P("rep", "tm", "height", None, None),
        P("rep", "tm", "height", None, None),
        P(),
        P(),
        P(),
        P(),
    )
    return jax.shard_map(shards, mesh=mesh, in_specs=in_specs, out_specs=out_specs, check_vma=False)
```

time: 735 us -> 160 us (0.22)
  waiting for transfers between devices: 471 us -> 29.5 us
  blocking collectives: 190 us -> 40.6 us
  starting transfers between devices: 17 us -> 51.2 us
  Pallas kernels: 0 us -> 19.9 us
  matrix products: 14.7 us -> 0 us
  between operations: 15.2 us -> 0.93 us
  other arithmetic: 14.4 us -> 1.63 us
    psum x1 -> x0, waiting for transfers between devices: 464 us -> none  [shards(): lax.psum((spatial_part, temporal_part, gain_part, shift_part), ('rep', 't...]
    psum x3 -> x0, blocking collectives: 140 us -> none  [the longest x1 108 us: shards(): lax.psum((spatial_part, temporal_part, gain_part, shift_part), ('rep', 't...]
    unnamed x2 -> x0, blocking collectives: 50 us -> none
    all_to_all x0 -> x2, blocking collectives: none -> 40.6 us  [the longest x1 22.9 us: shards(): partial = lax.all_to_all(partial, 'tm', 0, 0, tiled=True)]
    all_to_all x0 -> x3, starting transfers between devices: none -> 36.4 us  [the longest x2 29.2 us: shards(): got = lax.all_to_all(payload, share, 0, 0, tiled=True)]
    all_to_all x0 -> x3, waiting for transfers between devices: none -> 25.4 us  [the longest x2 16.9 us: shards(): got = lax.all_to_all(payload, share, 0, 0, tiled=True)]
    pallas_call x0 -> x9, Pallas kernels: none -> 19.9 us  [call(): pl.pallas_call(body, name=name, out_shape=outs, in_specs=[whole] * len(ar...]
    dot_general x36 -> x0, matrix products: 14.7 us -> none  [the longest x9 3.81 us: shards(): jnp.einsum('frwd,cd->frwc', back, spatial_kernel[row_tap, col_tap], prefe...]
  transfers between devices with their start and end apart: 7 -> 7, of which waited for: 3 -> 4; matrix products, arithmetic and copies ran while one was open for 1% -> 1% of each run, Pallas kernels for 0% -> 7%
where the time goes in v2:
time: 160 us; the launch traced here: 159 us
  starting transfers between devices  51.2 us (32%)
  blocking collectives  40.6 us (25%)
  waiting for transfers between devices  29.5 us (18%)
  Pallas kernels  19.9 us (12%)
  local copies, waits for them, and re-layouts  15.7 us (10%)
  other arithmetic  1.63 us (1%)
    all_to_all x2, starting transfers between devices, shards(): got = lax.all_to_all(payload, share, 0, 0, tiled=True)  29.2 us
    all_to_all x1, blocking collectives, shards(): partial = lax.all_to_all(partial, 'tm', 0, 0, tiled=True)  22.9 us
    pallas_call x9, Pallas kernels, call(): pl.pallas_call(body, name=name, out_shape=outs, in_specs=[whole] * len(ar...  19.9 us
    all_to_all x1, blocking collectives, shards(): partial = lax.all_to_all(partial, ends, 0, 0, tiled=True)  17.7 us
    all_to_all x2, waiting for transfers between devices, shards(): got = lax.all_to_all(payload, share, 0, 0, tiled=True)  16.9 us
    unnamed x42, local copies, waits for them, and re-layouts  11.9 us
    all_to_all x1, waiting for transfers between devices, shards(): sums = lax.all_to_all(partial, ends, 0, 0, tiled=True).astype(f32)  8.51 us
    all_to_all x1, starting transfers between devices, shards(): sums = lax.all_to_all(partial, ends, 0, 0, tiled=True).astype(f32)  7.18 us
  transfers between devices with their start and end apart: 7, of which 4 were waited for; matrix products, arithmetic and copies ran while one was open for 1% of the time, Pallas kernels for 7%

profile of v2, /device:TPU:1, one launch (start us, length us, event | category | flops | bytes accessed | tf_op | source)
XLA Modules:
  0.0 159.4 jit_solution(11406730467518839596)
XLA Ops:
  0.6 1.0 fusion.2
  1.6 0.0 copy-start
  1.6 0.0 copy-start.14
  1.6 4.7 %collective-permute-start = (bf16[8,2,32,128]{3,2,1,0:T(8,128)(2,1)S(1)}, bf16[8,2,32,128]{3,2,1,0:T(8,128)(2,1)S(1)}, u32[]{:S(2)}, u32[]{:S(2)}) collective-permute-start(bf16[8,2,32,128]{3,2,1,0:T(8,128)(2,1)S(1)} %pad_maximum_fusion.1), channel_id=1, source_target_pairs={{0,1},{1,2},{2,3},{3,4},{4,5},{5,6},{6,7},{8,9},{9,10},{10,11},{11... | collective-permute-start | bytes 393224 | tf_op jit(solution)/shard_map/ppermute | solution.py:459
  6.4 5.5 %collective-permute-start.1 = (bf16[8,2,32,128]{3,2,1,0:T(8,128)(2,1)S(1)}, bf16[8,2,32,128]{3,2,1,0:T(8,128)(2,1)S(1)}, u32[]{:S(2)}, u32[]{:S(2)}) collective-permute-start(bf16[8,2,32,128]{3,2,1,0:T(8,128)(2,1)S(1)} %pad_maximum_fusion.2), channel_id=1, source_target_pairs={{1,0},{2,1},{3,2},{4,3},{5,4},{6,5},{7,6},{9,8},{10,9},{11,10},{12... | collective-permute-start | bytes 393224 | tf_op jit(solution)/shard_map/ppermute | solution.py:460
  11.9 1.2 slice_bitcast_fusion.1
  13.0 0.0 collective-permute-done.1.after_ref
  13.1 0.0 copy-start.7
  13.1 0.0 collective-permute-done.before_ref
  13.1 0.0 copy-start.5
  13.1 0.0 copy-start.11
  13.2 3.3 %collective-permute-start.2 = (bf16[2,20,32,128]{3,2,1,0:T(8,128)(2,1)S(1)}, bf16[2,20,32,128]{3,2,1,0:T(8,128)(2,1)S(1)}, u32[]{:S(2)}, u32[]{:S(2)}) collective-permute-start(bf16[2,20,32,128]{3,2,1,0:T(8,128)(2,1)S(1)} %pad_maximum_fusion), channel_id=1, source_target_pairs={{0,8},{8,16},{16,24},{24,32},{32,40},{40,48},{48,56},{56,64},{64,7... | collective-permute-start | bytes 983048 | tf_op jit(solution)/shard_map/ppermute | solution.py:464
  16.5 0.0 copy-done
  16.5 0.0 copy-done.14
  16.5 1.7 %own_features.1.feature_ref = bf16[4,18,32,128]{3,2,1,0:T(8,128)(2,1)S(1)} custom-call(bf16[4,16,32,128]{3,2,1,0:T(8,128)(2,1)S(1)} %bitcast.26, bf16[8,2,32,128]{3,2,1,0:T(8,128)(2,1)S(1)} %collective-permute-done.before_ref, bf16[8,2,32,128]{3,2,1,0:T(8,128)(2,1)S(1)} %collective-permute-done.1.after_ref, bf16[3,3,128,128]{3,2,1,0:T(8,128)(2,1)S(1)} %copy-done.14), custom_call_target="tpu_custom_call" | custom-call | flops 679477248 | bytes 1671168 | tf_op jit(solution)/shard_map/own_features/pallas_call | solution.py:430
  18.3 0.0 copy-done.7
  18.3 0.0 copy-done.5
  18.3 0.0 copy-start.1
  18.3 0.0 copy-start.19
  18.3 0.0 copy-start.20
  18.3 4.1 %collective-permute-done.2.prev_ref = bf16[2,20,32,128]{3,2,1,0:T(8,128)(2,1)S(1)} collective-permute-done((bf16[2,20,32,128]{3,2,1,0:T(8,128)(2,1)S(1)}, bf16[2,20,32,128]{3,2,1,0:T(8,128)(2,1)S(1)}, u32[]{:S(2)}, u32[]{:S(2)}) %collective-permute-start.2) | collective-permute-done | bytes 327712 | tf_op jit(solution)/shard_map/ppermute | solution.py:464
  22.4 0.0 copy-done.11
  22.4 2.4 %mixed_and_sums.1 = (bf16[2,18,32,128]{3,2,1,0:T(8,128)(2,1)S(1)}, f32[4,18,32,128]{3,2,1,0:T(8,128)S(1)}, f32[256,128]{1,0:T(8,128)}) custom-call(bf16[4,18,32,128]{3,2,1,0:T(8,128)(2,1)S(1)} %own_features.1.feature_ref, bf16[2,20,32,128]{3,2,1,0:T(8,128)(2,1)S(1)} %collective-permute-done.2.prev_ref, bf16[3,3,128,128]{3,2,1,0:T(8,128)(2,1)S(1)} %copy-done.14, ...), custom_call_target="tpu_custom_call" | custom-call | flops 679477248 | bytes 2916352 | tf_op jit(solution)/shard_map/mixed_and_sums/pallas_call | solution.py:430
  24.8 0.0 copy-start.9
  24.8 0.8 copy-done.9
  25.7 0.7 copy-done.17
  26.4 21.4 %all-to-all-start = ((f32[128,2,128]{2,1,0:T(2,128)}), f32[128,2,128]{2,1,0:T(2,128)S(1)}, u32[]{:S(2)}, u32[]{:S(2)}) async-start(f32[128,2,128]{2,1,0:T(2,128)} %bitcast.3), calls=%async_computation | async-start | bytes 262144 | tf_op jit(solution)/shard_map/all_to_all | solution.py:497
  47.8 0.9 maximum_maximum_fusion
  48.7 1.3 collective-permute-start.3
  50.0 13.8 %all-to-all-done = f32[128,2,128]{2,1,0:T(2,128)S(1)} async-done(((f32[128,2,128]{2,1,0:T(2,128)}), f32[128,2,128]{2,1,0:T(2,128)S(1)}, u32[]{:S(2)}, u32[]{:S(2)}) %all-to-all-start) | async-done | bytes 131104 | tf_op jit(solution)/shard_map/all_to_all | solution.py:497
  63.8 0.0 copy-done.1
  63.8 0.0 copy-done.19
  63.8 0.0 copy-done.20
  63.8 2.2 %statistics_and_sums.1 = (f32[128,128]{1,0:T(8,128)S(1)}, f32[256,128]{1,0:T(8,128)}, f32[16,128]{1,0:T(8,128)S(1)}) custom-call(f32[256,128]{1,0:T(8,128)S(1)} %bitcast.33, f32[4,18,32,128]{3,2,1,0:T(8,128)S(1)} %get-tuple-element.20.mixed_ref, bf16[4,16,32,128]{3,2,1,0:T(8,128)(2,1)S(1)} %bitcast.30, f32[1,128]{1,0:T(1,128)S(1)} %bitcast.34, ...), custom_call_target="tpu_custom_call" | custom-call | bytes 2040832 | tf_op jit(solution)/shard_map/statistics_and_sums/pallas_call | solution.py:430
  65.9 7.8 %all-to-all-start.1 = ((f32[128,2,128]{2,1,0:T(2,128)}), f32[128,2,128]{2,1,0:T(2,128)}, u32[]{:S(2)}, u32[]{:S(2)}) async-start(f32[128,2,128]{2,1,0:T(2,128)} %bitcast.10), calls=%async_computation.1 | async-start | bytes 262144 | tf_op jit(solution)/shard_map/all_to_all | solution.py:520
  73.8 0.0 collective-permute-done.3.next_ref
  73.8 0.0 copy-start.6
  73.8 0.9 copy-done.6
  74.7 0.9 copy-done.8
  75.6 1.1 copy-done.10
  76.7 0.9 copy-done.12
  77.6 1.0 copy-done.15
  78.5 1.0 copy-done.18
  79.5 2.9 %next_and_turned.1 = (f32[2,18,32,128]{3,2,1,0:T(8,128)S(1)}, bf16[4,384,512]{2,1,0:T(8,128)(2,1)S(1)}, bf16[4,384,512]{2,1,0:T(8,128)(2,1)}) custom-call(bf16[4,20,32,128]{3,2,1,0:T(8,128)(2,1)S(1)} %collective-permute-done.3.next_ref, bf16[4,18,32,128]{3,2,1,0:T(8,128)(2,1)S(1)} %copy-done.10, bf16[2,18,32,128]{3,2,1,0:T(8,128)(2,1)S(1)} %copy-done.18, ...), custom_call_target="tpu_custom_call" | custom-call | flops 339738624 | bytes 6455296 | tf_op jit(solution)/shard_map/next_and_turned/pallas_call | solution.py:430
  82.4 1.1 copy-done.3
  83.6 2.0 %outputs_and_grads.1 = (f32[6,18,32,128]{3,2,1,0:T(8,128)S(1)}, bf16[4,16,32,128]{3,2,1,0:T(8,128)(2,1)}) custom-call(f32[128,128]{1,0:T(8,128)S(1)} %get-tuple-element.21.stats_ref, f32[4,18,32,128]{3,2,1,0:T(8,128)S(1)} %get-tuple-element.20.mixed_ref, f32[2,18,32,128]{3,2,1,0:T(8,128)S(1)} %get-tuple-element.23.mixed_next_ref, ...), custom_call_target="tpu_custom_call" | custom-call | bytes 6095872 | tf_op jit(solution)/shard_map/outputs_and_grads/pallas_call | solution.py:430
  85.5 1.2 copy-done.2
  86.8 3.1 %all-to-all-done.1 = f32[128,2,128]{2,1,0:T(2,128)} async-done(((f32[128,2,128]{2,1,0:T(2,128)}), f32[128,2,128]{2,1,0:T(2,128)}, u32[]{:S(2)}, u32[]{:S(2)}) %all-to-all-start.1) | async-done | bytes 131104 | tf_op jit(solution)/shard_map/all_to_all | solution.py:520
  89.9 1.4 copy-done.4
  91.3 0.9 copy-done.13
  92.2 5.3 %parameter_grads.1 = (bf16[4,18,32,128]{3,2,1,0:T(8,128)(2,1)S(1)}, bf16[32,56,128]{2,1,0:T(8,128)(2,1)S(1)}) custom-call(f32[256,128]{1,0:T(8,128)} %bitcast.11.got_ref, f32[128,128]{1,0:T(8,128)S(1)} %get-tuple-element.21.stats_ref, f32[6,18,32,128]{3,2,1,0:T(8,128)} %copy-done.2, f32[4,18,32,128]{3,2,1,0:T(8,128)S(1)} %get-tuple-element.20.mixed_ref, ...), custom_call_target="tpu_custom_call" | custom-call | flops 1207959552 | bytes 8036352 | tf_op jit(solution)/shard_map/parameter_grads/pallas_call | solution.py:430
  97.5 17.7 %all_to_all.37.got_ref = bf16[32,56,128]{2,1,0:T(8,128)(2,1)S(1)} all-to-all(bf16[32,56,128]{2,1,0:T(8,128)(2,1)S(1)} %get-tuple-element.31), channel_id=1, replica_groups=mesh['rep'=4,'tm'=16,'height'=8] {'rep','height'}, dimensions={0} | all-to-all | bytes 917504 | tf_op jit(solution)/shard_map/all_to_all | solution.py:543
  115.2 0.1 sum_first.1
  115.2 22.9 %all_to_all.38.got_ref = bf16[16,56,128]{2,1,0:T(8,128)(2,1)S(1)} all-to-all(bf16[16,56,128]{2,1,0:T(8,128)(2,1)S(1)} %sum_first.1), channel_id=1, replica_groups=mesh['rep'=4,'tm'=16,'height'=8] {'tm'}, dimensions={0} | all-to-all | bytes 458752 | tf_op jit(solution)/shard_map/all_to_all | solution.py:554
  138.1 0.8 sum_second.1
  138.9 7.2 %all-to-all-start.4 = ((bf16[32,56,128]{2,1,0:T(8,128)(2,1)}), bf16[32,56,128]{2,1,0:T(8,128)(2,1)S(1)}, u32[]{:S(2)}, u32[]{:S(2)}) async-start(bf16[32,56,128]{2,1,0:T(8,128)(2,1)} %sum_second.1), calls=%async_computation.4 | async-start | bytes 917504 | tf_op jit(solution)/shard_map/all_to_all | solution.py:556
  146.1 0.0 copy-done.16
  146.1 2.5 %input_grads.1 = bf16[4,16,32,128]{3,2,1,0:T(8,128)(2,1)} custom-call(bf16[4,18,32,128]{3,2,1,0:T(8,128)(2,1)S(1)} %get-tuple-element.30.grad_ref, bf16[4,16,32,128]{3,2,1,0:T(8,128)(2,1)S(1)} %bitcast.32, bf16[3,3,128,128]{3,2,1,0:T(8,128)(2,1)S(1)} %copy-done.16), custom_call_target="tpu_custom_call" | custom-call | flops 603979776 | bytes 1933312 | tf_op jit(solution)/shard_map/input_grads/pallas_call | solution.py:430
  148.7 8.5 %all-to-all-done.4 = bf16[32,56,128]{2,1,0:T(8,128)(2,1)S(1)} async-done(((bf16[32,56,128]{2,1,0:T(8,128)(2,1)}), bf16[32,56,128]{2,1,0:T(8,128)(2,1)S(1)}, u32[]{:S(2)}, u32[]{:S(2)}) %all-to-all-start.4) | async-done | bytes 458784 | tf_op jit(solution)/shard_map/all_to_all | solution.py:556
  157.2 0.1 convert_element_type.3
  157.2 0.1 slice_multiply_fusion
  157.3 0.7 slice.101
  158.0 0.5 fusion
  158.5 0.9 copy.14
  (17 shorter events, 0.1 us)
Async XLA Ops:
  1.6 14.9 %copy-start = (bf16[1,4,16,32,128]{4,3,2,1,0:T(8,128)(2,1)S(1)}, bf16[1,4,16,32,128]{4,3,2,1,0:T(8,128)(2,1)}, u32[]{:S(2)}) copy-start(bf16[1,4,16,32,128]{4,3,2,1,0:T(8,128)(2,1)} %param.6) | copy-start | bytes 1572868
  1.6 14.9 %copy-start.14 = (bf16[3,3,128,128]{3,2,1,0:T(8,128)(2,1)S(1)}, bf16[3,3,128,128]{3,2,1,0:T(8,128)(2,1)}, u32[]{:S(2)}) copy-start(bf16[3,3,128,128]{3,2,1,0:T(8,128)(2,1)} %spatial_ref.7) | copy-start | bytes 884740
  1.6 11.4 %collective-permute-start = (bf16[8,2,32,128]{3,2,1,0:T(8,128)(2,1)S(1)}, bf16[8,2,32,128]{3,2,1,0:T(8,128)(2,1)S(1)}, u32[]{:S(2)}, u32[]{:S(2)}) collective-permute-start(bf16[8,2,32,128]{3,2,1,0:T(8,128)(2,1)S(1)} %pad_maximum_fusion.1), channel_id=1, source_target_pairs={{0,1},{1,2},{2,3},{3,4},{4,5},{5,6},{6,7},{8,9},{9,10},{10,11},{11... | collective-permute-start | bytes 393224 | tf_op jit(solution)/shard_map/ppermute | solution.py:459
  6.4 6.7 %collective-permute-start.1 = (bf16[8,2,32,128]{3,2,1,0:T(8,128)(2,1)S(1)}, bf16[8,2,32,128]{3,2,1,0:T(8,128)(2,1)S(1)}, u32[]{:S(2)}, u32[]{:S(2)}) collective-permute-start(bf16[8,2,32,128]{3,2,1,0:T(8,128)(2,1)S(1)} %pad_maximum_fusion.2), channel_id=1, source_target_pairs={{1,0},{2,1},{3,2},{4,3},{5,4},{6,5},{7,6},{9,8},{10,9},{11,10},{12... | collective-permute-start | bytes 393224 | tf_op jit(solution)/shard_map/ppermute | solution.py:460
  13.1 5.2 %copy-start.7 = (bf16[8,2,32,128]{3,2,1,0:T(8,128)(2,1)}, bf16[8,2,32,128]{3,2,1,0:T(8,128)(2,1)S(1)}, u32[]{:S(2)}) copy-start(bf16[8,2,32,128]{3,2,1,0:T(8,128)(2,1)S(1)} %collective-permute-done.1.after_ref) | copy-start | bytes 393220
  13.1 5.2 %copy-start.5 = (bf16[8,2,32,128]{3,2,1,0:T(8,128)(2,1)}, bf16[8,2,32,128]{3,2,1,0:T(8,128)(2,1)S(1)}, u32[]{:S(2)}) copy-start(bf16[8,2,32,128]{3,2,1,0:T(8,128)(2,1)S(1)} %collective-permute-done.before_ref) | copy-start | bytes 393220
  13.1 9.3 %copy-start.11 = (bf16[3,128,128]{2,1,0:T(8,128)(2,1)S(1)}, bf16[3,128,128]{2,1,0:T(8,128)(2,1)}, u32[]{:S(2)}) copy-start(bf16[3,128,128]{2,1,0:T(8,128)(2,1)} %temporal_ref.5) | copy-start | bytes 294916
  13.2 9.2 %collective-permute-start.2 = (bf16[2,20,32,128]{3,2,1,0:T(8,128)(2,1)S(1)}, bf16[2,20,32,128]{3,2,1,0:T(8,128)(2,1)S(1)}, u32[]{:S(2)}, u32[]{:S(2)}) collective-permute-start(bf16[2,20,32,128]{3,2,1,0:T(8,128)(2,1)S(1)} %pad_maximum_fusion), channel_id=1, source_target_pairs={{0,8},{8,16},{16,24},{24,32},{32,40},{40,48},{48,56},{56,64},{64,7... | collective-permute-start | bytes 983048 | tf_op jit(solution)/shard_map/ppermute | solution.py:464
  18.3 45.5 %copy-start.1 = (bf16[1,4,16,32,128]{4,3,2,1,0:T(8,128)(2,1)S(1)}, bf16[1,4,16,32,128]{4,3,2,1,0:T(8,128)(2,1)}, u32[]{:S(2)}) copy-start(bf16[1,4,16,32,128]{4,3,2,1,0:T(8,128)(2,1)} %param.11) | copy-start | bytes 1572868
  18.3 45.5 %copy-start.19 = (f32[128]{0:T(128)S(1)}, f32[128]{0:T(128)}, u32[]{:S(2)}) copy-start(f32[128]{0:T(128)} %param.9) | copy-start | bytes 1540
  18.3 45.5 %copy-start.20 = (f32[128]{0:T(128)S(1)}, f32[128]{0:T(128)}, u32[]{:S(2)}) copy-start(f32[128]{0:T(128)} %param.10) | copy-start | bytes 1540
  24.8 0.8 copy-start.9
  25.7 0.7 copy-start.17
  26.4 37.4 %all-to-all-start = ((f32[128,2,128]{2,1,0:T(2,128)}), f32[128,2,128]{2,1,0:T(2,128)S(1)}, u32[]{:S(2)}, u32[]{:S(2)}) async-start(f32[128,2,128]{2,1,0:T(2,128)} %bitcast.3), calls=%async_computation | async-start | bytes 262144 | tf_op jit(solution)/shard_map/all_to_all | solution.py:497
  48.7 25.1 %collective-permute-start.3 = (bf16[4,20,32,128]{3,2,1,0:T(8,128)(2,1)}, bf16[4,20,32,128]{3,2,1,0:T(8,128)(2,1)S(1)}, u32[]{:S(2)}, u32[]{:S(2)}) collective-permute-start(bf16[4,20,32,128]{3,2,1,0:T(8,128)(2,1)} %maximum_maximum_fusion), channel_id=1, source_target_pairs={{8,0},{16,8},{24,16},{32,24},{40,32},{48,40},{56,48},{64,56},{72,6... | collective-permute-start | bytes 1966088 | tf_op jit(solution)/shard_map/ppermute | solution.py:473
  65.9 23.9 %all-to-all-start.1 = ((f32[128,2,128]{2,1,0:T(2,128)}), f32[128,2,128]{2,1,0:T(2,128)}, u32[]{:S(2)}, u32[]{:S(2)}) async-start(f32[128,2,128]{2,1,0:T(2,128)} %bitcast.10), calls=%async_computation.1 | async-start | bytes 262144 | tf_op jit(solution)/shard_map/all_to_all | solution.py:520
  73.8 0.9 copy-start.6
  74.7 0.9 copy-start.8
  75.6 1.1 copy-start.10
  76.7 0.9 copy-start.12
  77.5 1.0 copy-start.15
  78.5 1.0 copy-start.18
  82.4 1.2 copy-start.3
  85.5 1.2 copy-start.2
  89.9 1.4 copy-start.4
  91.3 0.9 copy-start.13
  115.2 30.9 %copy-start.16 = (bf16[3,3,128,128]{3,2,1,0:T(8,128)(2,1)S(1)}, bf16[3,3,128,128]{3,2,1,0:T(8,128)(2,1)}, u32[]{:S(2)}) copy-start(bf16[3,3,128,128]{3,2,1,0:T(8,128)(2,1)} %spatial_ref.7) | copy-start | bytes 884740
  138.9 18.2 %all-to-all-start.4 = ((bf16[32,56,128]{2,1,0:T(8,128)(2,1)}), bf16[32,56,128]{2,1,0:T(8,128)(2,1)S(1)}, u32[]{:S(2)}, u32[]{:S(2)}) async-start(bf16[32,56,128]{2,1,0:T(8,128)(2,1)} %sum_second.1), calls=%async_computation.4 | async-start | bytes 917504 | tf_op jit(solution)/shard_map/all_to_all | solution.py:556

commit v3 on v2

--- a/solution.py
+++ b/solution.py
@@ -13,6 +13,7 @@
 
 EPS = 1e-05
 TILE = 128
+WIDE, NARROW = 58, 16
 
 
 def iota(shape, dim):
@@ -102,7 +103,31 @@
         out_ref[i * 8 : (i + 1) * 8] = line
 
 
-def own_features(x_ref, before_ref, after_ref, spatial_ref, feature_ref, weight_ref):
+def fetch(pairs, sems):
+    copies = [pltpu.make_async_copy(a, b, sems.at[i]) for i, (a, b) in enumerate(pairs)]
+    for copy in copies:
+        copy.start()
+    return copies
+
+
+def turned(value):
+    return value.astype(jnp.float32).T.astype(jnp.bfloat16)
+
+
+def own_features(
+    x_ref,
+    before_ref,
+    after_ref,
+    spatial_ref,
+    feature_ref,
+    late_ref,
+    xt_ref,
+    ft_ref,
+    weight_ref,
+    xt_held,
+    ft_held,
+    sems,
+):
     put_weight(weight_ref, spatial_ref)
     frames, rows, columns, _ = x_ref.shape
 
@@ -113,6 +138,22 @@
         return 0
 
     lax.fori_loop(0, frames, one, 0)
+    for f in range(frames):
+        block = jnp.concatenate(
+            [flat(before_ref[f, 1:]), flat(x_ref[f]), flat(after_ref[f, :1])], 0
+        )
+        xt_held[f] = turned(three_rows(block, rows, columns))
+        ft_held[f] = turned(flat(feature_ref[f, 1 : rows + 1]))
+    copies = fetch(
+        [
+            (feature_ref.at[pl.ds(frames - 2, 2)], late_ref),
+            (xt_held, xt_ref),
+            (ft_held, ft_ref),
+        ],
+        sems,
+    )
+    for copy in copies:
+        copy.wait()
 
 
 def mix(blocks, temporal_ref):
@@ -120,7 +161,17 @@
 
 
 def mixed_and_sums(
-    feature_ref, prev_ref, spatial_ref, temporal_ref, prior_ref, mixed_ref, out_ref, weight_ref
+    feature_ref,
+    prev_ref,
+    spatial_ref,
+    temporal_ref,
+    mixed_ref,
+    out_ref,
+    ft_ref,
+    weight_ref,
+    prior_ref,
+    ft_held,
+    sems,
 ):
     put_weight(weight_ref, spatial_ref)
     frames, rows, columns, _ = mixed_ref.shape
@@ -131,6 +182,9 @@
         return 0
 
     lax.fori_loop(0, 2, one, 0)
+    for f in range(2):
+        ft_held[f] = turned(flat(prior_ref[f, 1 : rows - 1]))
+    copies = fetch([(ft_held, ft_ref)], sems)
     firsts, seconds = [], []
     for f in range(frames):
         blocks = [
@@ -142,26 +196,36 @@
         firsts.append(inner.sum(0, keepdims=True))
         seconds.append((inner * inner).sum(0, keepdims=True))
     put_payload(out_ref, firsts, seconds)
-
-
-def next_and_turned(
+    copies[0].wait()
+
+
+def next_frames(
+    next_hbm,
+    late_hbm,
+    spatial_hbm,
+    temporal_hbm,
+    mixed_ref,
+    weight_ref,
+    held_ref,
     next_ref,
-    feature_ref,
-    prior_ref,
-    x_ref,
-    before_ref,
-    after_ref,
+    late_ref,
     spatial_ref,
     temporal_ref,
-    mixed_ref,
-    xt_ref,
-    ft_ref,
-    weight_ref,
-    held_ref,
+    sems,
 ):
+    copies = fetch(
+        [
+            (spatial_hbm, spatial_ref),
+            (next_hbm.at[pl.ds(0, 2)], next_ref),
+            (late_hbm, late_ref),
+            (temporal_hbm, temporal_ref),
+        ],
+        sems,
+    )
+    _, ext, columns, _ = mixed_ref.shape
+    copies[0].wait()
     put_weight(weight_ref, spatial_ref)
-    frames, rows, columns, _ = x_ref.shape
-    ext = rows + 2
+    copies[1].wait()
 
     def one(f, _):
         out = convolve(flat(next_ref[f]), weight_ref[...], ext, columns, False)
@@ -169,25 +233,11 @@
         return 0
 
     lax.fori_loop(0, 2, one, 0)
+    copies[2].wait()
+    copies[3].wait()
     for f in range(2):
-        blocks = [
-            flat(feature_ref[f + 2 + k]) if f + k < 2 else flat(held_ref[f + k - 2])
-            for k in range(3)
-        ]
+        blocks = [flat(late_ref[f + k]) if f + k < 2 else flat(held_ref[f + k - 2]) for k in range(3)]
         mixed_ref[f] = mix(blocks, temporal_ref).reshape(mixed_ref.shape[1:])
-
-    for f in range(frames):
-        block = jnp.concatenate(
-            [flat(before_ref[f, 1:]), flat(x_ref[f]), flat(after_ref[f, :1])], 0
-        )
-        xt_ref[f] = three_rows(block, rows, columns).astype(jnp.float32).T.astype(jnp.bfloat16)
-        seen = [
-            flat(prior_ref[f + k, 1 : rows + 1])
-            if f + k < 2
-            else flat(feature_ref[f + k - 2, 1 : rows + 1])
-            for k in range(3)
-        ]
-        ft_ref[f] = jnp.concatenate(seen, axis=1).astype(jnp.float32).T.astype(jnp.bfloat16)
 
 
 def counts(f, frames, time_devices, per_frame):
@@ -258,15 +308,29 @@
     mixed_next_ref,
     x_ref,
     cot_ref,
+    gain_ref,
+    shift_ref,
+    before_hbm,
+    after_hbm,
+    next_hbm,
+    outputs_ref,
+    scaled_hbm,
+    scaled_ref,
     before_ref,
     after_ref,
     next_ref,
-    gain_ref,
-    shift_ref,
-    scaled_ref,
-    outputs_ref,
+    in_sems,
+    out_sems,
 ):
     frames, rows, columns, _ = cot_ref.shape
+    copies = fetch(
+        [
+            (before_hbm.at[pl.ds(frames, frames)], before_ref),
+            (after_hbm.at[pl.ds(frames, frames)], after_ref),
+            (next_hbm.at[pl.ds(2, 2)], next_ref),
+        ],
+        in_sems,
+    )
     me = lax.axis_index("tm")
     following = jnp.minimum(me + 1, time_devices - 1)
     gain, shift = gain_ref[...], shift_ref[...]
@@ -277,6 +341,8 @@
         sigma = 1.0 / (1.0 + jnp.exp(-pre))
         grad = cot.astype(jnp.float32) * (sigma * (1.0 + pre * (1.0 - sigma)))
         return pre * sigma, inv_std * (grad * gain)
+
+    leaving = []
 
     for f in range(frames + 2):
         own = f < frames
@@ -289,12 +355,13 @@
             _, scaled = grads(source[g, row], cot, mean, inv_std)
             scaled_ref[f, row] = scaled
 
-        edge(0, before_ref[frames + g, 1] if own else next_ref[2 + g, 1])
-        edge(rows + 1, after_ref[frames + g, 0] if own else next_ref[2 + g, rows + 2])
+
+        if f == frames:
+            copies[2].wait()
 
         def some(i, _, f=f, g=g, own=own, mean=mean, inv_std=inv_std, source=source):
             here = pl.ds(1 + i * step, step)
-            cot = cot_ref[g, pl.ds(i * step, step)] if own else next_ref[2 + g, pl.ds(2 + i * step, step)]
+            cot = cot_ref[g, pl.ds(i * step, step)] if own else next_ref[g, pl.ds(2 + i * step, step)]
             silu, scaled = grads(flat(source[g, here]), flat(cot), mean, inv_std)
             scaled_ref[f, here] = scaled.reshape(step, columns, TILE)
             if own:
@@ -305,6 +372,16 @@
             return 0
 
         lax.fori_loop(0, rows // step, some, 0, unroll=2)
+        if f == 0:
+            copies[0].wait()
+            copies[1].wait()
+        edge(0, before_ref[g, 1] if own else next_ref[g, 1])
+        edge(rows + 1, after_ref[g, 0] if own else next_ref[g, rows + 2])
+        copy = pltpu.make_async_copy(scaled_ref.at[f], scaled_hbm.at[f], out_sems.at[f])
+        copy.start()
+        leaving.append(copy)
+    for copy in leaving:
+        copy.wait()
 
 
 def parameter_grads(
@@ -313,20 +390,41 @@
     per_frame,
     got_ref,
     stats_ref,
+    parts_ref,
+    mixed_hbm,
+    mixed_next_hbm,
+    scaled_hbm,
+    xt_hbm,
+    ft_hbm,
+    ft_prior_hbm,
+    temporal_hbm,
+    out_ref,
+    feature_grad_hbm,
+    carry_ref,
+    mixed_grad_ref,
+    feature_grad_ref,
+    mixed_ref,
     scaled_ref,
-    mixed_ref,
-    mixed_next_ref,
     xt_ref,
     ft_ref,
     temporal_ref,
-    parts_ref,
-    feature_grad_ref,
-    out_ref,
-    carry_ref,
-    mixed_grad_ref,
+    sems,
+    out_sems,
 ):
-    frames, ext, columns, _ = mixed_ref.shape
+    frames, ext, columns, _ = feature_grad_ref.shape
     rows = ext - 2
+    copies = fetch(
+        [
+            (mixed_hbm, mixed_ref.at[pl.ds(0, frames)]),
+            (mixed_next_hbm, mixed_ref.at[pl.ds(frames, 2)]),
+            (scaled_hbm, scaled_ref),
+            (temporal_hbm, temporal_ref),
+            (xt_hbm, xt_ref),
+            (ft_hbm, ft_ref.at[pl.ds(2, frames)]),
+            (ft_prior_hbm, ft_ref.at[pl.ds(0, 2)]),
+        ],
+        sems,
+    )
     me, level = lax.axis_index("tm"), lax.axis_index("height")
     following = jnp.minimum(me + 1, time_devices - 1)
     here = per_device_sums(got_ref[...], time_devices, height_devices, False)
@@ -350,33 +448,43 @@
             run = run + values[f]
             at = (2 * f + kind) * time_devices
             carry_ref[at : at + time_devices] = run
+    for copy in copies[:3]:
+        copy.wait()
     exists = (me < time_devices - 1).astype(jnp.float32)
     for f in range(frames + 2):
         own = f < frames
         at, g = (me, f) if own else (following, f - frames)
         first = carry_ref[pl.ds(2 * g * time_devices + at, 1)]
         second = 2.0 * carry_ref[pl.ds((2 * g + 1) * time_devices + at, 1)]
-        source = mixed_ref if own else mixed_next_ref
-
-        def some(i, _, f=f, g=g, own=own, first=first, second=second, source=source):
+
+        def some(i, _, f=f, own=own, first=first, second=second):
             at = pl.ds(i * 3, 3)
-            grad = flat(scaled_ref[f, at]) + first + flat(source[g, at]) * second
+            grad = flat(scaled_ref[f, at]) + first + flat(mixed_ref[f, at]) * second
             if not own:
                 grad = grad * exists
             mixed_grad_ref[f, at] = grad.astype(jnp.bfloat16).reshape(3, columns, TILE)
             return 0
 
         lax.fori_loop(0, ext // 3, some, 0, unroll=3)
-    turned = jnp.concatenate([temporal_ref[k] for k in range(3)], axis=1)
+    copies[3].wait()
+    back = jnp.concatenate([temporal_ref[k] for k in range(3)], axis=1)
+    for copy in copies[4:]:
+        copy.wait()
+    leaving = []
     place = iota((ext * columns, TILE), 0) // columns
     outside = ((place == 0) & (level == 0)) | ((place == ext - 1) & (level == height_devices - 1))
     spatial = jnp.zeros((3 * TILE, 3 * TILE), jnp.float32)
     temporal = jnp.zeros((3 * TILE, TILE), jnp.float32)
     for f in range(frames):
         blocks = [flat(mixed_grad_ref[f + 2 - k]) for k in range(3)]
-        grad = dot(jnp.concatenate(blocks, axis=1), turned, True)
+        grad = dot(jnp.concatenate(blocks, axis=1), back, True)
         grad = jnp.where(outside, 0.0, grad).astype(jnp.bfloat16)
         feature_grad_ref[f] = grad.reshape(ext, columns, TILE)
+        copy = pltpu.make_async_copy(
+            feature_grad_ref.at[f], feature_grad_hbm.at[f], out_sems.at[f]
+        )
+        copy.start()
+        leaving.append(copy)
         inner = grad[columns : (rows + 1) * columns]
         wide = inner.astype(jnp.float32)
         shifted = jnp.concatenate(
@@ -388,7 +496,7 @@
             axis=1,
         )
         spatial = spatial + dot(xt_ref[f], shifted)
-        temporal = temporal + dot(ft_ref[f], flat(mixed_grad_ref[f, 1 : rows + 1]))
+        temporal = temporal + dot(flat(ft_ref[f : f + 3]), flat(mixed_grad_ref[f, 1 : rows + 1]))
     pieces = out_ref.shape[0]
     piece = 12 * TILE // pieces
     blocks = [spatial[:, j * TILE : (j + 1) * TILE] for j in range(3)] + [temporal]
@@ -398,6 +506,8 @@
         tail = parts_ref[8 * min(p, 1) : 8 * min(p, 1) + 8]
         tail = jnp.where((iota((8, TILE), 0) == 0) & (p < 2), tail, 0.0)
         out_ref[p, piece : piece + 8] = tail.astype(jnp.bfloat16)
+    for copy in leaving:
+        copy.wait()
 
 
 def input_grads(grad_ref, cot_ref, spatial_ref, out_ref, weight_ref):
@@ -424,21 +534,40 @@
         out_ref[i] = total
 
 
-def call(body, name, outs, args, scratch=(), flops=0):
-    moved_bytes = sum(a.size * a.dtype.itemsize for a in (*args, *outs))
-    whole = pl.BlockSpec(memory_space=pltpu.VMEM)
+def finish(scale, got_ref, spatial_ref, temporal_ref, gain_ref, shift_ref):
+    pieces, piece = got_ref.shape[0], got_ref.shape[1] - 8
+    for p in range(pieces):
+        value = got_ref[p].astype(jnp.float32) * scale
+        if p < 2:
+            (gain_ref, shift_ref)[p][...] = value[piece : piece + 1]
+        at = p * piece
+        while at < (p + 1) * piece:
+            block, row = at // TILE, at % TILE
+            size = min(TILE - row, (p + 1) * piece - at)
+            part = value[at - p * piece : at - p * piece + size]
+            if block < 9:
+                spatial_ref[block % 3, block // 3, row : row + size] = part
+            else:
+                temporal_ref[block - 9, row : row + size] = part
+            at += size
+
+
+def call(body, name, outs, args, scratch=(), flops=0, far=(), far_outs=(), limit=WIDE):
+    everything = (*args, *far, *outs, *far_outs)
+    moved_bytes = sum(a.size * a.dtype.itemsize for a in everything)
+    near, away = pl.BlockSpec(memory_space=pltpu.VMEM), pl.BlockSpec(memory_space=pl.ANY)
     return pl.pallas_call(
         body,
         name=name,
-        out_shape=outs,
-        in_specs=[whole] * len(args),
-        out_specs=[whole] * len(outs),
+        out_shape=[*outs, *far_outs],
+        in_specs=[near] * len(args) + [away] * len(far),
+        out_specs=[near] * len(outs) + [away] * len(far_outs),
         scratch_shapes=list(scratch),
-        compiler_params=pltpu.CompilerParams(vmem_limit_bytes=48 * 1024 * 1024),
+        compiler_params=pltpu.CompilerParams(vmem_limit_bytes=limit * 1024 * 1024),
         cost_estimate=pl.CostEstimate(
             flops=flops, bytes_accessed=moved_bytes, transcendentals=0
         ),
-    )(*args)
+    )(*args, *far)
 
 
 def shards(inputs, spatial_kernel, temporal_kernel, norm_gain, norm_shift, cotangent):
@@ -472,40 +601,49 @@
     )
     following = lax.ppermute(first, "tm", back)
 
-    (feature,) = call(
+    dma = lambda count: pltpu.SemaphoreType.DMA((count,))
+    turned_x = out((frames, 3 * channels, rows * columns), bf16)
+    turned_own = out((frames, channels, rows * columns), bf16)
+    turned_prior = out((2, channels, rows * columns), bf16)
+    held = lambda a: pltpu.VMEM(a.shape, a.dtype)
+    two = out((2, ext) + frame, bf16)
+    feature, late, xt, ft = call(
         own_features,
         "own_features",
         [out((frames, ext) + frame, bf16)],
         (x, before, after, spatial_kernel),
-        [weight],
+        [weight, held(turned_x), held(turned_own), dma(3)],
         conv * frames * ext,
+        far_outs=[two, turned_x, turned_own],
     )
     peers = time_devices * height_devices
-    prior, mixed, payload = call(
+    mixed, payload, ft_prior = call(
         mixed_and_sums,
         "mixed_and_sums",
-        [
-            out((2, ext) + frame, bf16),
-            out((frames, ext) + frame, f32),
-            out((2 * peers, channels), f32),
-        ],
+        [out((frames, ext) + frame, f32), out((2 * peers, channels), f32)],
         (feature, prev, spatial_kernel, temporal_kernel),
-        [weight],
+        [weight, held(two), held(turned_prior), dma(1)],
         conv * frames * ext,
+        far_outs=[turned_prior],
     )
     share = ("tm", "height")
     got = lax.all_to_all(payload, share, 0, 0, tiled=True)
-    mixed_next, xt, ft = call(
-        next_and_turned,
-        "next_and_turned",
-        [
-            out((2, ext) + frame, f32),
-            out((frames, 3 * channels, rows * columns), bf16),
-            out((frames, 3 * channels, rows * columns), bf16),
-        ],
-        (following, feature, prior, x, before, after, spatial_kernel, temporal_kernel),
-        [weight, pltpu.VMEM((2, ext) + frame, bf16)],
+    (mixed_next,) = call(
+        next_frames,
+        "next_frames",
+        [out((2, ext) + frame, f32)],
+        (),
+        [
+            weight,
+            held(two),
+            pltpu.VMEM((2, rows + 4) + frame, bf16),
+            held(two),
+            held(spatial_kernel),
+            held(temporal_kernel),
+            dma(4),
+        ],
         conv * 2 * ext,
+        far=(following, late, spatial_kernel, temporal_kernel),
     )
     stats, payload, parts = call(
         functools.partial(statistics_and_sums, time_devices, height_devices, per_frame),
@@ -516,29 +654,49 @@
             out((16, channels), f32),
         ],
         (got, mixed, cot, gain, shift),
+        limit=NARROW,
     )
     got = lax.all_to_all(payload, share, 0, 0, tiled=True)
-    scaled, outputs = call(
+    scaled_shape = out((frames + 2, ext) + frame, f32)
+    outputs, scaled = call(
         functools.partial(outputs_and_grads, time_devices),
         "outputs_and_grads",
-        [out((frames + 2, ext) + frame, f32), out((frames, rows) + frame, bf16)],
-        (stats, mixed, mixed_next, x, cot, before, after, following, gain, shift),
+        [out((frames, rows) + frame, bf16)],
+        (stats, mixed, mixed_next, x, cot, gain, shift),
+        [
+            held(scaled_shape),
+            pltpu.VMEM((frames, 2) + frame, bf16),
+            pltpu.VMEM((frames, 2) + frame, bf16),
+            pltpu.VMEM((2, rows + 4) + frame, bf16),
+            dma(3),
+            dma(frames + 2),
+        ],
+        far=(before, after, following),
+        far_outs=[scaled_shape],
     )
     ends = ("rep", "height")
     pieces = reps * height_devices
-    feature_grad, partial = call(
+    own_two = out((frames, ext) + frame, bf16)
+    partial, feature_grad = call(
         functools.partial(parameter_grads, time_devices, height_devices, per_frame),
         "parameter_grads",
-        [
-            out((frames, ext) + frame, bf16),
-            out((pieces, 12 * TILE // pieces + 8, channels), bf16),
-        ],
-        (got, stats, scaled, mixed, mixed_next, xt, ft, temporal_kernel, parts),
+        [out((pieces, 12 * TILE // pieces + 8, channels), bf16)],
+        (got, stats, parts),
         [
             pltpu.VMEM((2 * frames * time_devices, channels), f32),
             pltpu.VMEM((frames + 2, ext) + frame, bf16),
+            held(own_two),
+            held(scaled_shape),
+            held(scaled_shape),
+            held(turned_x),
+            pltpu.VMEM((frames + 2, channels, rows * columns), bf16),
+            held(temporal_kernel),
+            dma(7),
+            dma(frames),
         ],
         conv * frames * rows * 2,
+        far=(mixed, mixed_next, scaled, xt, ft, ft_prior, temporal_kernel),
+        far_outs=[own_two],
     )
     partial = lax.all_to_all(partial, ends, 0, 0, tiled=True)
     (grad_inputs,) = call(
@@ -550,22 +708,30 @@
         conv * frames * rows,
     )
     piece = partial.shape[1:]
-    (partial,) = call(sum_and_copy, "sum_first", [out((time_devices,) + piece, bf16)], (partial,))
+    (partial,) = call(sum_and_copy, "sum_first", [out((time_devices,) + piece, bf16)], (partial,), limit=NARROW)
     partial = lax.all_to_all(partial, "tm", 0, 0, tiled=True)
-    (partial,) = call(sum_and_copy, "sum_second", [out((pieces,) + piece, bf16)], (partial,))
-    sums = lax.all_to_all(partial, ends, 0, 0, tiled=True).astype(f32)
+    (partial,) = call(sum_and_copy, "sum_second", [out((pieces,) + piece, bf16)], (partial,), limit=NARROW)
+    sums = lax.all_to_all(partial, ends, 0, 0, tiled=True)
     pixel_total = reps * frames * time_devices * rows * height_devices * columns
-    scale = 1.0 / math.sqrt(pixel_total)
-    body = piece[0] - 8
-    grads = (sums[:, :body] * scale).reshape(12, channels, channels)
-    spatial_sum = grads[:9].reshape(3, 3, channels, channels).swapaxes(0, 1)
+    spatial_sum, temporal_sum, gain_sum, shift_sum = call(
+        functools.partial(finish, 1.0 / math.sqrt(pixel_total)),
+        "finish",
+        [
+            out(spatial_kernel.shape, f32),
+            out(temporal_kernel.shape, f32),
+            out((1, channels), f32),
+            out((1, channels), f32),
+        ],
+        (sums,),
+        limit=NARROW,
+    )
     return (
         outputs[None],
         grad_inputs[None],
         spatial_sum,
-        grads[9:],
-        sums[0, body] * scale,
-        sums[1, body] * scale,
+        temporal_sum,
+        gain_sum[0],
+        shift_sum[0],
     )
 
 

time: 160 us -> 158 us (0.988)
  Pallas kernels: 19.9 us -> 33.8 us
  local copies, waits for them, and re-layouts: 15.7 us -> 5.63 us
  blocking collectives: 40.6 us -> 37.2 us
    pallas_call x9 -> x10, Pallas kernels: 19.9 us -> 33.8 us  [call(): pl.pallas_call(body, name=name, out_shape=[*outs, *far_outs], in_specs=[n...]
    unnamed x42 -> x22, local copies, waits for them, and re-layouts: 11.9 us -> 3.47 us
    all_to_all x2, waiting for transfers between devices: 16.9 us -> 21.3 us  [shards(): got = lax.all_to_all(payload, share, 0, 0, tiled=True)]
    all_to_all x1, blocking collectives: 22.9 us -> 18.8 us  [shards(): partial = lax.all_to_all(partial, 'tm', 0, 0, tiled=True)]
    ppermute x1, waiting for transfers between devices: 4.11 us -> 0.2 us  [shards(): prev = lax.ppermute(last, 'tm', onward)]
  transfers between devices with their start and end apart: 7 -> 7, of which waited for: 4 -> 4; matrix products, arithmetic and copies ran while one was open for 1% -> 1% of each run, Pallas kernels for 7% -> 13%
where the time goes in v3:
time: 158 us; the launch traced here: 157 us
  starting transfers between devices  50.6 us (32%)
  blocking collectives  37.2 us (24%)
  Pallas kernels  33.8 us (21%)
  waiting for transfers between devices  28.7 us (18%)
  local copies, waits for them, and re-layouts  5.63 us (4%)
    pallas_call x10, Pallas kernels, call(): pl.pallas_call(body, name=name, out_shape=[*outs, *far_outs], in_specs=[n...  33.8 us
    all_to_all x2, starting transfers between devices, shards(): got = lax.all_to_all(payload, share, 0, 0, tiled=True)  28.9 us
    all_to_all x2, waiting for transfers between devices, shards(): got = lax.all_to_all(payload, share, 0, 0, tiled=True)  21.3 us
    all_to_all x1, blocking collectives, shards(): partial = lax.all_to_all(partial, 'tm', 0, 0, tiled=True)  18.8 us
    all_to_all x1, blocking collectives, shards(): partial = lax.all_to_all(partial, ends, 0, 0, tiled=True)  18.4 us
    all_to_all x1, waiting for transfers between devices, shards(): sums = lax.all_to_all(partial, ends, 0, 0, tiled=True)  7.22 us
    all_to_all x1, starting transfers between devices, shards(): sums = lax.all_to_all(partial, ends, 0, 0, tiled=True)  7.17 us
    ppermute x1, starting transfers between devices, shards(): lax.ppermute(jnp.concatenate([x[:, :2], cot[:, :2]], 0), 'height', down)  5.46 us
  transfers between devices with their start and end apart: 7, of which 4 were waited for; matrix products, arithmetic and copies ran while one was open for 1% of the time, Pallas kernels for 13%

profile of v3, /device:TPU:1, one launch (start us, length us, event | category | flops | bytes accessed | tf_op | source)
XLA Modules:
  0.0 156.9 jit_solution(921012591437473294)
XLA Ops:
  0.6 1.0 fusion
  1.6 4.6 %collective-permute-start = (bf16[8,2,32,128]{3,2,1,0:T(8,128)(2,1)S(1)}, bf16[8,2,32,128]{3,2,1,0:T(8,128)(2,1)S(1)}, u32[]{:S(2)}, u32[]{:S(2)}) collective-permute-start(bf16[8,2,32,128]{3,2,1,0:T(8,128)(2,1)S(1)} %pad_maximum_fusion.1), channel_id=1, source_target_pairs={{0,1},{1,2},{2,3},{3,4},{4,5},{5,6},{6,7},{8,9},{9,10},{10,11},{11... | collective-permute-start | bytes 393224 | tf_op jit(solution)/shard_map/ppermute | solution.py:588
  6.2 5.5 %collective-permute-start.1 = (bf16[8,2,32,128]{3,2,1,0:T(8,128)(2,1)S(1)}, bf16[8,2,32,128]{3,2,1,0:T(8,128)(2,1)S(1)}, u32[]{:S(2)}, u32[]{:S(2)}) collective-permute-start(bf16[8,2,32,128]{3,2,1,0:T(8,128)(2,1)S(1)} %pad_maximum_fusion.2), channel_id=1, source_target_pairs={{1,0},{2,1},{3,2},{4,3},{5,4},{6,5},{7,6},{9,8},{10,9},{11,10},{12... | collective-permute-start | bytes 393224 | tf_op jit(solution)/shard_map/ppermute | solution.py:589
  11.7 1.2 slice_bitcast_fusion.1
  12.9 0.0 collective-permute-done.1.after_ref.after_hbm
  12.9 0.0 copy-start.9
  12.9 0.0 collective-permute-done.before_ref.before_hbm
  12.9 0.0 copy-start.8
  13.0 3.2 %collective-permute-start.2 = (bf16[2,20,32,128]{3,2,1,0:T(8,128)(2,1)S(1)}, bf16[2,20,32,128]{3,2,1,0:T(8,128)(2,1)S(1)}, u32[]{:S(2)}, u32[]{:S(2)}) collective-permute-start(bf16[2,20,32,128]{3,2,1,0:T(8,128)(2,1)S(1)} %pad_maximum_fusion), channel_id=1, source_target_pairs={{0,8},{8,16},{16,24},{24,32},{32,40},{40,48},{48,56},{56,64},{64,7... | collective-permute-start | bytes 983048 | tf_op jit(solution)/shard_map/ppermute | solution.py:593
  16.2 0.0 copy-done.9
  16.2 0.0 copy-done.8
  16.2 5.7 %own_features.1 = (bf16[4,18,32,128]{3,2,1,0:T(8,128)(2,1)}, bf16[2,18,32,128]{3,2,1,0:T(8,128)(2,1)}, bf16[4,384,512]{2,1,0:T(8,128)(2,1)}, bf16[4,128,512]{2,1,0:T(8,128)(2,1)}) custom-call(bf16[4,16,32,128]{3,2,1,0:T(8,128)(2,1)} %bitcast.28, bf16[8,2,32,128]{3,2,1,0:T(8,128)(2,1)} %copy-done.8, bf16[8,2,32,128]{3,2,1,0:T(8,128)(2,1)} %copy-done.9, ...), custom_call_target="tpu_custom_call" | custom-call | flops 679477248 | bytes 4063232 | tf_op jit(solution)/shard_map/own_features/pallas_call | solution.py:559
  21.9 0.2 collective-permute-done.2.prev_ref
  22.1 0.0 copy-start.10
  22.1 0.7 copy-done.10
  22.9 0.0 copy-start.1
  22.9 0.0 copy-start.4
  22.9 0.0 copy-start.5
  22.9 4.8 %mixed_and_sums.1 = (f32[4,18,32,128]{3,2,1,0:T(8,128)}, f32[256,128]{1,0:T(8,128)}, bf16[2,128,512]{2,1,0:T(8,128)(2,1)}) custom-call(bf16[4,18,32,128]{3,2,1,0:T(8,128)(2,1)} %get-tuple-element.24.feature_ref, bf16[2,20,32,128]{3,2,1,0:T(8,128)(2,1)} %copy-done.10, bf16[3,3,128,128]{3,2,1,0:T(8,128)(2,1)} %spatial_ref.5, bf16[3,128,128]{2,1,0:T(8,128)(2,1)} %temporal_hbm.3), custom_call_target="tpu_custom_call" | custom-call | flops 679477248 | bytes 2883584 | tf_op jit(solution)/shard_map/mixed_and_sums/pallas_call | solution.py:559
  27.7 0.0 copy-start
  27.7 21.5 %all-to-all-start = ((f32[128,2,128]{2,1,0:T(2,128)}), f32[128,2,128]{2,1,0:T(2,128)S(1)}, u32[]{:S(2)}, u32[]{:S(2)}) async-start(f32[128,2,128]{2,1,0:T(2,128)} %bitcast.31), calls=%async_computation | async-start | bytes 262144 | tf_op jit(solution)/shard_map/all_to_all | solution.py:630
  49.2 0.1 maximum_maximum_fusion
  49.3 1.3 collective-permute-start.3
  50.6 14.6 %all-to-all-done = f32[128,2,128]{2,1,0:T(2,128)S(1)} async-done(((f32[128,2,128]{2,1,0:T(2,128)}), f32[128,2,128]{2,1,0:T(2,128)S(1)}, u32[]{:S(2)}, u32[]{:S(2)}) %all-to-all-start) | async-done | bytes 131104 | tf_op jit(solution)/shard_map/all_to_all | solution.py:630
  65.2 0.0 copy-done.1
  65.2 0.0 copy-done.4
  65.2 0.0 copy-done.5
  65.2 0.0 copy-done
  65.2 2.2 %statistics_and_sums.1 = (f32[128,128]{1,0:T(8,128)S(1)}, f32[256,128]{1,0:T(8,128)}, f32[16,128]{1,0:T(8,128)S(1)}) custom-call(f32[256,128]{1,0:T(8,128)S(1)} %bitcast.22, f32[4,18,32,128]{3,2,1,0:T(8,128)S(1)} %copy-done, bf16[4,16,32,128]{3,2,1,0:T(8,128)(2,1)S(1)} %bitcast.21, f32[1,128]{1,0:T(1,128)S(1)} %bitcast.24, f32[1,128]{1,0:T(1,128)S(1)} %bitcast.26), custom_call_target="tpu_custom_call" | custom-call | bytes 2040832 | tf_op jit(solution)/shard_map/statistics_and_sums/pallas_call | solution.py:559
  67.4 0.0 copy-start.2
  67.4 0.6 copy-done.2
  68.0 0.0 copy-start.3
  68.0 0.6 copy-done.3
  68.6 7.3 %all-to-all-start.1 = ((f32[128,2,128]{2,1,0:T(2,128)}), f32[128,2,128]{2,1,0:T(2,128)S(1)}, u32[]{:S(2)}, u32[]{:S(2)}) async-start(f32[128,2,128]{2,1,0:T(2,128)} %bitcast.10), calls=%async_computation.1 | async-start | bytes 262144 | tf_op jit(solution)/shard_map/all_to_all | solution.py:659
  76.0 0.0 collective-permute-done.3.next_hbm
  76.0 0.0 copy-start.6
  76.0 0.8 copy-done.6
  76.8 3.1 %next_frames.1.mixed_next_ref.mixed_next_hbm = f32[2,18,32,128]{3,2,1,0:T(8,128)} custom-call(bf16[4,20,32,128]{3,2,1,0:T(8,128)(2,1)} %copy-done.6, bf16[2,18,32,128]{3,2,1,0:T(8,128)(2,1)} %get-tuple-element.28.late_hbm, bf16[3,3,128,128]{3,2,1,0:T(8,128)(2,1)} %spatial_ref.5, bf16[3,128,128]{2,1,0:T(8,128)(2,1)} %temporal_hbm.3), custom_call_target="tpu_custom_call" | custom-call | flops 339738624 | bytes 1933312 | tf_op jit(solution)/shard_map/next_frames/pallas_call | solution.py:559
  80.0 5.3 %outputs_and_grads.1 = (bf16[4,16,32,128]{3,2,1,0:T(8,128)(2,1)}, f32[6,18,32,128]{3,2,1,0:T(8,128)}) custom-call(f32[128,128]{1,0:T(8,128)} %copy-done.2, f32[4,18,32,128]{3,2,1,0:T(8,128)} %get-tuple-element.26.mixed_ref.mixed_hbm, f32[2,18,32,128]{3,2,1,0:T(8,128)} %next_frames.1.mixed_next_ref.mixed_next_hbm, bf16[4,16,32,128]{3,2,1,0:T(8,128)(2,1)} %bitcast.29, ...), custom_call_target="tpu_custom_call" | custom-call | bytes 6095872 | tf_op jit(solution)/shard_map/outputs_and_grads/pallas_call | solution.py:559
  85.3 6.6 %all-to-all-done.1 = f32[128,2,128]{2,1,0:T(2,128)S(1)} async-done(((f32[128,2,128]{2,1,0:T(2,128)}), f32[128,2,128]{2,1,0:T(2,128)S(1)}, u32[]{:S(2)}, u32[]{:S(2)}) %all-to-all-start.1) | async-done | bytes 131104 | tf_op jit(solution)/shard_map/all_to_all | solution.py:659
  91.9 0.0 copy-start.7
  91.9 0.7 copy-done.7
  92.6 7.1 %parameter_grads.1 = (bf16[32,56,128]{2,1,0:T(8,128)(2,1)}, bf16[4,18,32,128]{3,2,1,0:T(8,128)(2,1)}) custom-call(f32[256,128]{1,0:T(8,128)} %bitcast.30, f32[128,128]{1,0:T(8,128)} %copy-done.2, f32[16,128]{1,0:T(8,128)} %copy-done.3, f32[4,18,32,128]{3,2,1,0:T(8,128)} %get-tuple-element.26.mixed_ref.mixed_hbm, ...), custom_call_target="tpu_custom_call" | custom-call | flops 1207959552 | bytes 7249920 | tf_op jit(solution)/shard_map/parameter_grads/pallas_call | solution.py:559
  99.7 18.4 %all_to_all.37.got_ref = bf16[32,56,128]{2,1,0:T(8,128)(2,1)S(1)} all-to-all(bf16[32,56,128]{2,1,0:T(8,128)(2,1)} %get-tuple-element.37), channel_id=1, replica_groups=mesh['rep'=4,'tm'=16,'height'=8] {'rep','height'}, dimensions={0} | all-to-all | bytes 917504 | tf_op jit(solution)/shard_map/all_to_all | solution.py:701
  118.1 0.1 sum_first.1
  118.2 18.8 %all_to_all.38.got_ref = bf16[16,56,128]{2,1,0:T(8,128)(2,1)S(1)} all-to-all(bf16[16,56,128]{2,1,0:T(8,128)(2,1)S(1)} %sum_first.1), channel_id=1, replica_groups=mesh['rep'=4,'tm'=16,'height'=8] {'tm'}, dimensions={0} | all-to-all | bytes 458752 | tf_op jit(solution)/shard_map/all_to_all | solution.py:712
  137.0 0.8 sum_second.1
  137.8 7.2 %all-to-all-start.4 = ((bf16[32,56,128]{2,1,0:T(8,128)(2,1)}), bf16[32,56,128]{2,1,0:T(8,128)(2,1)S(1)}, u32[]{:S(2)}, u32[]{:S(2)}) async-start(bf16[32,56,128]{2,1,0:T(8,128)(2,1)} %sum_second.1), calls=%async_computation.4 | async-start | bytes 917504 | tf_op jit(solution)/shard_map/all_to_all | solution.py:714
  145.0 3.8 %input_grads.1 = bf16[4,16,32,128]{3,2,1,0:T(8,128)(2,1)} custom-call(bf16[4,18,32,128]{3,2,1,0:T(8,128)(2,1)} %get-tuple-element.36.grad_ref, bf16[4,16,32,128]{3,2,1,0:T(8,128)(2,1)} %bitcast.20, bf16[3,3,128,128]{3,2,1,0:T(8,128)(2,1)} %spatial_ref.5), custom_call_target="tpu_custom_call" | custom-call | flops 603979776 | bytes 1933312 | tf_op jit(solution)/shard_map/input_grads/pallas_call | solution.py:559
  148.8 7.2 %all-to-all-done.4.got_ref = bf16[32,56,128]{2,1,0:T(8,128)(2,1)S(1)} async-done(((bf16[32,56,128]{2,1,0:T(8,128)(2,1)}), bf16[32,56,128]{2,1,0:T(8,128)(2,1)S(1)}, u32[]{:S(2)}, u32[]{:S(2)}) %all-to-all-start.4) | async-done | bytes 458784 | tf_op jit(solution)/shard_map/all_to_all | solution.py:714
  156.0 0.9 finish.1
  (5 shorter events, 0.1 us)
Async XLA Ops:
  1.6 11.3 %collective-permute-start = (bf16[8,2,32,128]{3,2,1,0:T(8,128)(2,1)S(1)}, bf16[8,2,32,128]{3,2,1,0:T(8,128)(2,1)S(1)}, u32[]{:S(2)}, u32[]{:S(2)}) collective-permute-start(bf16[8,2,32,128]{3,2,1,0:T(8,128)(2,1)S(1)} %pad_maximum_fusion.1), channel_id=1, source_target_pairs={{0,1},{1,2},{2,3},{3,4},{4,5},{5,6},{6,7},{8,9},{9,10},{10,11},{11... | collective-permute-start | bytes 393224 | tf_op jit(solution)/shard_map/ppermute | solution.py:588
  6.2 6.7 %collective-permute-start.1 = (bf16[8,2,32,128]{3,2,1,0:T(8,128)(2,1)S(1)}, bf16[8,2,32,128]{3,2,1,0:T(8,128)(2,1)S(1)}, u32[]{:S(2)}, u32[]{:S(2)}) collective-permute-start(bf16[8,2,32,128]{3,2,1,0:T(8,128)(2,1)S(1)} %pad_maximum_fusion.2), channel_id=1, source_target_pairs={{1,0},{2,1},{3,2},{4,3},{5,4},{6,5},{7,6},{9,8},{10,9},{11,10},{12... | collective-permute-start | bytes 393224 | tf_op jit(solution)/shard_map/ppermute | solution.py:589
  12.9 3.3 %copy-start.9 = (bf16[8,2,32,128]{3,2,1,0:T(8,128)(2,1)}, bf16[8,2,32,128]{3,2,1,0:T(8,128)(2,1)S(1)}, u32[]{:S(2)}) copy-start(bf16[8,2,32,128]{3,2,1,0:T(8,128)(2,1)S(1)} %collective-permute-done.1.after_ref.after_hbm) | copy-start | bytes 393220
  12.9 3.3 %copy-start.8 = (bf16[8,2,32,128]{3,2,1,0:T(8,128)(2,1)}, bf16[8,2,32,128]{3,2,1,0:T(8,128)(2,1)S(1)}, u32[]{:S(2)}) copy-start(bf16[8,2,32,128]{3,2,1,0:T(8,128)(2,1)S(1)} %collective-permute-done.before_ref.before_hbm) | copy-start | bytes 393220
  13.0 9.1 %collective-permute-start.2 = (bf16[2,20,32,128]{3,2,1,0:T(8,128)(2,1)S(1)}, bf16[2,20,32,128]{3,2,1,0:T(8,128)(2,1)S(1)}, u32[]{:S(2)}, u32[]{:S(2)}) collective-permute-start(bf16[2,20,32,128]{3,2,1,0:T(8,128)(2,1)S(1)} %pad_maximum_fusion), channel_id=1, source_target_pairs={{0,8},{8,16},{16,24},{24,32},{32,40},{40,48},{48,56},{56,64},{64,7... | collective-permute-start | bytes 983048 | tf_op jit(solution)/shard_map/ppermute | solution.py:593
  22.1 0.7 copy-start.10
  22.9 42.3 %copy-start.1 = (bf16[1,4,16,32,128]{4,3,2,1,0:T(8,128)(2,1)S(1)}, bf16[1,4,16,32,128]{4,3,2,1,0:T(8,128)(2,1)}, u32[]{:S(2)}) copy-start(bf16[1,4,16,32,128]{4,3,2,1,0:T(8,128)(2,1)} %param.11) | copy-start | bytes 1572868
  22.9 42.3 %copy-start.4 = (f32[128]{0:T(128)S(1)}, f32[128]{0:T(128)}, u32[]{:S(2)}) copy-start(f32[128]{0:T(128)} %param.9) | copy-start | bytes 1540
  22.9 42.3 %copy-start.5 = (f32[128]{0:T(128)S(1)}, f32[128]{0:T(128)}, u32[]{:S(2)}) copy-start(f32[128]{0:T(128)} %param.10) | copy-start | bytes 1540
  27.7 37.5 %copy-start = (f32[4,18,32,128]{3,2,1,0:T(8,128)S(1)}, f32[4,18,32,128]{3,2,1,0:T(8,128)}, u32[]{:S(2)}) copy-start(f32[4,18,32,128]{3,2,1,0:T(8,128)} %get-tuple-element.26.mixed_ref.mixed_hbm) | copy-start | bytes 3538948
  27.7 37.5 %all-to-all-start = ((f32[128,2,128]{2,1,0:T(2,128)}), f32[128,2,128]{2,1,0:T(2,128)S(1)}, u32[]{:S(2)}, u32[]{:S(2)}) async-start(f32[128,2,128]{2,1,0:T(2,128)} %bitcast.31), calls=%async_computation | async-start | bytes 262144 | tf_op jit(solution)/shard_map/all_to_all | solution.py:630
  49.3 26.7 %collective-permute-start.3 = (bf16[4,20,32,128]{3,2,1,0:T(8,128)(2,1)S(1)}, bf16[4,20,32,128]{3,2,1,0:T(8,128)(2,1)S(1)}, u32[]{:S(2)}, u32[]{:S(2)}) collective-permute-start(bf16[4,20,32,128]{3,2,1,0:T(8,128)(2,1)S(1)} %maximum_maximum_fusion), channel_id=1, source_target_pairs={{8,0},{16,8},{24,16},{32,24},{40,32},{48,40},{56,48},{64,56},{72,6... | collective-permute-start | bytes 1966088 | tf_op jit(solution)/shard_map/ppermute | solution.py:602
  67.4 0.6 copy-start.2
  68.0 0.6 copy-start.3
  68.6 23.3 %all-to-all-start.1 = ((f32[128,2,128]{2,1,0:T(2,128)}), f32[128,2,128]{2,1,0:T(2,128)S(1)}, u32[]{:S(2)}, u32[]{:S(2)}) async-start(f32[128,2,128]{2,1,0:T(2,128)} %bitcast.10), calls=%async_computation.1 | async-start | bytes 262144 | tf_op jit(solution)/shard_map/all_to_all | solution.py:659
  76.0 0.9 copy-start.6
  91.9 0.7 copy-start.7
  137.8 18.2 %all-to-all-start.4 = ((bf16[32,56,128]{2,1,0:T(8,128)(2,1)}), bf16[32,56,128]{2,1,0:T(8,128)(2,1)S(1)}, u32[]{:S(2)}, u32[]{:S(2)}) async-start(bf16[32,56,128]{2,1,0:T(8,128)(2,1)} %sum_second.1), calls=%async_computation.4 | async-start | bytes 917504 | tf_op jit(solution)/shard_map/all_to_all | solution.py:714

commit v4 on v3

--- a/solution.py
+++ b/solution.py
@@ -115,18 +115,7 @@
 
 
 def own_features(
-    x_ref,
-    before_ref,
-    after_ref,
-    spatial_ref,
-    feature_ref,
-    late_ref,
-    xt_ref,
-    ft_ref,
-    weight_ref,
-    xt_held,
-    ft_held,
-    sems,
+    x_ref, before_ref, after_ref, spatial_ref, feature_ref, far_ref, weight_ref, sems
 ):
     put_weight(weight_ref, spatial_ref)
     frames, rows, columns, _ = x_ref.shape
@@ -138,22 +127,40 @@
         return 0
 
     lax.fori_loop(0, frames, one, 0)
+    for copy in fetch([(feature_ref, far_ref)], sems):
+        copy.wait()
+
+
+def turn(
+    x_ref,
+    before_ref,
+    after_ref,
+    prev_ref,
+    feature_ref,
+    spatial_ref,
+    xt_ref,
+    ft_ref,
+    weight_ref,
+    prior_ref,
+):
+    put_weight(weight_ref, spatial_ref)
+    frames, rows, columns, _ = x_ref.shape
+    size = rows * columns
+
+    def one(f, _):
+        out = convolve(flat(prev_ref[f]), weight_ref[...], rows + 2, columns, False)
+        prior_ref[f] = out.astype(jnp.bfloat16).reshape(prior_ref.shape[1:])
+        return 0
+
+    lax.fori_loop(0, 2, one, 0)
+    for f in range(frames + 2):
+        seen = prior_ref[f, 1 : rows + 1] if f < 2 else feature_ref[f - 2, 1 : rows + 1]
+        ft_ref[:, f * size : (f + 1) * size] = turned(flat(seen))
     for f in range(frames):
         block = jnp.concatenate(
             [flat(before_ref[f, 1:]), flat(x_ref[f]), flat(after_ref[f, :1])], 0
         )
-        xt_held[f] = turned(three_rows(block, rows, columns))
-        ft_held[f] = turned(flat(feature_ref[f, 1 : rows + 1]))
-    copies = fetch(
-        [
-            (feature_ref.at[pl.ds(frames - 2, 2)], late_ref),
-            (xt_held, xt_ref),
-            (ft_held, ft_ref),
-        ],
-        sems,
-    )
-    for copy in copies:
-        copy.wait()
+        xt_ref[:, f * size : (f + 1) * size] = turned(three_rows(block, rows, columns))
 
 
 def mix(blocks, temporal_ref):
@@ -167,11 +174,8 @@
     temporal_ref,
     mixed_ref,
     out_ref,
-    ft_ref,
     weight_ref,
     prior_ref,
-    ft_held,
-    sems,
 ):
     put_weight(weight_ref, spatial_ref)
     frames, rows, columns, _ = mixed_ref.shape
@@ -182,9 +186,6 @@
         return 0
 
     lax.fori_loop(0, 2, one, 0)
-    for f in range(2):
-        ft_held[f] = turned(flat(prior_ref[f, 1 : rows - 1]))
-    copies = fetch([(ft_held, ft_ref)], sems)
     firsts, seconds = [], []
     for f in range(frames):
         blocks = [
@@ -196,7 +197,6 @@
         firsts.append(inner.sum(0, keepdims=True))
         seconds.append((inner * inner).sum(0, keepdims=True))
     put_payload(out_ref, firsts, seconds)
-    copies[0].wait()
 
 
 def next_frames(
@@ -217,7 +217,7 @@
         [
             (spatial_hbm, spatial_ref),
             (next_hbm.at[pl.ds(0, 2)], next_ref),
-            (late_hbm, late_ref),
+            (late_hbm.at[pl.ds(late_hbm.shape[0] - 2, 2)], late_ref),
             (temporal_hbm, temporal_ref),
         ],
         sems,
@@ -256,9 +256,8 @@
     shift_ref,
     stats_ref,
     out_ref,
-    parts_ref,
 ):
-    frames, rows, columns, _ = cot_ref.shape
+    frames, rows, _, _ = cot_ref.shape
     me = lax.axis_index("tm")
     got = got_ref[...]
     here = per_device_sums(got, time_devices, height_devices, False)
@@ -298,7 +297,8 @@
         seconds.append(b.sum(0, keepdims=True))
     put_payload(out_ref, [a * gain for a in firsts], [b * gain for b in seconds])
     total_a, total_b = sum(firsts[1:], firsts[0]), sum(seconds[1:], seconds[0])
-    parts_ref[...] = jnp.where(iota((16, TILE), 0) < 8, total_b, total_a)
+    at = 2 * frames * time_devices
+    stats_ref[at : at + 16] = jnp.where(iota((16, TILE), 0) < 8, total_b, total_a)
 
 
 def outputs_and_grads(
@@ -390,13 +390,11 @@
     per_frame,
     got_ref,
     stats_ref,
-    parts_ref,
     mixed_hbm,
     mixed_next_hbm,
     scaled_hbm,
     xt_hbm,
     ft_hbm,
-    ft_prior_hbm,
     temporal_hbm,
     out_ref,
     feature_grad_hbm,
@@ -408,6 +406,7 @@
     xt_ref,
     ft_ref,
     temporal_ref,
+    shifted_ref,
     sems,
     out_sems,
 ):
@@ -420,8 +419,7 @@
             (scaled_hbm, scaled_ref),
             (temporal_hbm, temporal_ref),
             (xt_hbm, xt_ref),
-            (ft_hbm, ft_ref.at[pl.ds(2, frames)]),
-            (ft_prior_hbm, ft_ref.at[pl.ds(0, 2)]),
+            (ft_hbm, ft_ref),
         ],
         sems,
     )
@@ -468,13 +466,10 @@
         lax.fori_loop(0, ext // 3, some, 0, unroll=3)
     copies[3].wait()
     back = jnp.concatenate([temporal_ref[k] for k in range(3)], axis=1)
-    for copy in copies[4:]:
-        copy.wait()
     leaving = []
     place = iota((ext * columns, TILE), 0) // columns
     outside = ((place == 0) & (level == 0)) | ((place == ext - 1) & (level == height_devices - 1))
-    spatial = jnp.zeros((3 * TILE, 3 * TILE), jnp.float32)
-    temporal = jnp.zeros((3 * TILE, TILE), jnp.float32)
+    size = rows * columns
     for f in range(frames):
         blocks = [flat(mixed_grad_ref[f + 2 - k]) for k in range(3)]
         grad = dot(jnp.concatenate(blocks, axis=1), back, True)
@@ -487,7 +482,7 @@
         leaving.append(copy)
         inner = grad[columns : (rows + 1) * columns]
         wide = inner.astype(jnp.float32)
-        shifted = jnp.concatenate(
+        shifted_ref[f * size : (f + 1) * size] = jnp.concatenate(
             [
                 moved(wide, -1, columns).astype(jnp.bfloat16),
                 inner,
@@ -495,15 +490,19 @@
             ],
             axis=1,
         )
-        spatial = spatial + dot(xt_ref[f], shifted)
-        temporal = temporal + dot(flat(ft_ref[f : f + 3]), flat(mixed_grad_ref[f, 1 : rows + 1]))
+    for copy in copies[4:]:
+        copy.wait()
+    inner = flat(mixed_grad_ref[:frames, 1 : rows + 1])
+    temporal = [dot(ft_ref[:, k * size : (k + frames) * size], inner) for k in range(3)]
+    spatial = dot(xt_ref[...], shifted_ref[...])
     pieces = out_ref.shape[0]
     piece = 12 * TILE // pieces
-    blocks = [spatial[:, j * TILE : (j + 1) * TILE] for j in range(3)] + [temporal]
+    blocks = [spatial[:, j * TILE : (j + 1) * TILE] for j in range(3)] + temporal
     whole = jnp.concatenate(blocks, axis=0).astype(jnp.bfloat16)
     for p in range(pieces):
         out_ref[p, :piece] = whole[p * piece : (p + 1) * piece]
-        tail = parts_ref[8 * min(p, 1) : 8 * min(p, 1) + 8]
+        at = 2 * frames * time_devices + 8 * min(p, 1)
+        tail = stats_ref[at : at + 8]
         tail = jnp.where((iota((8, TILE), 0) == 0) & (p < 2), tail, 0.0)
         out_ref[p, piece : piece + 8] = tail.astype(jnp.bfloat16)
     for copy in leaving:
@@ -552,13 +551,12 @@
             at += size
 
 
-def call(body, name, outs, args, scratch=(), flops=0, far=(), far_outs=(), limit=WIDE):
+def call(body, outs, args, scratch=(), flops=0, far=(), far_outs=(), limit=WIDE):
     everything = (*args, *far, *outs, *far_outs)
     moved_bytes = sum(a.size * a.dtype.itemsize for a in everything)
     near, away = pl.BlockSpec(memory_space=pltpu.VMEM), pl.BlockSpec(memory_space=pl.ANY)
     return pl.pallas_call(
         body,
-        name=name,
         out_shape=[*outs, *far_outs],
         in_specs=[near] * len(args) + [away] * len(far),
         out_specs=[near] * len(outs) + [away] * len(far_outs),
@@ -602,35 +600,40 @@
     following = lax.ppermute(first, "tm", back)
 
     dma = lambda count: pltpu.SemaphoreType.DMA((count,))
-    turned_x = out((frames, 3 * channels, rows * columns), bf16)
-    turned_own = out((frames, channels, rows * columns), bf16)
-    turned_prior = out((2, channels, rows * columns), bf16)
+    turned_x = out((3 * channels, frames * rows * columns), bf16)
+    turned_features = out((channels, (frames + 2) * rows * columns), bf16)
     held = lambda a: pltpu.VMEM(a.shape, a.dtype)
     two = out((2, ext) + frame, bf16)
-    feature, late, xt, ft = call(
+    own_two = out((frames, ext) + frame, bf16)
+    feature, late = call(
         own_features,
-        "own_features",
-        [out((frames, ext) + frame, bf16)],
+        [own_two],
         (x, before, after, spatial_kernel),
-        [weight, held(turned_x), held(turned_own), dma(3)],
+        [weight, dma(1)],
         conv * frames * ext,
-        far_outs=[two, turned_x, turned_own],
+        far_outs=[own_two],
+        limit=NARROW,
     )
     peers = time_devices * height_devices
-    mixed, payload, ft_prior = call(
+    mixed, payload = call(
         mixed_and_sums,
-        "mixed_and_sums",
         [out((frames, ext) + frame, f32), out((2 * peers, channels), f32)],
         (feature, prev, spatial_kernel, temporal_kernel),
-        [weight, held(two), held(turned_prior), dma(1)],
+        [weight, held(two)],
         conv * frames * ext,
-        far_outs=[turned_prior],
+        limit=NARROW,
     )
     share = ("tm", "height")
     got = lax.all_to_all(payload, share, 0, 0, tiled=True)
+    xt, ft = call(
+        turn,
+        [turned_x, turned_features],
+        (x, before, after, prev, late, spatial_kernel),
+        [weight, held(two)],
+        conv * frames * ext,
+    )
     (mixed_next,) = call(
         next_frames,
-        "next_frames",
         [out((2, ext) + frame, f32)],
         (),
         [
@@ -645,13 +648,11 @@
         conv * 2 * ext,
         far=(following, late, spatial_kernel, temporal_kernel),
     )
-    stats, payload, parts = call(
+    stats, payload = call(
         functools.partial(statistics_and_sums, time_devices, height_devices, per_frame),
-        "statistics_and_sums",
-        [
-            out((2 * frames * time_devices, channels), f32),
+        [
+            out((2 * frames * time_devices + 16, channels), f32),
             out((2 * peers, channels), f32),
-            out((16, channels), f32),
         ],
         (got, mixed, cot, gain, shift),
         limit=NARROW,
@@ -660,7 +661,6 @@
     scaled_shape = out((frames + 2, ext) + frame, f32)
     outputs, scaled = call(
         functools.partial(outputs_and_grads, time_devices),
-        "outputs_and_grads",
         [out((frames, rows) + frame, bf16)],
         (stats, mixed, mixed_next, x, cot, gain, shift),
         [
@@ -676,12 +676,10 @@
     )
     ends = ("rep", "height")
     pieces = reps * height_devices
-    own_two = out((frames, ext) + frame, bf16)
     partial, feature_grad = call(
         functools.partial(parameter_grads, time_devices, height_devices, per_frame),
-        "parameter_grads",
         [out((pieces, 12 * TILE // pieces + 8, channels), bf16)],
-        (got, stats, parts),
+        (got, stats),
         [
             pltpu.VMEM((2 * frames * time_devices, channels), f32),
             pltpu.VMEM((frames + 2, ext) + frame, bf16),
@@ -689,33 +687,32 @@
             held(scaled_shape),
             held(scaled_shape),
             held(turned_x),
-            pltpu.VMEM((frames + 2, channels, rows * columns), bf16),
+            held(turned_features),
             held(temporal_kernel),
-            dma(7),
+            pltpu.VMEM((frames * rows * columns, 3 * channels), bf16),
+            dma(6),
             dma(frames),
         ],
         conv * frames * rows * 2,
-        far=(mixed, mixed_next, scaled, xt, ft, ft_prior, temporal_kernel),
+        far=(mixed, mixed_next, scaled, xt, ft, temporal_kernel),
         far_outs=[own_two],
     )
     partial = lax.all_to_all(partial, ends, 0, 0, tiled=True)
     (grad_inputs,) = call(
         input_grads,
-        "input_grads",
         [out((frames, rows) + frame, bf16)],
         (feature_grad, cot, spatial_kernel),
         [weight],
         conv * frames * rows,
     )
     piece = partial.shape[1:]
-    (partial,) = call(sum_and_copy, "sum_first", [out((time_devices,) + piece, bf16)], (partial,), limit=NARROW)
+    (partial,) = call(sum_and_copy, [out((time_devices,) + piece, bf16)], (partial,), limit=NARROW)
     partial = lax.all_to_all(partial, "tm", 0, 0, tiled=True)
-    (partial,) = call(sum_and_copy, "sum_second", [out((pieces,) + piece, bf16)], (partial,), limit=NARROW)
+    (partial,) = call(sum_and_copy, [out((pieces,) + piece, bf16)], (partial,), limit=NARROW)
     sums = lax.all_to_all(partial, ends, 0, 0, tiled=True)
     pixel_total = reps * frames * time_devices * rows * height_devices * columns
     spatial_sum, temporal_sum, gain_sum, shift_sum = call(
         functools.partial(finish, 1.0 / math.sqrt(pixel_total)),
-        "finish",
         [
             out(spatial_kernel.shape, f32),
             out(temporal_kernel.shape, f32),

time: 158 us -> 158 us (level)
  blocking collectives: 37.2 us -> 41.4 us
  Pallas kernels: 33.8 us -> 30.9 us
  waiting for transfers between devices: 28.7 us -> 26.6 us
    all_to_all x2, waiting for transfers between devices: 21.3 us -> 16.2 us  [shards(): got = lax.all_to_all(payload, share, 0, 0, tiled=True)]
    all_to_all x1, blocking collectives: 18.8 us -> 23.1 us  [shards(): partial = lax.all_to_all(partial, 'tm', 0, 0, tiled=True)]
    ppermute x1, waiting for transfers between devices: 0.2 us -> 3.18 us  [shards(): prev = lax.ppermute(last, 'tm', onward)]
    pallas_call x10 -> x11, Pallas kernels: 33.8 us -> 30.9 us  [call(): pl.pallas_call(body, out_shape=[*outs, *far_outs], in_specs=[near] * len(...]
    unnamed x22 -> x34, local copies, waits for them, and re-layouts: 3.47 us -> 3 us
  transfers between devices with their start and end apart: 7 -> 7, of which waited for: 4 -> 4; matrix products, arithmetic and copies ran while one was open for 1% -> 2% of each run, Pallas kernels for 13% -> 13%
where the time goes in v4:
time: 158 us; the launch traced here: 157 us
  starting transfers between devices  49.8 us (32%)
  blocking collectives  41.4 us (26%)
  Pallas kernels  30.9 us (20%)
  waiting for transfers between devices  26.6 us (17%)
  local copies, waits for them, and re-layouts  6.54 us (4%)
    pallas_call x11, Pallas kernels, call(): pl.pallas_call(body, out_shape=[*outs, *far_outs], in_specs=[near] * len(...  30.9 us
    all_to_all x2, starting transfers between devices, shards(): got = lax.all_to_all(payload, share, 0, 0, tiled=True)  28.8 us
    all_to_all x1, blocking collectives, shards(): partial = lax.all_to_all(partial, 'tm', 0, 0, tiled=True)  23.1 us
    all_to_all x1, blocking collectives, shards(): partial = lax.all_to_all(partial, ends, 0, 0, tiled=True)  18.3 us
    all_to_all x2, waiting for transfers between devices, shards(): got = lax.all_to_all(payload, share, 0, 0, tiled=True)  16.2 us
    all_to_all x1, waiting for transfers between devices, shards(): sums = lax.all_to_all(partial, ends, 0, 0, tiled=True)  7.22 us
    all_to_all x1, starting transfers between devices, shards(): sums = lax.all_to_all(partial, ends, 0, 0, tiled=True)  7.17 us
    ppermute x1, starting transfers between devices, shards(): lax.ppermute(jnp.concatenate([x[:, :2], cot[:, :2]], 0), 'height', down)  5.46 us
  transfers between devices with their start and end apart: 7, of which 4 were waited for; matrix products, arithmetic and copies ran while one was open for 2% of the time, Pallas kernels for 13%

profile of v4, /device:TPU:1, one launch (start us, length us, event | category | flops | bytes accessed | tf_op | source)
XLA Modules:
  0.0 157.2 jit_solution(727508992579967709)
XLA Ops:
  0.6 1.0 fusion
  1.6 0.0 copy-start.2
  1.6 0.0 copy-start.7
  1.6 4.7 %collective-permute-start = (bf16[8,2,32,128]{3,2,1,0:T(8,128)(2,1)S(1)}, bf16[8,2,32,128]{3,2,1,0:T(8,128)(2,1)S(1)}, u32[]{:S(2)}, u32[]{:S(2)}) collective-permute-start(bf16[8,2,32,128]{3,2,1,0:T(8,128)(2,1)S(1)} %pad_maximum_fusion.1), channel_id=1, source_target_pairs={{0,1},{1,2},{2,3},{3,4},{4,5},{5,6},{6,7},{8,9},{9,10},{10,11},{11... | collective-permute-start | bytes 393224 | tf_op jit(solution)/shard_map/ppermute | solution.py:586
  6.4 5.5 %collective-permute-start.1 = (bf16[8,2,32,128]{3,2,1,0:T(8,128)(2,1)S(1)}, bf16[8,2,32,128]{3,2,1,0:T(8,128)(2,1)S(1)}, u32[]{:S(2)}, u32[]{:S(2)}) collective-permute-start(bf16[8,2,32,128]{3,2,1,0:T(8,128)(2,1)S(1)} %pad_maximum_fusion.2), channel_id=1, source_target_pairs={{1,0},{2,1},{3,2},{4,3},{5,4},{6,5},{7,6},{9,8},{10,9},{11,10},{12... | collective-permute-start | bytes 393224 | tf_op jit(solution)/shard_map/ppermute | solution.py:587
  11.9 1.9 %slice_bitcast_fusion.1 = (bf16[2,16,32,128]{3,2,1,0:T(8,128)(2,1)S(1)}, bf16[2,16,32,128]{3,2,1,0:T(8,128)(2,1)S(1)}, bf16[2,16,32,128]{3,2,1,0:T(8,128)(2,1)}) fusion(bf16[1,4,16,32,128]{4,3,2,1,0:T(8,128)(2,1)} %param.6, bf16[1,4,16,32,128]{4,3,2,1,0:T(8,128)(2,1)} %param.11), kind=kLoop, calls=%fused_computation.3 | loop fusion | bytes 1572864 | tf_op jit(solution)/shard_map/slice | solution.py:595
  13.7 0.0 collective-permute-done.before_ref.before_hbm
  13.7 0.0 copy-start.4
  13.8 0.0 collective-permute-done.1.after_ref.after_hbm
  13.8 0.0 copy-start.5
  13.8 0.7 fusion.3
  14.5 0.0 copy-start.6
  14.5 2.4 %collective-permute-start.2 = (bf16[2,20,32,128]{3,2,1,0:T(8,128)(2,1)S(1)}, bf16[2,20,32,128]{3,2,1,0:T(8,128)(2,1)S(1)}, u32[]{:S(2)}, u32[]{:S(2)}) collective-permute-start(bf16[2,20,32,128]{3,2,1,0:T(8,128)(2,1)S(1)} %pad_maximum_fusion), channel_id=1, source_target_pairs={{0,8},{8,16},{16,24},{24,32},{32,40},{40,48},{48,56},{56,64},{64,7... | collective-permute-start | bytes 983048 | tf_op jit(solution)/shard_map/ppermute | solution.py:591
  17.0 0.0 copy-done.2
  17.0 0.0 copy-done.7
  17.0 1.9 %shard_map.109 = (bf16[4,18,32,128]{3,2,1,0:T(8,128)(2,1)S(1)}, bf16[4,18,32,128]{3,2,1,0:T(8,128)(2,1)S(1)}) custom-call(bf16[4,16,32,128]{3,2,1,0:T(8,128)(2,1)S(1)} %bitcast.25, bf16[8,2,32,128]{3,2,1,0:T(8,128)(2,1)S(1)} %collective-permute-done.before_ref.before_hbm, bf16[8,2,32,128]{3,2,1,0:T(8,128)(2,1)S(1)} %collective-permute-done.1.after_ref.after_hbm, ...), custom_call_target="tpu_custom_call" | custom-call | flops 679477248 | bytes 2260992 | tf_op jit(solution)/shard_map/pallas_call | solution.py:558
  18.9 0.0 copy-done.4
  18.9 0.0 copy-done.5
  18.9 0.0 copy-start.3
  18.9 0.8 copy-done.3
  19.7 0.0 copy-start.15
  19.7 0.0 copy-start.16
  19.7 3.2 %collective-permute-done.2.prev_ref = bf16[2,20,32,128]{3,2,1,0:T(8,128)(2,1)S(1)} collective-permute-done((bf16[2,20,32,128]{3,2,1,0:T(8,128)(2,1)S(1)}, bf16[2,20,32,128]{3,2,1,0:T(8,128)(2,1)S(1)}, u32[]{:S(2)}, u32[]{:S(2)}) %collective-permute-start.2) | collective-permute-done | bytes 327712 | tf_op jit(solution)/shard_map/ppermute | solution.py:591
  22.9 0.0 copy-start.11
  22.9 0.0 copy-done.6
  22.9 0.0 copy-start.1
  22.9 0.0 copy-start.9
  22.9 0.0 copy-start.10
  22.9 2.4 %shard_map.110 = (f32[4,18,32,128]{3,2,1,0:T(8,128)S(1)}, f32[256,128]{1,0:T(8,128)}) custom-call(bf16[4,18,32,128]{3,2,1,0:T(8,128)(2,1)S(1)} %get-tuple-element.22.feature_ref, bf16[2,20,32,128]{3,2,1,0:T(8,128)(2,1)S(1)} %collective-permute-done.2.prev_ref, bf16[3,3,128,128]{3,2,1,0:T(8,128)(2,1)S(1)} %copy-done.7, bf16[3,128,128]{2,1,0:T(8,128)(2,1)S(1)} %copy-done.6), custom_call_target="tpu_custom_call" | custom-call | flops 679477248 | bytes 2621440 | tf_op jit(solution)/shard_map/pallas_call | solution.py:558
  25.3 0.0 copy-start
  25.3 21.4 %all-to-all-start = ((f32[128,2,128]{2,1,0:T(2,128)}), f32[128,2,128]{2,1,0:T(2,128)S(1)}, u32[]{:S(2)}, u32[]{:S(2)}) async-start(f32[128,2,128]{2,1,0:T(2,128)} %bitcast.3), calls=%async_computation | async-start | bytes 262144 | tf_op jit(solution)/shard_map/all_to_all | solution.py:627
  46.7 0.0 copy-done.13
  46.7 0.0 copy-done.15
  46.8 0.0 copy-done.16
  46.8 0.9 maximum_maximum_fusion
  47.7 0.0 copy-done.11
  47.7 1.3 collective-permute-start.3
  49.0 13.8 %all-to-all-done = f32[128,2,128]{2,1,0:T(2,128)S(1)} async-done(((f32[128,2,128]{2,1,0:T(2,128)}), f32[128,2,128]{2,1,0:T(2,128)S(1)}, u32[]{:S(2)}, u32[]{:S(2)}) %all-to-all-start) | async-done | bytes 131104 | tf_op jit(solution)/shard_map/all_to_all | solution.py:627
  62.7 0.0 copy-done.1
  62.7 0.0 copy-done.9
  62.7 0.0 copy-done.10
  62.7 2.2 %shard_map.111 = (f32[144,128]{1,0:T(8,128)S(1)}, f32[256,128]{1,0:T(8,128)}) custom-call(f32[256,128]{1,0:T(8,128)S(1)} %bitcast.26, f32[4,18,32,128]{3,2,1,0:T(8,128)S(1)} %get-tuple-element.24.mixed_ref.mixed_hbm, bf16[4,16,32,128]{3,2,1,0:T(8,128)(2,1)S(1)} %bitcast.21, f32[1,128]{1,0:T(1,128)S(1)} %bitcast.28, f32[1,128]{1,0:T(1,128)S(1)} %bitcast.30), custom_call_target="tpu_custom_call" | custom-call | bytes 2040832 | tf_op jit(solution)/shard_map/pallas_call | solution.py:558
  64.9 0.0 copy-done
  64.9 0.0 copy-start.8
  64.9 0.6 copy-done.8
  65.5 7.4 %all-to-all-start.1 = ((f32[128,2,128]{2,1,0:T(2,128)}), f32[128,2,128]{2,1,0:T(2,128)S(1)}, u32[]{:S(2)}, u32[]{:S(2)}) async-start(f32[128,2,128]{2,1,0:T(2,128)} %bitcast.10), calls=%async_computation.1 | async-start | bytes 262144 | tf_op jit(solution)/shard_map/all_to_all | solution.py:660
  72.9 4.2 %shard_map.114 = (bf16[384,2048]{1,0:T(8,128)(2,1)}, bf16[128,3072]{1,0:T(8,128)(2,1)}) custom-call(bf16[4,16,32,128]{3,2,1,0:T(8,128)(2,1)} %bitcast.23, bf16[8,2,32,128]{3,2,1,0:T(8,128)(2,1)} %copy-done.4, bf16[8,2,32,128]{3,2,1,0:T(8,128)(2,1)} %copy-done.5, bf16[2,20,32,128]{3,2,1,0:T(8,128)(2,1)} %copy-done.11, bf16[4,18,32,128]{3,2,1,0:T(8,128)(2,1)} %copy-done.3, ...), custom_call_target="tpu_custom_call" | custom-call | flops 679477248 | bytes 4358144 | tf_op jit(solution)/shard_map/pallas_call | solution.py:558
  77.1 0.0 collective-permute-done.3.next_hbm
  77.1 0.0 copy-start.12
  77.1 0.8 copy-done.12
  78.0 3.1 %shard_map.112.mixed_next_ref.mixed_next_hbm = f32[2,18,32,128]{3,2,1,0:T(8,128)} custom-call(bf16[4,20,32,128]{3,2,1,0:T(8,128)(2,1)} %copy-done.12, bf16[4,18,32,128]{3,2,1,0:T(8,128)(2,1)} %copy-done.3, bf16[3,3,128,128]{3,2,1,0:T(8,128)(2,1)} %spatial_ref.7, bf16[3,128,128]{2,1,0:T(8,128)(2,1)} %temporal_hbm.3), custom_call_target="tpu_custom_call" | custom-call | flops 339738624 | bytes 2228224 | tf_op jit(solution)/shard_map/pallas_call | solution.py:558
  81.1 5.3 %shard_map.113 = (bf16[4,16,32,128]{3,2,1,0:T(8,128)(2,1)}, f32[6,18,32,128]{3,2,1,0:T(8,128)}) custom-call(f32[144,128]{1,0:T(8,128)} %copy-done.8, f32[4,18,32,128]{3,2,1,0:T(8,128)} %copy-done, f32[2,18,32,128]{3,2,1,0:T(8,128)} %shard_map.112.mixed_next_ref.mixed_next_hbm, bf16[4,16,32,128]{3,2,1,0:T(8,128)(2,1)} %bitcast.24, ...), custom_call_target="tpu_custom_call" | custom-call | bytes 6104064 | tf_op jit(solution)/shard_map/pallas_call | solution.py:558
  86.5 2.4 %all-to-all-done.1 = f32[128,2,128]{2,1,0:T(2,128)S(1)} async-done(((f32[128,2,128]{2,1,0:T(2,128)}), f32[128,2,128]{2,1,0:T(2,128)S(1)}, u32[]{:S(2)}, u32[]{:S(2)}) %all-to-all-start.1) | async-done | bytes 131104 | tf_op jit(solution)/shard_map/all_to_all | solution.py:660
  88.9 0.0 copy-start.14
  88.9 0.7 copy-done.14
  89.6 6.1 %shard_map.115 = (bf16[32,56,128]{2,1,0:T(8,128)(2,1)}, bf16[4,18,32,128]{3,2,1,0:T(8,128)(2,1)}) custom-call(f32[256,128]{1,0:T(8,128)} %bitcast.31, f32[144,128]{1,0:T(8,128)} %copy-done.8, f32[4,18,32,128]{3,2,1,0:T(8,128)} %copy-done, f32[2,18,32,128]{3,2,1,0:T(8,128)} %shard_map.112.mixed_next_ref.mixed_next_hbm, ...), custom_call_target="tpu_custom_call" | custom-call | flops 1207959552 | bytes 7249920 | tf_op jit(solution)/shard_map/pallas_call | solution.py:558
  95.7 18.3 %all_to_all.37.got_ref = bf16[32,56,128]{2,1,0:T(8,128)(2,1)S(1)} all-to-all(bf16[32,56,128]{2,1,0:T(8,128)(2,1)} %get-tuple-element.33), channel_id=1, replica_groups=mesh['rep'=4,'tm'=16,'height'=8] {'rep','height'}, dimensions={0} | all-to-all | bytes 917504 | tf_op jit(solution)/shard_map/all_to_all | solution.py:700
  114.0 0.1 shard_map.117
  114.1 23.1 %all_to_all.38.got_ref = bf16[16,56,128]{2,1,0:T(8,128)(2,1)S(1)} all-to-all(bf16[16,56,128]{2,1,0:T(8,128)(2,1)S(1)} %shard_map.117), channel_id=1, replica_groups=mesh['rep'=4,'tm'=16,'height'=8] {'tm'}, dimensions={0} | all-to-all | bytes 458752 | tf_op jit(solution)/shard_map/all_to_all | solution.py:710
  137.2 0.8 shard_map.118
  138.1 7.2 %all-to-all-start.4 = ((bf16[32,56,128]{2,1,0:T(8,128)(2,1)}), bf16[32,56,128]{2,1,0:T(8,128)(2,1)S(1)}, u32[]{:S(2)}, u32[]{:S(2)}) async-start(bf16[32,56,128]{2,1,0:T(8,128)(2,1)} %shard_map.118), calls=%async_computation.4 | async-start | bytes 917504 | tf_op jit(solution)/shard_map/all_to_all | solution.py:712
  145.2 3.8 %shard_map.116 = bf16[4,16,32,128]{3,2,1,0:T(8,128)(2,1)} custom-call(bf16[4,18,32,128]{3,2,1,0:T(8,128)(2,1)} %get-tuple-element.32.grad_ref, bf16[4,16,32,128]{3,2,1,0:T(8,128)(2,1)} %bitcast.20, bf16[3,3,128,128]{3,2,1,0:T(8,128)(2,1)} %spatial_ref.7), custom_call_target="tpu_custom_call" | custom-call | flops 603979776 | bytes 1933312 | tf_op jit(solution)/shard_map/pallas_call | solution.py:558
  149.1 7.2 %all-to-all-done.4.got_ref = bf16[32,56,128]{2,1,0:T(8,128)(2,1)S(1)} async-done(((bf16[32,56,128]{2,1,0:T(8,128)(2,1)}), bf16[32,56,128]{2,1,0:T(8,128)(2,1)S(1)}, u32[]{:S(2)}, u32[]{:S(2)}) %all-to-all-start.4) | async-done | bytes 458784 | tf_op jit(solution)/shard_map/all_to_all | solution.py:712
  156.3 0.9 shard_map.119
  (5 shorter events, 0.1 us)
Async XLA Ops:
  1.6 15.4 %copy-start.2 = (bf16[1,4,16,32,128]{4,3,2,1,0:T(8,128)(2,1)S(1)}, bf16[1,4,16,32,128]{4,3,2,1,0:T(8,128)(2,1)}, u32[]{:S(2)}) copy-start(bf16[1,4,16,32,128]{4,3,2,1,0:T(8,128)(2,1)} %param.6) | copy-start | bytes 1572868
  1.6 15.4 %copy-start.7 = (bf16[3,3,128,128]{3,2,1,0:T(8,128)(2,1)S(1)}, bf16[3,3,128,128]{3,2,1,0:T(8,128)(2,1)}, u32[]{:S(2)}) copy-start(bf16[3,3,128,128]{3,2,1,0:T(8,128)(2,1)} %spatial_ref.7) | copy-start | bytes 884740
  1.6 12.1 %collective-permute-start = (bf16[8,2,32,128]{3,2,1,0:T(8,128)(2,1)S(1)}, bf16[8,2,32,128]{3,2,1,0:T(8,128)(2,1)S(1)}, u32[]{:S(2)}, u32[]{:S(2)}) collective-permute-start(bf16[8,2,32,128]{3,2,1,0:T(8,128)(2,1)S(1)} %pad_maximum_fusion.1), channel_id=1, source_target_pairs={{0,1},{1,2},{2,3},{3,4},{4,5},{5,6},{6,7},{8,9},{9,10},{10,11},{11... | collective-permute-start | bytes 393224 | tf_op jit(solution)/shard_map/ppermute | solution.py:586
  6.4 7.4 %collective-permute-start.1 = (bf16[8,2,32,128]{3,2,1,0:T(8,128)(2,1)S(1)}, bf16[8,2,32,128]{3,2,1,0:T(8,128)(2,1)S(1)}, u32[]{:S(2)}, u32[]{:S(2)}) collective-permute-start(bf16[8,2,32,128]{3,2,1,0:T(8,128)(2,1)S(1)} %pad_maximum_fusion.2), channel_id=1, source_target_pairs={{1,0},{2,1},{3,2},{4,3},{5,4},{6,5},{7,6},{9,8},{10,9},{11,10},{12... | collective-permute-start | bytes 393224 | tf_op jit(solution)/shard_map/ppermute | solution.py:587
  13.7 5.1 %copy-start.4 = (bf16[8,2,32,128]{3,2,1,0:T(8,128)(2,1)}, bf16[8,2,32,128]{3,2,1,0:T(8,128)(2,1)S(1)}, u32[]{:S(2)}) copy-start(bf16[8,2,32,128]{3,2,1,0:T(8,128)(2,1)S(1)} %collective-permute-done.before_ref.before_hbm) | copy-start | bytes 393220
  13.8 5.1 %copy-start.5 = (bf16[8,2,32,128]{3,2,1,0:T(8,128)(2,1)}, bf16[8,2,32,128]{3,2,1,0:T(8,128)(2,1)S(1)}, u32[]{:S(2)}) copy-start(bf16[8,2,32,128]{3,2,1,0:T(8,128)(2,1)S(1)} %collective-permute-done.1.after_ref.after_hbm) | copy-start | bytes 393220
  14.5 8.4 %copy-start.6 = (bf16[3,128,128]{2,1,0:T(8,128)(2,1)S(1)}, bf16[3,128,128]{2,1,0:T(8,128)(2,1)}, u32[]{:S(2)}) copy-start(bf16[3,128,128]{2,1,0:T(8,128)(2,1)} %temporal_hbm.3) | copy-start | bytes 294916
  14.5 8.4 %collective-permute-start.2 = (bf16[2,20,32,128]{3,2,1,0:T(8,128)(2,1)S(1)}, bf16[2,20,32,128]{3,2,1,0:T(8,128)(2,1)S(1)}, u32[]{:S(2)}, u32[]{:S(2)}) collective-permute-start(bf16[2,20,32,128]{3,2,1,0:T(8,128)(2,1)S(1)} %pad_maximum_fusion), channel_id=1, source_target_pairs={{0,8},{8,16},{16,24},{24,32},{32,40},{40,48},{48,56},{56,64},{64,7... | collective-permute-start | bytes 983048 | tf_op jit(solution)/shard_map/ppermute | solution.py:591
  18.9 0.8 copy-start.3
  19.7 27.0 %copy-start.13 = (bf16[2,16,32,128]{3,2,1,0:T(8,128)(2,1)S(1)}, bf16[2,16,32,128]{3,2,1,0:T(8,128)(2,1)}, u32[]{:S(2)}) copy-start(bf16[2,16,32,128]{3,2,1,0:T(8,128)(2,1)} %get-tuple-element.52) | copy-start | bytes 786436
  19.7 27.0 %copy-start.15 = (bf16[2,2,32,128]{3,2,1,0:T(8,128)(2,1)S(1)}, bf16[2,2,32,128]{3,2,1,0:T(8,128)(2,1)}, u32[]{:S(2)}) copy-start(bf16[2,2,32,128]{3,2,1,0:T(8,128)(2,1)} %get-tuple-element.47) | copy-start | bytes 98308
  19.7 27.0 %copy-start.16 = (bf16[2,2,32,128]{3,2,1,0:T(8,128)(2,1)S(1)}, bf16[2,2,32,128]{3,2,1,0:T(8,128)(2,1)}, u32[]{:S(2)}) copy-start(bf16[2,2,32,128]{3,2,1,0:T(8,128)(2,1)} %get-tuple-element.48) | copy-start | bytes 98308
  22.9 24.8 %copy-start.11 = (bf16[2,20,32,128]{3,2,1,0:T(8,128)(2,1)}, bf16[2,20,32,128]{3,2,1,0:T(8,128)(2,1)S(1)}, u32[]{:S(2)}) copy-start(bf16[2,20,32,128]{3,2,1,0:T(8,128)(2,1)S(1)} %collective-permute-done.2.prev_ref) | copy-start | bytes 983044
  22.9 39.8 %copy-start.1 = (bf16[1,4,16,32,128]{4,3,2,1,0:T(8,128)(2,1)S(1)}, bf16[1,4,16,32,128]{4,3,2,1,0:T(8,128)(2,1)}, u32[]{:S(2)}) copy-start(bf16[1,4,16,32,128]{4,3,2,1,0:T(8,128)(2,1)} %param.11) | copy-start | bytes 1572868
  22.9 39.8 %copy-start.9 = (f32[128]{0:T(128)S(1)}, f32[128]{0:T(128)}, u32[]{:S(2)}) copy-start(f32[128]{0:T(128)} %param.9) | copy-start | bytes 1540
  22.9 39.8 %copy-start.10 = (f32[128]{0:T(128)S(1)}, f32[128]{0:T(128)}, u32[]{:S(2)}) copy-start(f32[128]{0:T(128)} %param.10) | copy-start | bytes 1540
  25.3 39.6 %copy-start = (f32[4,18,32,128]{3,2,1,0:T(8,128)}, f32[4,18,32,128]{3,2,1,0:T(8,128)S(1)}, u32[]{:S(2)}) copy-start(f32[4,18,32,128]{3,2,1,0:T(8,128)S(1)} %get-tuple-element.24.mixed_ref.mixed_hbm) | copy-start | bytes 3538948
  25.3 37.4 %all-to-all-start = ((f32[128,2,128]{2,1,0:T(2,128)}), f32[128,2,128]{2,1,0:T(2,128)S(1)}, u32[]{:S(2)}, u32[]{:S(2)}) async-start(f32[128,2,128]{2,1,0:T(2,128)} %bitcast.3), calls=%async_computation | async-start | bytes 262144 | tf_op jit(solution)/shard_map/all_to_all | solution.py:627
  47.7 29.5 %collective-permute-start.3 = (bf16[4,20,32,128]{3,2,1,0:T(8,128)(2,1)}, bf16[4,20,32,128]{3,2,1,0:T(8,128)(2,1)S(1)}, u32[]{:S(2)}, u32[]{:S(2)}) collective-permute-start(bf16[4,20,32,128]{3,2,1,0:T(8,128)(2,1)} %maximum_maximum_fusion), channel_id=1, source_target_pairs={{8,0},{16,8},{24,16},{32,24},{40,32},{48,40},{56,48},{64,56},{72,6... | collective-permute-start | bytes 1966088 | tf_op jit(solution)/shard_map/ppermute | solution.py:600
  64.9 0.6 copy-start.8
  65.5 23.4 %all-to-all-start.1 = ((f32[128,2,128]{2,1,0:T(2,128)}), f32[128,2,128]{2,1,0:T(2,128)S(1)}, u32[]{:S(2)}, u32[]{:S(2)}) async-start(f32[128,2,128]{2,1,0:T(2,128)} %bitcast.10), calls=%async_computation.1 | async-start | bytes 262144 | tf_op jit(solution)/shard_map/all_to_all | solution.py:660
  77.1 0.9 copy-start.12
  88.9 0.7 copy-start.14
  138.1 18.2 %all-to-all-start.4 = ((bf16[32,56,128]{2,1,0:T(8,128)(2,1)}), bf16[32,56,128]{2,1,0:T(8,128)(2,1)S(1)}, u32[]{:S(2)}, u32[]{:S(2)}) async-start(bf16[32,56,128]{2,1,0:T(8,128)(2,1)} %shard_map.118), calls=%async_computation.4 | async-start | bytes 917504 | tf_op jit(solution)/shard_map/all_to_all | solution.py:712

commit v5 on v4

--- a/solution.py
+++ b/solution.py
@@ -114,6 +114,10 @@
     return value.astype(jnp.float32).T.astype(jnp.bfloat16)
 
 
+def joined(before_ref, main_ref, after_ref, f):
+    return jnp.concatenate([flat(before_ref[f]), flat(main_ref[f]), flat(after_ref[f])], 0)
+
+
 def own_features(
     x_ref, before_ref, after_ref, spatial_ref, feature_ref, far_ref, weight_ref, sems
 ):
@@ -136,6 +140,8 @@
     before_ref,
     after_ref,
     prev_ref,
+    prev_before_ref,
+    prev_after_ref,
     feature_ref,
     spatial_ref,
     xt_ref,
@@ -148,7 +154,8 @@
     size = rows * columns
 
     def one(f, _):
-        out = convolve(flat(prev_ref[f]), weight_ref[...], rows + 2, columns, False)
+        block = joined(prev_before_ref, prev_ref, prev_after_ref, f)
+        out = convolve(block, weight_ref[...], rows + 2, columns, False)
         prior_ref[f] = out.astype(jnp.bfloat16).reshape(prior_ref.shape[1:])
         return 0
 
@@ -170,6 +177,8 @@
 def mixed_and_sums(
     feature_ref,
     prev_ref,
+    prev_before_ref,
+    prev_after_ref,
     spatial_ref,
     temporal_ref,
     mixed_ref,
@@ -181,7 +190,8 @@
     frames, rows, columns, _ = mixed_ref.shape
 
     def one(f, _):
-        out = convolve(flat(prev_ref[f]), weight_ref[...], rows, columns, False)
+        block = joined(prev_before_ref, prev_ref, prev_after_ref, f)
+        out = convolve(block, weight_ref[...], rows, columns, False)
         prior_ref[f] = out.astype(jnp.bfloat16).reshape(prior_ref.shape[1:])
         return 0
 
@@ -301,82 +311,97 @@
     stats_ref[at : at + 16] = jnp.where(iota((16, TILE), 0) < 8, total_b, total_a)
 
 
-def outputs_and_grads(
+def normalised(mixed, mean, inv_std, gain, shift):
+    pre = (mixed - mean) * inv_std * gain + shift
+    return pre, 1.0 / (1.0 + jnp.exp(-pre))
+
+
+def write_outputs(time_devices, stats_ref, mixed_ref, x_ref, gain_ref, shift_ref, outputs_ref):
+    frames, rows, columns, _ = x_ref.shape
+    me = lax.axis_index("tm")
+    gain, shift = gain_ref[...], shift_ref[...]
+    step = 4
+    for f in range(frames):
+        mean = stats_ref[pl.ds(2 * f * time_devices + me, 1)]
+        inv_std = stats_ref[pl.ds((2 * f + 1) * time_devices + me, 1)]
+
+        def some(i, _, f=f, mean=mean, inv_std=inv_std):
+            at = pl.ds(i * step, step)
+            mixed = flat(mixed_ref[f, pl.ds(1 + i * step, step)])
+            pre, sigma = normalised(mixed, mean, inv_std, gain, shift)
+            kept = flat(x_ref[f, at]).astype(jnp.float32) + pre * sigma
+            outputs_ref[f, at] = kept.astype(jnp.bfloat16).reshape(step, columns, TILE)
+            return 0
+
+        lax.fori_loop(0, rows // step, some, 0, unroll=2)
+
+
+def mixed_grads(
     time_devices,
     stats_ref,
-    mixed_ref,
-    mixed_next_ref,
-    x_ref,
-    cot_ref,
     gain_ref,
     shift_ref,
+    mixed_hbm,
+    mixed_next_hbm,
+    cot_hbm,
     before_hbm,
     after_hbm,
     next_hbm,
-    outputs_ref,
     scaled_hbm,
     scaled_ref,
+    mixed_ref,
+    cot_ref,
     before_ref,
     after_ref,
-    next_ref,
     in_sems,
     out_sems,
 ):
-    frames, rows, columns, _ = cot_ref.shape
-    copies = fetch(
-        [
-            (before_hbm.at[pl.ds(frames, frames)], before_ref),
-            (after_hbm.at[pl.ds(frames, frames)], after_ref),
-            (next_hbm.at[pl.ds(2, 2)], next_ref),
-        ],
-        in_sems,
-    )
+    frames, rows, columns, _ = cot_hbm.shape
+    pairs = [
+        (before_hbm.at[pl.ds(frames, frames)], before_ref),
+        (after_hbm.at[pl.ds(frames, frames)], after_ref),
+    ]
+    for f in range(frames + 2):
+        own = f < frames
+        pairs.append((mixed_hbm.at[f] if own else mixed_next_hbm.at[f - frames], mixed_ref.at[f]))
+        if own:
+            pairs.append((cot_hbm.at[f], cot_ref.at[f, pl.ds(2, rows)]))
+        else:
+            pairs.append((next_hbm.at[2 + f - frames], cot_ref.at[f]))
+    copies = fetch(pairs, in_sems)
     me = lax.axis_index("tm")
     following = jnp.minimum(me + 1, time_devices - 1)
     gain, shift = gain_ref[...], shift_ref[...]
     step = 4
 
     def grads(mixed, cot, mean, inv_std):
-        pre = (mixed - mean) * inv_std * gain + shift
-        sigma = 1.0 / (1.0 + jnp.exp(-pre))
+        pre, sigma = normalised(mixed, mean, inv_std, gain, shift)
         grad = cot.astype(jnp.float32) * (sigma * (1.0 + pre * (1.0 - sigma)))
-        return pre * sigma, inv_std * (grad * gain)
+        return inv_std * (grad * gain)
 
     leaving = []
-
+    copies[0].wait()
+    copies[1].wait()
     for f in range(frames + 2):
         own = f < frames
         at, g = (me, f) if own else (following, f - frames)
         mean = stats_ref[pl.ds(2 * g * time_devices + at, 1)]
         inv_std = stats_ref[pl.ds((2 * g + 1) * time_devices + at, 1)]
-        source = mixed_ref if own else mixed_next_ref
-
-        def edge(row, cot, f=f, g=g, mean=mean, inv_std=inv_std, source=source):
-            _, scaled = grads(source[g, row], cot, mean, inv_std)
-            scaled_ref[f, row] = scaled
-
-
-        if f == frames:
-            copies[2].wait()
-
-        def some(i, _, f=f, g=g, own=own, mean=mean, inv_std=inv_std, source=source):
+        copies[2 + 2 * f].wait()
+        copies[3 + 2 * f].wait()
+
+        def some(i, _, f=f, mean=mean, inv_std=inv_std):
             here = pl.ds(1 + i * step, step)
-            cot = cot_ref[g, pl.ds(i * step, step)] if own else next_ref[g, pl.ds(2 + i * step, step)]
-            silu, scaled = grads(flat(source[g, here]), flat(cot), mean, inv_std)
+            cot = flat(cot_ref[f, pl.ds(2 + i * step, step)])
+            scaled = grads(flat(mixed_ref[f, here]), cot, mean, inv_std)
             scaled_ref[f, here] = scaled.reshape(step, columns, TILE)
-            if own:
-                kept = flat(x_ref[g, pl.ds(i * step, step)]).astype(jnp.float32) + silu
-                outputs_ref[g, pl.ds(i * step, step)] = kept.astype(jnp.bfloat16).reshape(
-                    step, columns, TILE
-                )
             return 0
 
         lax.fori_loop(0, rows // step, some, 0, unroll=2)
-        if f == 0:
-            copies[0].wait()
-            copies[1].wait()
-        edge(0, before_ref[g, 1] if own else next_ref[g, 1])
-        edge(rows + 1, after_ref[g, 0] if own else next_ref[g, rows + 2])
+        top = before_ref[f, 1] if own else cot_ref[f, 1]
+        bottom = after_ref[f, 0] if own else cot_ref[f, rows + 2]
+        for row, cot in ((0, top), (rows + 1, bottom)):
+            scaled_ref[f, row] = grads(mixed_ref[f, row], cot, mean, inv_std)
         copy = pltpu.make_async_copy(scaled_ref.at[f], scaled_hbm.at[f], out_sems.at[f])
         copy.start()
         leaving.append(copy)
@@ -581,14 +606,19 @@
     weight = pltpu.VMEM((3 * channels, 3 * channels), bf16)
     conv = 2 * 9 * channels * channels * columns
 
+    onward = [(i, i + 1) for i in range(time_devices - 1)]
+    back = [(j, i) for i, j in onward]
+    late_frames = x[frames - 2 :]
+    prev = lax.ppermute(late_frames, "tm", onward)
     up = [(i, i + 1) for i in range(height_devices - 1)]
     down = [(j, i) for i, j in up]
     before = lax.ppermute(jnp.concatenate([x[:, rows - 2 :], cot[:, rows - 2 :]], 0), "height", up)
     after = lax.ppermute(jnp.concatenate([x[:, :2], cot[:, :2]], 0), "height", down)
-    onward = [(i, i + 1) for i in range(time_devices - 1)]
-    back = [(j, i) for i, j in onward]
-    last = jnp.concatenate([before[2:4], x[2:4], after[2:4]], 1)
-    prev = lax.ppermute(last, "tm", onward)
+    cross = ("tm", "height")
+    slant = [(t * height_devices + i, (t + 1) * height_devices + j) for t, _ in onward for i, j in up]
+    prev_before = lax.ppermute(late_frames[:, rows - 2 :], cross, slant)
+    slant = [(t * height_devices + i, (t + 1) * height_devices + j) for t, _ in onward for i, j in down]
+    prev_after = lax.ppermute(late_frames[:, :2], cross, slant)
     first = jnp.concatenate(
         [
             jnp.concatenate([before[:2], before[4:6]], 0),
@@ -618,7 +648,7 @@
     mixed, payload = call(
         mixed_and_sums,
         [out((frames, ext) + frame, f32), out((2 * peers, channels), f32)],
-        (feature, prev, spatial_kernel, temporal_kernel),
+        (feature, prev, prev_before, prev_after, spatial_kernel, temporal_kernel),
         [weight, held(two)],
         conv * frames * ext,
         limit=NARROW,
@@ -628,7 +658,7 @@
     xt, ft = call(
         turn,
         [turned_x, turned_features],
-        (x, before, after, prev, late, spatial_kernel),
+        (x, before, after, prev, prev_before, prev_after, late, spatial_kernel),
         [weight, held(two)],
         conv * frames * ext,
     )
@@ -659,20 +689,26 @@
     )
     got = lax.all_to_all(payload, share, 0, 0, tiled=True)
     scaled_shape = out((frames + 2, ext) + frame, f32)
-    outputs, scaled = call(
-        functools.partial(outputs_and_grads, time_devices),
-        [out((frames, rows) + frame, bf16)],
-        (stats, mixed, mixed_next, x, cot, gain, shift),
+    (scaled,) = call(
+        functools.partial(mixed_grads, time_devices),
+        [],
+        (stats, gain, shift),
         [
             held(scaled_shape),
+            held(scaled_shape),
+            pltpu.VMEM((frames + 2, rows + 4) + frame, bf16),
             pltpu.VMEM((frames, 2) + frame, bf16),
             pltpu.VMEM((frames, 2) + frame, bf16),
-            pltpu.VMEM((2, rows + 4) + frame, bf16),
-            dma(3),
+            dma(2 * frames + 6),
             dma(frames + 2),
         ],
-        far=(before, after, following),
+        far=(mixed, mixed_next, cot, before, after, following),
         far_outs=[scaled_shape],
+    )
+    (outputs,) = call(
+        functools.partial(write_outputs, time_devices),
+        [out((frames, rows) + frame, bf16)],
+        (stats, mixed, x, gain, shift),
     )
     ends = ("rep", "height")
     pieces = reps * height_devices

time: 158 us -> 157 us (level)
  waiting for transfers between devices: 26.6 us -> 21.9 us
  starting transfers between devices: 49.8 us -> 52.9 us
    ppermute x1 -> x3, starting transfers between devices: 2.44 us -> 7.49 us  [the longest x1 3.97 us: shards(): prev_before = lax.ppermute(late_frames[:, rows - 2:], cross, slant)]
    ppermute x1 -> x3, waiting for transfers between devices: 3.18 us -> 0.01 us  [the longest x1 0.01 us: shards(): prev_before = lax.ppermute(late_frames[:, rows - 2:], cross, slant)]
    all_to_all x1, waiting for transfers between devices: 7.22 us -> 4.45 us  [shards(): sums = lax.all_to_all(partial, ends, 0, 0, tiled=True)]
    all_to_all x2, starting transfers between devices: 28.8 us -> 26.9 us  [shards(): got = lax.all_to_all(payload, share, 0, 0, tiled=True)]
    pallas_call x11 -> x12, Pallas kernels: 30.9 us -> 32.4 us  [call(): pl.pallas_call(body, out_shape=[*outs, *far_outs], in_specs=[near] * len(...]
  transfers between devices with their start and end apart: 7 -> 9, of which waited for: 4 -> 3; matrix products, arithmetic and copies ran while one was open for 2% -> 2% of each run, Pallas kernels for 13% -> 14%
where the time goes in v5:
time: 157 us; the launch traced here: 156 us
  starting transfers between devices  52.9 us (34%)
  blocking collectives  40.2 us (26%)
  Pallas kernels  32.4 us (21%)
  waiting for transfers between devices  21.9 us (14%)
  local copies, waits for them, and re-layouts  6.76 us (4%)
    pallas_call x12, Pallas kernels, call(): pl.pallas_call(body, out_shape=[*outs, *far_outs], in_specs=[near] * len(...  32.4 us
    all_to_all x2, starting transfers between devices, shards(): got = lax.all_to_all(payload, share, 0, 0, tiled=True)  26.9 us
    all_to_all x1, blocking collectives, shards(): partial = lax.all_to_all(partial, 'tm', 0, 0, tiled=True)  21.8 us
    all_to_all x1, blocking collectives, shards(): partial = lax.all_to_all(partial, ends, 0, 0, tiled=True)  18.3 us
    all_to_all x2, waiting for transfers between devices, shards(): got = lax.all_to_all(payload, share, 0, 0, tiled=True)  17.4 us
    all_to_all x1, starting transfers between devices, shards(): sums = lax.all_to_all(partial, ends, 0, 0, tiled=True)  7.18 us
    ppermute x1, starting transfers between devices, shards(): lax.ppermute(jnp.concatenate([x[:, :2], cot[:, :2]], 0), 'height', down)  5.46 us
    ppermute x1, starting transfers between devices, shards(): lax.ppermute(jnp.concatenate([x[:, rows - 2:], cot[:, rows - 2:]], 0), 'h...  4.58 us
  transfers between devices with their start and end apart: 9, of which 3 were waited for; matrix products, arithmetic and copies ran while one was open for 2% of the time, Pallas kernels for 14%

profile of v5, /device:TPU:1, one launch (start us, length us, event | category | flops | bytes accessed | tf_op | source)
XLA Modules:
  0.0 156.0 jit_solution(1777978241435100439)
XLA Ops:
  0.6 0.0 copy-start.2
  0.6 0.0 copy-start.6
  0.7 1.0 fusion
  1.6 0.9 fusion.1
  2.5 4.6 %collective-permute-start = (bf16[8,2,32,128]{3,2,1,0:T(8,128)(2,1)S(1)}, bf16[8,2,32,128]{3,2,1,0:T(8,128)(2,1)S(1)}, u32[]{:S(2)}, u32[]{:S(2)}) collective-permute-start(bf16[8,2,32,128]{3,2,1,0:T(8,128)(2,1)S(1)} %pad_maximum_fusion), channel_id=1, source_target_pairs={{0,1},{1,2},{2,3},{3,4},{4,5},{5,6},{6,7},{8,9},{9,10},{10,11},{11... | collective-permute-start | bytes 393224 | tf_op jit(solution)/shard_map/ppermute | solution.py:615
  7.1 5.5 %collective-permute-start.1 = (bf16[8,2,32,128]{3,2,1,0:T(8,128)(2,1)S(1)}, bf16[8,2,32,128]{3,2,1,0:T(8,128)(2,1)S(1)}, u32[]{:S(2)}, u32[]{:S(2)}) collective-permute-start(bf16[8,2,32,128]{3,2,1,0:T(8,128)(2,1)S(1)} %pad_maximum_fusion.1), channel_id=1, source_target_pairs={{1,0},{2,1},{3,2},{4,3},{5,4},{6,5},{7,6},{9,8},{10,9},{11,10},{12... | collective-permute-start | bytes 393224 | tf_op jit(solution)/shard_map/ppermute | solution.py:616
  12.6 1.9 %slice_bitcast_fusion.1 = (bf16[2,16,32,128]{3,2,1,0:T(8,128)(2,1)S(1)}, bf16[2,16,32,128]{3,2,1,0:T(8,128)(2,1)S(1)}, bf16[2,16,32,128]{3,2,1,0:T(8,128)(2,1)}) fusion(bf16[1,4,16,32,128]{4,3,2,1,0:T(8,128)(2,1)} %param.6, bf16[1,4,16,32,128]{4,3,2,1,0:T(8,128)(2,1)} %param.11), kind=kLoop, calls=%fused_computation.2 | loop fusion | bytes 1572864 | tf_op jit(solution)/shard_map/slice | solution.py:625
  14.5 0.0 copy-start.5
  14.5 1.4 collective-permute-start.2
  16.0 4.0 %collective-permute-start.3 = (bf16[2,2,32,128]{3,2,1,0:T(8,128)(2,1)S(1)}, bf16[2,2,32,128]{3,2,1,0:T(8,128)(2,1)S(1)}, u32[]{:S(2)}, u32[]{:S(2)}) collective-permute-start(bf16[2,2,32,128]{3,2,1,0:T(8,128)(2,1)S(1)} %get-tuple-element.41), channel_id=1, source_target_pairs={{0,9},{1,10},{2,11},{3,12},{4,13},{5,14},{6,15},{8,17},{9,18},{10,... | collective-permute-start | bytes 98312 | tf_op jit(solution)/shard_map/ppermute | solution.py:619
  19.9 2.1 %collective-permute-start.4 = (bf16[2,2,32,128]{3,2,1,0:T(8,128)(2,1)S(1)}, bf16[2,2,32,128]{3,2,1,0:T(8,128)(2,1)S(1)}, u32[]{:S(2)}, u32[]{:S(2)}) collective-permute-start(bf16[2,2,32,128]{3,2,1,0:T(8,128)(2,1)S(1)} %get-tuple-element.40), channel_id=1, source_target_pairs={{1,8},{2,9},{3,10},{4,11},{5,12},{6,13},{7,14},{9,16},{10,17},{11,... | collective-permute-start | bytes 98312 | tf_op jit(solution)/shard_map/ppermute | solution.py:621
  22.0 0.0 collective-permute-done.before_ref.before_hbm
  22.0 0.0 copy-start.7
  22.1 0.0 collective-permute-done.1.after_ref.after_hbm
  22.1 0.0 copy-done.2
  22.1 0.0 copy-done.6
  22.1 0.0 copy-start.8
  22.1 1.9 %shard_map.109 = (bf16[4,18,32,128]{3,2,1,0:T(8,128)(2,1)S(1)}, bf16[4,18,32,128]{3,2,1,0:T(8,128)(2,1)S(1)}) custom-call(bf16[4,16,32,128]{3,2,1,0:T(8,128)(2,1)S(1)} %bitcast.25, bf16[8,2,32,128]{3,2,1,0:T(8,128)(2,1)S(1)} %collective-permute-done.before_ref.before_hbm, bf16[8,2,32,128]{3,2,1,0:T(8,128)(2,1)S(1)} %collective-permute-done.1.after_ref.after_hbm, ...), custom_call_target="tpu_custom_call" | custom-call | flops 679477248 | bytes 2260992 | tf_op jit(solution)/shard_map/pallas_call | solution.py:583
  24.0 0.0 copy-start.4
  24.0 0.8 copy-done.4
  24.8 0.0 collective-permute-done.3.prev_before_ref
  24.8 0.0 collective-permute-done.4.prev_after_ref
  24.8 0.0 copy-start.13
  24.8 0.0 collective-permute-done.2.prev_ref
  24.8 0.0 copy-start.11
  24.9 0.0 copy-done.5
  24.9 0.0 copy-start.1
  24.9 0.0 copy-start.9
  24.9 0.0 copy-start.10
  24.9 2.4 %shard_map.110 = (f32[4,18,32,128]{3,2,1,0:T(8,128)S(1)}, f32[256,128]{1,0:T(8,128)}) custom-call(bf16[4,18,32,128]{3,2,1,0:T(8,128)(2,1)S(1)} %get-tuple-element.20.feature_ref, bf16[2,16,32,128]{3,2,1,0:T(8,128)(2,1)S(1)} %collective-permute-done.2.prev_ref, bf16[2,2,32,128]{3,2,1,0:T(8,128)(2,1)S(1)} %collective-permute-done.3.prev_before_ref, ...), custom_call_target="tpu_custom_call" | custom-call | flops 679477248 | bytes 2621440 | tf_op jit(solution)/shard_map/pallas_call | solution.py:583
  27.3 0.0 copy-done.7
  27.3 19.5 %all-to-all-start = ((f32[128,2,128]{2,1,0:T(2,128)}), f32[128,2,128]{2,1,0:T(2,128)S(1)}, u32[]{:S(2)}, u32[]{:S(2)}) async-start(f32[128,2,128]{2,1,0:T(2,128)} %bitcast.3), calls=%async_computation | async-start | bytes 262144 | tf_op jit(solution)/shard_map/all_to_all | solution.py:657
  46.8 0.0 copy-done.8
  46.9 0.0 copy-done.15
  46.9 0.9 maximum_maximum_fusion
  47.8 0.0 copy-done.12
  47.8 0.0 copy-done.13
  47.8 0.0 copy-done.11
  47.8 1.3 collective-permute-start.5
  49.1 13.7 %all-to-all-done = f32[128,2,128]{2,1,0:T(2,128)S(1)} async-done(((f32[128,2,128]{2,1,0:T(2,128)}), f32[128,2,128]{2,1,0:T(2,128)S(1)}, u32[]{:S(2)}, u32[]{:S(2)}) %all-to-all-start) | async-done | bytes 131104 | tf_op jit(solution)/shard_map/all_to_all | solution.py:657
  62.8 0.0 copy-done.1
  62.8 0.0 copy-done.9
  62.8 0.0 copy-done.10
  62.9 2.2 %shard_map.111 = (f32[144,128]{1,0:T(8,128)S(1)}, f32[256,128]{1,0:T(8,128)}) custom-call(f32[256,128]{1,0:T(8,128)S(1)} %bitcast.26, f32[4,18,32,128]{3,2,1,0:T(8,128)S(1)} %get-tuple-element.22.mixed_ref.mixed_hbm, bf16[4,16,32,128]{3,2,1,0:T(8,128)(2,1)S(1)} %bitcast.21, f32[1,128]{1,0:T(1,128)S(1)} %bitcast.29, f32[1,128]{1,0:T(1,128)S(1)} %bitcast.32), custom_call_target="tpu_custom_call" | custom-call | bytes 2040832 | tf_op jit(solution)/shard_map/pallas_call | solution.py:583
  65.0 0.0 copy-done
  65.0 0.6 copy-done.3
  65.6 7.4 %all-to-all-start.1 = ((f32[128,2,128]{2,1,0:T(2,128)}), f32[128,2,128]{2,1,0:T(2,128)S(1)}, u32[]{:S(2)}, u32[]{:S(2)}) async-start(f32[128,2,128]{2,1,0:T(2,128)} %bitcast.8), calls=%async_computation.1 | async-start | bytes 262144 | tf_op jit(solution)/shard_map/all_to_all | solution.py:690
  73.0 4.2 %shard_map.115 = (bf16[384,2048]{1,0:T(8,128)(2,1)}, bf16[128,3072]{1,0:T(8,128)(2,1)}) custom-call(bf16[4,16,32,128]{3,2,1,0:T(8,128)(2,1)} %bitcast.23, bf16[8,2,32,128]{3,2,1,0:T(8,128)(2,1)} %copy-done.7, bf16[8,2,32,128]{3,2,1,0:T(8,128)(2,1)} %copy-done.8, bf16[2,16,32,128]{3,2,1,0:T(8,128)(2,1)} %copy-done.11, bf16[2,2,32,128]{3,2,1,0:T(8,128)(2,1)} %copy-done.12, ...), custom_call_target="tpu_custom_call" | custom-call | flops 679477248 | bytes 4358144 | tf_op jit(solution)/shard_map/pallas_call | solution.py:583
  77.2 0.0 collective-permute-done.5.next_hbm
  77.3 0.8 copy-done.14
  78.1 3.2 %shard_map.113.mixed_next_hbm = f32[2,18,32,128]{3,2,1,0:T(8,128)} custom-call(bf16[4,20,32,128]{3,2,1,0:T(8,128)(2,1)} %copy-done.14, bf16[4,18,32,128]{3,2,1,0:T(8,128)(2,1)} %copy-done.4, bf16[3,3,128,128]{3,2,1,0:T(8,128)(2,1)} %spatial_ref.7, bf16[3,128,128]{2,1,0:T(8,128)(2,1)} %temporal_hbm.3), custom_call_target="tpu_custom_call" | custom-call | flops 339738624 | bytes 2228224 | tf_op jit(solution)/shard_map/pallas_call | solution.py:583
  81.3 4.0 %shard_map.114.scaled_hbm = f32[6,18,32,128]{3,2,1,0:T(8,128)} custom-call(f32[144,128]{1,0:T(8,128)} %copy-done.3, f32[1,128]{1,0:T(1,128)} %bitcast.27, f32[1,128]{1,0:T(1,128)} %bitcast.30, f32[4,18,32,128]{3,2,1,0:T(8,128)} %copy-done, f32[2,18,32,128]{3,2,1,0:T(8,128)} %shard_map.113.mixed_next_hbm, bf16[4,16,32,128]{3,2,1,0:T(8,128)(2,1)} %bitcast.19, ...), custom_call_target="tpu_custom_call" | custom-call | bytes 5055488 | tf_op jit(solution)/shard_map/pallas_call | solution.py:583
  85.3 3.7 %all-to-all-done.1 = f32[128,2,128]{2,1,0:T(2,128)S(1)} async-done(((f32[128,2,128]{2,1,0:T(2,128)}), f32[128,2,128]{2,1,0:T(2,128)S(1)}, u32[]{:S(2)}, u32[]{:S(2)}) %all-to-all-start.1) | async-done | bytes 131104 | tf_op jit(solution)/shard_map/all_to_all | solution.py:690
  89.0 0.7 copy-done.16
  89.7 6.1 %shard_map.116 = (bf16[32,56,128]{2,1,0:T(8,128)(2,1)}, bf16[4,18,32,128]{3,2,1,0:T(8,128)(2,1)}) custom-call(f32[256,128]{1,0:T(8,128)} %bitcast.33, f32[144,128]{1,0:T(8,128)} %copy-done.3, f32[4,18,32,128]{3,2,1,0:T(8,128)} %copy-done, f32[2,18,32,128]{3,2,1,0:T(8,128)} %shard_map.113.mixed_next_hbm, f32[6,18,32,128]{3,2,1,0:T(8,128)} %shard_map.114.scaled_hbm, ...), custom_call_target="tpu_custom_call" | custom-call | flops 1207959552 | bytes 7249920 | tf_op jit(solution)/shard_map/pallas_call | solution.py:583
  95.8 18.3 %all_to_all.37.got_ref = bf16[32,56,128]{2,1,0:T(8,128)(2,1)S(1)} all-to-all(bf16[32,56,128]{2,1,0:T(8,128)(2,1)} %get-tuple-element.29), channel_id=1, replica_groups=mesh['rep'=4,'tm'=16,'height'=8] {'rep','height'}, dimensions={0} | all-to-all | bytes 917504 | tf_op jit(solution)/shard_map/all_to_all | solution.py:736
  114.2 0.1 shard_map.118
  114.2 21.8 %all_to_all.38.got_ref = bf16[16,56,128]{2,1,0:T(8,128)(2,1)S(1)} all-to-all(bf16[16,56,128]{2,1,0:T(8,128)(2,1)S(1)} %shard_map.118), channel_id=1, replica_groups=mesh['rep'=4,'tm'=16,'height'=8] {'tm'}, dimensions={0} | all-to-all | bytes 458752 | tf_op jit(solution)/shard_map/all_to_all | solution.py:746
  136.1 0.8 shard_map.119
  136.9 7.2 %all-to-all-start.4 = ((bf16[32,56,128]{2,1,0:T(8,128)(2,1)}), bf16[32,56,128]{2,1,0:T(8,128)(2,1)S(1)}, u32[]{:S(2)}, u32[]{:S(2)}) async-start(bf16[32,56,128]{2,1,0:T(8,128)(2,1)} %shard_map.119), calls=%async_computation.4 | async-start | bytes 917504 | tf_op jit(solution)/shard_map/all_to_all | solution.py:748
  144.1 2.8 %shard_map.112 = bf16[4,16,32,128]{3,2,1,0:T(8,128)(2,1)} custom-call(f32[144,128]{1,0:T(8,128)} %copy-done.3, f32[4,18,32,128]{3,2,1,0:T(8,128)} %copy-done, bf16[4,16,32,128]{3,2,1,0:T(8,128)(2,1)} %bitcast.24, f32[1,128]{1,0:T(1,128)} %bitcast.28, f32[1,128]{1,0:T(1,128)} %bitcast.31), custom_call_target="tpu_custom_call" | custom-call | bytes 2302976 | tf_op jit(solution)/shard_map/pallas_call | solution.py:583
  146.9 3.8 %shard_map.117 = bf16[4,16,32,128]{3,2,1,0:T(8,128)(2,1)} custom-call(bf16[4,18,32,128]{3,2,1,0:T(8,128)(2,1)} %get-tuple-element.28.grad_ref, bf16[4,16,32,128]{3,2,1,0:T(8,128)(2,1)} %bitcast.20, bf16[3,3,128,128]{3,2,1,0:T(8,128)(2,1)} %spatial_ref.7), custom_call_target="tpu_custom_call" | custom-call | flops 603979776 | bytes 1933312 | tf_op jit(solution)/shard_map/pallas_call | solution.py:583
  150.7 4.5 %all-to-all-done.4.got_ref = bf16[32,56,128]{2,1,0:T(8,128)(2,1)S(1)} async-done(((bf16[32,56,128]{2,1,0:T(8,128)(2,1)}), bf16[32,56,128]{2,1,0:T(8,128)(2,1)S(1)}, u32[]{:S(2)}, u32[]{:S(2)}) %all-to-all-start.4) | async-done | bytes 458784 | tf_op jit(solution)/shard_map/all_to_all | solution.py:748
  155.1 0.9 shard_map.120
  (11 shorter events, 0.1 us)
Async XLA Ops:
  0.6 21.5 %copy-start.2 = (bf16[1,4,16,32,128]{4,3,2,1,0:T(8,128)(2,1)S(1)}, bf16[1,4,16,32,128]{4,3,2,1,0:T(8,128)(2,1)}, u32[]{:S(2)}) copy-start(bf16[1,4,16,32,128]{4,3,2,1,0:T(8,128)(2,1)} %param.6) | copy-start | bytes 1572868
  0.6 21.5 %copy-start.6 = (bf16[3,3,128,128]{3,2,1,0:T(8,128)(2,1)S(1)}, bf16[3,3,128,128]{3,2,1,0:T(8,128)(2,1)}, u32[]{:S(2)}) copy-start(bf16[3,3,128,128]{3,2,1,0:T(8,128)(2,1)} %spatial_ref.7) | copy-start | bytes 884740
  2.5 19.5 %collective-permute-start = (bf16[8,2,32,128]{3,2,1,0:T(8,128)(2,1)S(1)}, bf16[8,2,32,128]{3,2,1,0:T(8,128)(2,1)S(1)}, u32[]{:S(2)}, u32[]{:S(2)}) collective-permute-start(bf16[8,2,32,128]{3,2,1,0:T(8,128)(2,1)S(1)} %pad_maximum_fusion), channel_id=1, source_target_pairs={{0,1},{1,2},{2,3},{3,4},{4,5},{5,6},{6,7},{8,9},{9,10},{10,11},{11... | collective-permute-start | bytes 393224 | tf_op jit(solution)/shard_map/ppermute | solution.py:615
  7.1 14.9 %collective-permute-start.1 = (bf16[8,2,32,128]{3,2,1,0:T(8,128)(2,1)S(1)}, bf16[8,2,32,128]{3,2,1,0:T(8,128)(2,1)S(1)}, u32[]{:S(2)}, u32[]{:S(2)}) collective-permute-start(bf16[8,2,32,128]{3,2,1,0:T(8,128)(2,1)S(1)} %pad_maximum_fusion.1), channel_id=1, source_target_pairs={{1,0},{2,1},{3,2},{4,3},{5,4},{6,5},{7,6},{9,8},{10,9},{11,10},{12... | collective-permute-start | bytes 393224 | tf_op jit(solution)/shard_map/ppermute | solution.py:616
  14.5 10.4 %copy-start.5 = (bf16[3,128,128]{2,1,0:T(8,128)(2,1)S(1)}, bf16[3,128,128]{2,1,0:T(8,128)(2,1)}, u32[]{:S(2)}) copy-start(bf16[3,128,128]{2,1,0:T(8,128)(2,1)} %temporal_hbm.3) | copy-start | bytes 294916
  14.5 10.3 %collective-permute-start.2 = (bf16[2,16,32,128]{3,2,1,0:T(8,128)(2,1)S(1)}, bf16[2,16,32,128]{3,2,1,0:T(8,128)(2,1)S(1)}, u32[]{:S(2)}, u32[]{:S(2)}) collective-permute-start(bf16[2,16,32,128]{3,2,1,0:T(8,128)(2,1)S(1)} %get-tuple-element.35), channel_id=1, source_target_pairs={{0,8},{8,16},{16,24},{24,32},{32,40},{40,48},{48,56},{56,64},{64,7... | collective-permute-start | bytes 786440 | tf_op jit(solution)/shard_map/ppermute | solution.py:612
  16.0 8.9 %collective-permute-start.3 = (bf16[2,2,32,128]{3,2,1,0:T(8,128)(2,1)S(1)}, bf16[2,2,32,128]{3,2,1,0:T(8,128)(2,1)S(1)}, u32[]{:S(2)}, u32[]{:S(2)}) collective-permute-start(bf16[2,2,32,128]{3,2,1,0:T(8,128)(2,1)S(1)} %get-tuple-element.41), channel_id=1, source_target_pairs={{0,9},{1,10},{2,11},{3,12},{4,13},{5,14},{6,15},{8,17},{9,18},{10,... | collective-permute-start | bytes 98312 | tf_op jit(solution)/shard_map/ppermute | solution.py:619
  19.9 4.9 %collective-permute-start.4 = (bf16[2,2,32,128]{3,2,1,0:T(8,128)(2,1)S(1)}, bf16[2,2,32,128]{3,2,1,0:T(8,128)(2,1)S(1)}, u32[]{:S(2)}, u32[]{:S(2)}) collective-permute-start(bf16[2,2,32,128]{3,2,1,0:T(8,128)(2,1)S(1)} %get-tuple-element.40), channel_id=1, source_target_pairs={{1,8},{2,9},{3,10},{4,11},{5,12},{6,13},{7,14},{9,16},{10,17},{11,... | collective-permute-start | bytes 98312 | tf_op jit(solution)/shard_map/ppermute | solution.py:621
  22.0 5.3 %copy-start.7 = (bf16[8,2,32,128]{3,2,1,0:T(8,128)(2,1)}, bf16[8,2,32,128]{3,2,1,0:T(8,128)(2,1)S(1)}, u32[]{:S(2)}) copy-start(bf16[8,2,32,128]{3,2,1,0:T(8,128)(2,1)S(1)} %collective-permute-done.before_ref.before_hbm) | copy-start | bytes 393220
  22.1 24.7 %copy-start.8 = (bf16[8,2,32,128]{3,2,1,0:T(8,128)(2,1)}, bf16[8,2,32,128]{3,2,1,0:T(8,128)(2,1)S(1)}, u32[]{:S(2)}) copy-start(bf16[8,2,32,128]{3,2,1,0:T(8,128)(2,1)S(1)} %collective-permute-done.1.after_ref.after_hbm) | copy-start | bytes 393220
  24.0 0.8 copy-start.4
  24.8 22.1 %copy-start.15 = (bf16[2,16,32,128]{3,2,1,0:T(8,128)(2,1)S(1)}, bf16[2,16,32,128]{3,2,1,0:T(8,128)(2,1)}, u32[]{:S(2)}) copy-start(bf16[2,16,32,128]{3,2,1,0:T(8,128)(2,1)} %get-tuple-element.46) | copy-start | bytes 786436
  24.8 23.0 %copy-start.12 = (bf16[2,2,32,128]{3,2,1,0:T(8,128)(2,1)}, bf16[2,2,32,128]{3,2,1,0:T(8,128)(2,1)S(1)}, u32[]{:S(2)}) copy-start(bf16[2,2,32,128]{3,2,1,0:T(8,128)(2,1)S(1)} %collective-permute-done.3.prev_before_ref) | copy-start | bytes 98308
  24.8 23.0 %copy-start.13 = (bf16[2,2,32,128]{3,2,1,0:T(8,128)(2,1)}, bf16[2,2,32,128]{3,2,1,0:T(8,128)(2,1)S(1)}, u32[]{:S(2)}) copy-start(bf16[2,2,32,128]{3,2,1,0:T(8,128)(2,1)S(1)} %collective-permute-done.4.prev_after_ref) | copy-start | bytes 98308
  24.8 23.0 %copy-start.11 = (bf16[2,16,32,128]{3,2,1,0:T(8,128)(2,1)}, bf16[2,16,32,128]{3,2,1,0:T(8,128)(2,1)S(1)}, u32[]{:S(2)}) copy-start(bf16[2,16,32,128]{3,2,1,0:T(8,128)(2,1)S(1)} %collective-permute-done.2.prev_ref) | copy-start | bytes 786436
  24.9 38.0 %copy-start.1 = (bf16[1,4,16,32,128]{4,3,2,1,0:T(8,128)(2,1)S(1)}, bf16[1,4,16,32,128]{4,3,2,1,0:T(8,128)(2,1)}, u32[]{:S(2)}) copy-start(bf16[1,4,16,32,128]{4,3,2,1,0:T(8,128)(2,1)} %param.11) | copy-start | bytes 1572868
  24.9 38.0 %copy-start.9 = (f32[128]{0:T(128)S(1)}, f32[128]{0:T(128)}, u32[]{:S(2)}) copy-start(f32[128]{0:T(128)} %param.9) | copy-start | bytes 1540
  24.9 38.0 %copy-start.10 = (f32[128]{0:T(128)S(1)}, f32[128]{0:T(128)}, u32[]{:S(2)}) copy-start(f32[128]{0:T(128)} %param.10) | copy-start | bytes 1540
  27.3 37.7 %copy-start = (f32[4,18,32,128]{3,2,1,0:T(8,128)}, f32[4,18,32,128]{3,2,1,0:T(8,128)S(1)}, u32[]{:S(2)}) copy-start(f32[4,18,32,128]{3,2,1,0:T(8,128)S(1)} %get-tuple-element.22.mixed_ref.mixed_hbm) | copy-start | bytes 3538948
  27.3 35.5 %all-to-all-start = ((f32[128,2,128]{2,1,0:T(2,128)}), f32[128,2,128]{2,1,0:T(2,128)S(1)}, u32[]{:S(2)}, u32[]{:S(2)}) async-start(f32[128,2,128]{2,1,0:T(2,128)} %bitcast.3), calls=%async_computation | async-start | bytes 262144 | tf_op jit(solution)/shard_map/all_to_all | solution.py:657
  47.8 29.4 %collective-permute-start.5 = (bf16[4,20,32,128]{3,2,1,0:T(8,128)(2,1)}, bf16[4,20,32,128]{3,2,1,0:T(8,128)(2,1)S(1)}, u32[]{:S(2)}, u32[]{:S(2)}) collective-permute-start(bf16[4,20,32,128]{3,2,1,0:T(8,128)(2,1)} %maximum_maximum_fusion), channel_id=1, source_target_pairs={{8,0},{16,8},{24,16},{32,24},{40,32},{48,40},{56,48},{64,56},{72,6... | collective-permute-start | bytes 1966088 | tf_op jit(solution)/shard_map/ppermute | solution.py:630
  65.0 0.6 copy-start.3
  65.6 23.4 %all-to-all-start.1 = ((f32[128,2,128]{2,1,0:T(2,128)}), f32[128,2,128]{2,1,0:T(2,128)S(1)}, u32[]{:S(2)}, u32[]{:S(2)}) async-start(f32[128,2,128]{2,1,0:T(2,128)} %bitcast.8), calls=%async_computation.1 | async-start | bytes 262144 | tf_op jit(solution)/shard_map/all_to_all | solution.py:690
  77.2 0.9 copy-start.14
  89.0 0.7 copy-start.16
  136.9 18.2 %all-to-all-start.4 = ((bf16[32,56,128]{2,1,0:T(8,128)(2,1)}), bf16[32,56,128]{2,1,0:T(8,128)(2,1)S(1)}, u32[]{:S(2)}, u32[]{:S(2)}) async-start(bf16[32,56,128]{2,1,0:T(8,128)(2,1)} %shard_map.119), calls=%async_computation.4 | async-start | bytes 917504 | tf_op jit(solution)/shard_map/all_to_all | solution.py:748

commit v6 on v5

--- a/solution.py
+++ b/solution.py
@@ -13,7 +13,7 @@
 
 EPS = 1e-05
 TILE = 128
-WIDE, NARROW = 58, 16
+FULL, WIDE, NARROW = 58, 53, 16
 
 
 def iota(shape, dim):
@@ -114,10 +114,6 @@
     return value.astype(jnp.float32).T.astype(jnp.bfloat16)
 
 
-def joined(before_ref, main_ref, after_ref, f):
-    return jnp.concatenate([flat(before_ref[f]), flat(main_ref[f]), flat(after_ref[f])], 0)
-
-
 def own_features(
     x_ref, before_ref, after_ref, spatial_ref, feature_ref, far_ref, weight_ref, sems
 ):
@@ -140,8 +136,6 @@
     before_ref,
     after_ref,
     prev_ref,
-    prev_before_ref,
-    prev_after_ref,
     feature_ref,
     spatial_ref,
     xt_ref,
@@ -154,8 +148,7 @@
     size = rows * columns
 
     def one(f, _):
-        block = joined(prev_before_ref, prev_ref, prev_after_ref, f)
-        out = convolve(block, weight_ref[...], rows + 2, columns, False)
+        out = convolve(flat(prev_ref[f]), weight_ref[...], rows + 2, columns, False)
         prior_ref[f] = out.astype(jnp.bfloat16).reshape(prior_ref.shape[1:])
         return 0
 
@@ -177,8 +170,6 @@
 def mixed_and_sums(
     feature_ref,
     prev_ref,
-    prev_before_ref,
-    prev_after_ref,
     spatial_ref,
     temporal_ref,
     mixed_ref,
@@ -190,8 +181,7 @@
     frames, rows, columns, _ = mixed_ref.shape
 
     def one(f, _):
-        block = joined(prev_before_ref, prev_ref, prev_after_ref, f)
-        out = convolve(block, weight_ref[...], rows, columns, False)
+        out = convolve(flat(prev_ref[f]), weight_ref[...], rows, columns, False)
         prior_ref[f] = out.astype(jnp.bfloat16).reshape(prior_ref.shape[1:])
         return 0
 
@@ -606,19 +596,14 @@
     weight = pltpu.VMEM((3 * channels, 3 * channels), bf16)
     conv = 2 * 9 * channels * channels * columns
 
-    onward = [(i, i + 1) for i in range(time_devices - 1)]
-    back = [(j, i) for i, j in onward]
-    late_frames = x[frames - 2 :]
-    prev = lax.ppermute(late_frames, "tm", onward)
     up = [(i, i + 1) for i in range(height_devices - 1)]
     down = [(j, i) for i, j in up]
     before = lax.ppermute(jnp.concatenate([x[:, rows - 2 :], cot[:, rows - 2 :]], 0), "height", up)
     after = lax.ppermute(jnp.concatenate([x[:, :2], cot[:, :2]], 0), "height", down)
-    cross = ("tm", "height")
-    slant = [(t * height_devices + i, (t + 1) * height_devices + j) for t, _ in onward for i, j in up]
-    prev_before = lax.ppermute(late_frames[:, rows - 2 :], cross, slant)
-    slant = [(t * height_devices + i, (t + 1) * height_devices + j) for t, _ in onward for i, j in down]
-    prev_after = lax.ppermute(late_frames[:, :2], cross, slant)
+    onward = [(i, i + 1) for i in range(time_devices - 1)]
+    back = [(j, i) for i, j in onward]
+    last = jnp.concatenate([before[2:4], x[2:4], after[2:4]], 1)
+    prev = lax.ppermute(last, "tm", onward)
     first = jnp.concatenate(
         [
             jnp.concatenate([before[:2], before[4:6]], 0),
@@ -648,7 +633,7 @@
     mixed, payload = call(
         mixed_and_sums,
         [out((frames, ext) + frame, f32), out((2 * peers, channels), f32)],
-        (feature, prev, prev_before, prev_after, spatial_kernel, temporal_kernel),
+        (feature, prev, spatial_kernel, temporal_kernel),
         [weight, held(two)],
         conv * frames * ext,
         limit=NARROW,
@@ -658,7 +643,7 @@
     xt, ft = call(
         turn,
         [turned_x, turned_features],
-        (x, before, after, prev, prev_before, prev_after, late, spatial_kernel),
+        (x, before, after, prev, late, spatial_kernel),
         [weight, held(two)],
         conv * frames * ext,
     )
@@ -677,6 +662,7 @@
         ],
         conv * 2 * ext,
         far=(following, late, spatial_kernel, temporal_kernel),
+        limit=FULL,
     )
     stats, payload = call(
         functools.partial(statistics_and_sums, time_devices, height_devices, per_frame),

time: 157 us -> 150 us (0.955)
  waiting for transfers between devices: 21.9 us -> 29.5 us
  starting transfers between devices: 52.9 us -> 47.3 us
  local copies, waits for them, and re-layouts: 6.76 us -> 3 us
  Pallas kernels: 32.4 us -> 29.5 us
  blocking collectives: 40.2 us -> 38.4 us
    ppermute x3 -> x1, starting transfers between devices: 7.49 us -> 1.31 us  [shards(): prev = lax.ppermute(last, 'tm', onward)]
    ppermute x3 -> x1, waiting for transfers between devices: 0.01 us -> 4.77 us  [shards(): prev = lax.ppermute(last, 'tm', onward)]
    ppermute x1, starting transfers between devices: 5.46 us -> 8.88 us  [shards(): lax.ppermute(jnp.concatenate([x[:, :2], cot[:, :2]], 0), 'height', down)]
    pallas_call x12, Pallas kernels: 32.4 us -> 29.5 us  [call(): pl.pallas_call(body, out_shape=[*outs, *far_outs], in_specs=[near] * len(...]
    ppermute x1, starting transfers between devices: 4.58 us -> 1.92 us  [shards(): lax.ppermute(jnp.concatenate([x[:, rows - 2:], cot[:, rows - 2:]], 0), 'h...]
    unnamed x34 -> x22, local copies, waits for them, and re-layouts: 3 us -> 0.85 us
    all_to_all x2, waiting for transfers between devices: 17.4 us -> 19.2 us  [shards(): got = lax.all_to_all(payload, share, 0, 0, tiled=True)]
    all_to_all x1, blocking collectives: 21.8 us -> 20.2 us  [shards(): partial = lax.all_to_all(partial, 'tm', 0, 0, tiled=True)]
  transfers between devices with their start and end apart: 9 -> 7, of which waited for: 3 -> 5; matrix products, arithmetic and copies ran while one was open for 2% -> 1% of each run, Pallas kernels for 14% -> 14%
where the time goes in v6:
time: 150 us; the launch traced here: 149 us
  starting transfers between devices  47.3 us (32%)
  blocking collectives  38.4 us (26%)
  waiting for transfers between devices  29.5 us (20%)
  Pallas kernels  29.5 us (20%)
  local copies, waits for them, and re-layouts  3 us (2%)
    pallas_call x12, Pallas kernels, call(): pl.pallas_call(body, out_shape=[*outs, *far_outs], in_specs=[near] * len(...  29.5 us
    all_to_all x2, starting transfers between devices, shards(): got = lax.all_to_all(payload, share, 0, 0, tiled=True)  26.6 us
    all_to_all x1, blocking collectives, shards(): partial = lax.all_to_all(partial, 'tm', 0, 0, tiled=True)  20.2 us
    all_to_all x2, waiting for transfers between devices, shards(): got = lax.all_to_all(payload, share, 0, 0, tiled=True)  19.2 us
    all_to_all x1, blocking collectives, shards(): partial = lax.all_to_all(partial, ends, 0, 0, tiled=True)  18.2 us
    ppermute x1, starting transfers between devices, shards(): lax.ppermute(jnp.concatenate([x[:, :2], cot[:, :2]], 0), 'height', down)  8.88 us
    all_to_all x1, starting transfers between devices, shards(): sums = lax.all_to_all(partial, ends, 0, 0, tiled=True)  7.31 us
    all_to_all x1, waiting for transfers between devices, shards(): sums = lax.all_to_all(partial, ends, 0, 0, tiled=True)  4.81 us
  transfers between devices with their start and end apart: 7, of which 5 were waited for; matrix products, arithmetic and copies ran while one was open for 1% of the time, Pallas kernels for 14%

profile of v6, /device:TPU:1, one launch (start us, length us, event | category | flops | bytes accessed | tf_op | source)
XLA Modules:
  0.0 149.4 jit_solution(12657762607558383264)
XLA Ops:
  0.6 1.0 fusion
  1.6 0.0 copy-start.2
  1.6 0.0 copy-start.7
  1.6 8.9 %collective-permute-start.1 = (bf16[8,2,32,128]{3,2,1,0:T(8,128)(2,1)S(1)}, bf16[8,2,32,128]{3,2,1,0:T(8,128)(2,1)S(1)}, u32[]{:S(2)}, u32[]{:S(2)}) collective-permute-start(bf16[8,2,32,128]{3,2,1,0:T(8,128)(2,1)S(1)} %pad_maximum_fusion.2), channel_id=1, source_target_pairs={{1,0},{2,1},{3,2},{4,3},{5,4},{6,5},{7,6},{9,8},{10,9},{11,10},{12... | collective-permute-start | bytes 393224 | tf_op jit(solution)/shard_map/ppermute | solution.py:602
  10.6 1.9 %collective-permute-start = (bf16[8,2,32,128]{3,2,1,0:T(8,128)(2,1)S(1)}, bf16[8,2,32,128]{3,2,1,0:T(8,128)(2,1)S(1)}, u32[]{:S(2)}, u32[]{:S(2)}) collective-permute-start(bf16[8,2,32,128]{3,2,1,0:T(8,128)(2,1)S(1)} %pad_maximum_fusion.1), channel_id=1, source_target_pairs={{0,1},{1,2},{2,3},{3,4},{4,5},{5,6},{6,7},{8,9},{9,10},{10,11},{11... | collective-permute-start | bytes 393224 | tf_op jit(solution)/shard_map/ppermute | solution.py:601
  12.5 1.2 slice_bitcast_fusion.1
  13.7 0.0 collective-permute-done.1.after_ref.after_hbm
  13.7 0.7 collective-permute-done.before_ref.before_hbm
  14.4 0.0 copy-start.5
  14.5 1.3 collective-permute-start.2
  15.8 0.0 copy-done.2
  15.8 0.0 copy-done.7
  15.8 1.9 %shard_map.109 = (bf16[4,18,32,128]{3,2,1,0:T(8,128)(2,1)S(1)}, bf16[4,18,32,128]{3,2,1,0:T(8,128)(2,1)S(1)}) custom-call(bf16[4,16,32,128]{3,2,1,0:T(8,128)(2,1)S(1)} %bitcast.24, bf16[8,2,32,128]{3,2,1,0:T(8,128)(2,1)S(1)} %collective-permute-done.before_ref.before_hbm, bf16[8,2,32,128]{3,2,1,0:T(8,128)(2,1)S(1)} %collective-permute-done.1.after_ref.after_hbm, ...), custom_call_target="tpu_custom_call" | custom-call | flops 679477248 | bytes 2260992 | tf_op jit(solution)/shard_map/pallas_call | solution.py:573
  17.7 0.0 copy-start.4
  17.7 0.8 copy-done.4
  18.5 4.8 %collective-permute-done.2.prev_ref = bf16[2,20,32,128]{3,2,1,0:T(8,128)(2,1)S(1)} collective-permute-done((bf16[2,20,32,128]{3,2,1,0:T(8,128)(2,1)S(1)}, bf16[2,20,32,128]{3,2,1,0:T(8,128)(2,1)S(1)}, u32[]{:S(2)}, u32[]{:S(2)}) %collective-permute-start.2) | collective-permute-done | bytes 327712 | tf_op jit(solution)/shard_map/ppermute | solution.py:606
  23.3 0.0 copy-done.5
  23.3 0.0 copy-start.1
  23.3 0.0 copy-start.9
  23.3 0.0 copy-start.10
  23.3 2.4 %shard_map.110 = (f32[4,18,32,128]{3,2,1,0:T(8,128)S(1)}, f32[256,128]{1,0:T(8,128)}) custom-call(bf16[4,18,32,128]{3,2,1,0:T(8,128)(2,1)S(1)} %get-tuple-element.20.feature_ref, bf16[2,20,32,128]{3,2,1,0:T(8,128)(2,1)S(1)} %collective-permute-done.2.prev_ref, bf16[3,3,128,128]{3,2,1,0:T(8,128)(2,1)S(1)} %copy-done.7, bf16[3,128,128]{2,1,0:T(8,128)(2,1)S(1)} %copy-done.5), custom_call_target="tpu_custom_call" | custom-call | flops 679477248 | bytes 2621440 | tf_op jit(solution)/shard_map/pallas_call | solution.py:573
  25.7 0.0 copy-start
  25.7 19.2 %all-to-all-start = ((f32[128,2,128]{2,1,0:T(2,128)}), f32[128,2,128]{2,1,0:T(2,128)S(1)}, u32[]{:S(2)}, u32[]{:S(2)}) async-start(f32[128,2,128]{2,1,0:T(2,128)} %bitcast.3), calls=%async_computation | async-start | bytes 262144 | tf_op jit(solution)/shard_map/all_to_all | solution.py:642
  44.9 0.9 maximum_maximum_fusion
  45.8 1.3 collective-permute-start.3
  47.1 13.8 %all-to-all-done = f32[128,2,128]{2,1,0:T(2,128)S(1)} async-done(((f32[128,2,128]{2,1,0:T(2,128)}), f32[128,2,128]{2,1,0:T(2,128)S(1)}, u32[]{:S(2)}, u32[]{:S(2)}) %all-to-all-start) | async-done | bytes 131104 | tf_op jit(solution)/shard_map/all_to_all | solution.py:642
  60.9 0.0 copy-done.1
  60.9 0.0 copy-done.9
  60.9 0.0 copy-done.10
  60.9 2.2 %shard_map.111 = (f32[144,128]{1,0:T(8,128)S(1)}, f32[256,128]{1,0:T(8,128)}) custom-call(f32[256,128]{1,0:T(8,128)S(1)} %bitcast.27, f32[4,18,32,128]{3,2,1,0:T(8,128)S(1)} %get-tuple-element.22.mixed_ref.mixed_hbm, bf16[4,16,32,128]{3,2,1,0:T(8,128)(2,1)S(1)} %bitcast.19, f32[1,128]{1,0:T(1,128)S(1)} %bitcast.28, f32[1,128]{1,0:T(1,128)S(1)} %bitcast.31), custom_call_target="tpu_custom_call" | custom-call | bytes 2040832 | tf_op jit(solution)/shard_map/pallas_call | solution.py:573
  63.1 0.0 copy-done
  63.1 7.4 %all-to-all-start.1 = ((f32[128,2,128]{2,1,0:T(2,128)}), f32[128,2,128]{2,1,0:T(2,128)S(1)}, u32[]{:S(2)}, u32[]{:S(2)}) async-start(f32[128,2,128]{2,1,0:T(2,128)} %bitcast.8), calls=%async_computation.1 | async-start | bytes 262144 | tf_op jit(solution)/shard_map/all_to_all | solution.py:676
  70.5 4.2 %shard_map.115 = (bf16[384,2048]{1,0:T(8,128)(2,1)}, bf16[128,3072]{1,0:T(8,128)(2,1)}) custom-call(bf16[4,16,32,128]{3,2,1,0:T(8,128)(2,1)} %bitcast.23, bf16[8,2,32,128]{3,2,1,0:T(8,128)(2,1)S(1)} %collective-permute-done.before_ref.before_hbm, bf16[8,2,32,128]{3,2,1,0:T(8,128)(2,1)S(1)} %collective-permute-done.1.after_ref.after_hbm, ...), custom_call_target="tpu_custom_call" | custom-call | flops 679477248 | bytes 4358144 | tf_op jit(solution)/shard_map/pallas_call | solution.py:573
  74.6 0.0 collective-permute-done.3.next_hbm
  74.6 3.2 %shard_map.113.mixed_next_hbm = f32[2,18,32,128]{3,2,1,0:T(8,128)} custom-call(bf16[4,20,32,128]{3,2,1,0:T(8,128)(2,1)} %collective-permute-done.3.next_hbm, bf16[4,18,32,128]{3,2,1,0:T(8,128)(2,1)} %copy-done.4, bf16[3,3,128,128]{3,2,1,0:T(8,128)(2,1)} %spatial_ref.7, bf16[3,128,128]{2,1,0:T(8,128)(2,1)} %temporal_hbm.3), custom_call_target="tpu_custom_call" | custom-call | flops 339738624 | bytes 2228224 | tf_op jit(solution)/shard_map/pallas_call | solution.py:573
  77.8 0.0 copy-start.6
  77.8 3.2 %shard_map.114.scaled_hbm = f32[6,18,32,128]{3,2,1,0:T(8,128)} custom-call(f32[144,128]{1,0:T(8,128)S(1)} %get-tuple-element.23.stats_ref, f32[1,128]{1,0:T(1,128)S(1)} %bitcast.29, f32[1,128]{1,0:T(1,128)S(1)} %bitcast.32, f32[4,18,32,128]{3,2,1,0:T(8,128)} %copy-done, f32[2,18,32,128]{3,2,1,0:T(8,128)} %shard_map.113.mixed_next_hbm, ...), custom_call_target="tpu_custom_call" | custom-call | bytes 5055488 | tf_op jit(solution)/shard_map/pallas_call | solution.py:573
  81.1 5.4 %all-to-all-done.1 = f32[128,2,128]{2,1,0:T(2,128)S(1)} async-done(((f32[128,2,128]{2,1,0:T(2,128)}), f32[128,2,128]{2,1,0:T(2,128)S(1)}, u32[]{:S(2)}, u32[]{:S(2)}) %all-to-all-start.1) | async-done | bytes 131104 | tf_op jit(solution)/shard_map/all_to_all | solution.py:676
  86.5 0.0 copy-done.6
  86.5 4.4 %shard_map.116 = (bf16[32,56,128]{2,1,0:T(8,128)(2,1)S(1)}, bf16[4,18,32,128]{3,2,1,0:T(8,128)(2,1)}) custom-call(f32[256,128]{1,0:T(8,128)S(1)} %bitcast.26, f32[144,128]{1,0:T(8,128)S(1)} %get-tuple-element.23.stats_ref, f32[4,18,32,128]{3,2,1,0:T(8,128)} %copy-done, f32[2,18,32,128]{3,2,1,0:T(8,128)} %shard_map.113.mixed_next_hbm, ...), custom_call_target="tpu_custom_call" | custom-call | flops 1207959552 | bytes 7249920 | tf_op jit(solution)/shard_map/pallas_call | solution.py:573
  90.9 18.2 %all_to_all.37.got_ref = bf16[32,56,128]{2,1,0:T(8,128)(2,1)S(1)} all-to-all(bf16[32,56,128]{2,1,0:T(8,128)(2,1)S(1)} %get-tuple-element.29), channel_id=1, replica_groups=mesh['rep'=4,'tm'=16,'height'=8] {'rep','height'}, dimensions={0} | all-to-all | bytes 917504 | tf_op jit(solution)/shard_map/all_to_all | solution.py:722
  109.1 0.0 copy-start.3
  109.1 0.1 shard_map.118
  109.1 20.2 %all_to_all.38.got_ref = bf16[16,56,128]{2,1,0:T(8,128)(2,1)S(1)} all-to-all(bf16[16,56,128]{2,1,0:T(8,128)(2,1)S(1)} %shard_map.118), channel_id=1, replica_groups=mesh['rep'=4,'tm'=16,'height'=8] {'tm'}, dimensions={0} | all-to-all | bytes 458752 | tf_op jit(solution)/shard_map/all_to_all | solution.py:732
  129.4 0.8 shard_map.119
  130.2 0.0 copy-start.8
  130.2 7.3 %all-to-all-start.4 = ((bf16[32,56,128]{2,1,0:T(8,128)(2,1)}), bf16[32,56,128]{2,1,0:T(8,128)(2,1)S(1)}, u32[]{:S(2)}, u32[]{:S(2)}) async-start(bf16[32,56,128]{2,1,0:T(8,128)(2,1)} %shard_map.119), calls=%async_computation.4 | async-start | bytes 917504 | tf_op jit(solution)/shard_map/all_to_all | solution.py:734
  137.5 0.0 copy-done.3
  137.5 2.6 %shard_map.112 = bf16[4,16,32,128]{3,2,1,0:T(8,128)(2,1)} custom-call(f32[144,128]{1,0:T(8,128)S(1)} %get-tuple-element.23.stats_ref, f32[4,18,32,128]{3,2,1,0:T(8,128)} %copy-done, bf16[4,16,32,128]{3,2,1,0:T(8,128)(2,1)S(1)} %bitcast.25, f32[1,128]{1,0:T(1,128)S(1)} %bitcast.30, f32[1,128]{1,0:T(1,128)S(1)} %bitcast.33), custom_call_target="tpu_custom_call" | custom-call | bytes 2302976 | tf_op jit(solution)/shard_map/pallas_call | solution.py:573
  140.1 0.0 copy-done.8
  140.1 3.6 %shard_map.117 = bf16[4,16,32,128]{3,2,1,0:T(8,128)(2,1)} custom-call(bf16[4,18,32,128]{3,2,1,0:T(8,128)(2,1)} %get-tuple-element.28.grad_ref, bf16[4,16,32,128]{3,2,1,0:T(8,128)(2,1)S(1)} %bitcast.21, bf16[3,3,128,128]{3,2,1,0:T(8,128)(2,1)S(1)} %copy-done.8), custom_call_target="tpu_custom_call" | custom-call | flops 603979776 | bytes 1933312 | tf_op jit(solution)/shard_map/pallas_call | solution.py:573
  143.7 4.8 %all-to-all-done.4.got_ref = bf16[32,56,128]{2,1,0:T(8,128)(2,1)S(1)} async-done(((bf16[32,56,128]{2,1,0:T(8,128)(2,1)}), bf16[32,56,128]{2,1,0:T(8,128)(2,1)S(1)}, u32[]{:S(2)}, u32[]{:S(2)}) %all-to-all-start.4) | async-done | bytes 458784 | tf_op jit(solution)/shard_map/all_to_all | solution.py:734
  148.5 0.9 shard_map.120
  (5 shorter events, 0.1 us)
Async XLA Ops:
  1.6 14.2 %copy-start.2 = (bf16[1,4,16,32,128]{4,3,2,1,0:T(8,128)(2,1)S(1)}, bf16[1,4,16,32,128]{4,3,2,1,0:T(8,128)(2,1)}, u32[]{:S(2)}) copy-start(bf16[1,4,16,32,128]{4,3,2,1,0:T(8,128)(2,1)} %param.6) | copy-start | bytes 1572868
  1.6 14.2 %copy-start.7 = (bf16[3,3,128,128]{3,2,1,0:T(8,128)(2,1)S(1)}, bf16[3,3,128,128]{3,2,1,0:T(8,128)(2,1)}, u32[]{:S(2)}) copy-start(bf16[3,3,128,128]{3,2,1,0:T(8,128)(2,1)} %spatial_ref.7) | copy-start | bytes 884740
  1.6 12.0 %collective-permute-start.1 = (bf16[8,2,32,128]{3,2,1,0:T(8,128)(2,1)S(1)}, bf16[8,2,32,128]{3,2,1,0:T(8,128)(2,1)S(1)}, u32[]{:S(2)}, u32[]{:S(2)}) collective-permute-start(bf16[8,2,32,128]{3,2,1,0:T(8,128)(2,1)S(1)} %pad_maximum_fusion.2), channel_id=1, source_target_pairs={{1,0},{2,1},{3,2},{4,3},{5,4},{6,5},{7,6},{9,8},{10,9},{11,10},{12... | collective-permute-start | bytes 393224 | tf_op jit(solution)/shard_map/ppermute | solution.py:602
  10.6 3.9 %collective-permute-start = (bf16[8,2,32,128]{3,2,1,0:T(8,128)(2,1)S(1)}, bf16[8,2,32,128]{3,2,1,0:T(8,128)(2,1)S(1)}, u32[]{:S(2)}, u32[]{:S(2)}) collective-permute-start(bf16[8,2,32,128]{3,2,1,0:T(8,128)(2,1)S(1)} %pad_maximum_fusion.1), channel_id=1, source_target_pairs={{0,1},{1,2},{2,3},{3,4},{4,5},{5,6},{6,7},{8,9},{9,10},{10,11},{11... | collective-permute-start | bytes 393224 | tf_op jit(solution)/shard_map/ppermute | solution.py:601
  14.4 8.9 %copy-start.5 = (bf16[3,128,128]{2,1,0:T(8,128)(2,1)S(1)}, bf16[3,128,128]{2,1,0:T(8,128)(2,1)}, u32[]{:S(2)}) copy-start(bf16[3,128,128]{2,1,0:T(8,128)(2,1)} %temporal_hbm.3) | copy-start | bytes 294916
  14.5 8.8 %collective-permute-start.2 = (bf16[2,20,32,128]{3,2,1,0:T(8,128)(2,1)S(1)}, bf16[2,20,32,128]{3,2,1,0:T(8,128)(2,1)S(1)}, u32[]{:S(2)}, u32[]{:S(2)}) collective-permute-start(bf16[2,20,32,128]{3,2,1,0:T(8,128)(2,1)S(1)} %pad_maximum_fusion), channel_id=1, source_target_pairs={{0,8},{8,16},{16,24},{24,32},{32,40},{40,48},{48,56},{56,64},{64,7... | collective-permute-start | bytes 983048 | tf_op jit(solution)/shard_map/ppermute | solution.py:606
  17.7 0.8 copy-start.4
  23.3 37.6 %copy-start.1 = (bf16[1,4,16,32,128]{4,3,2,1,0:T(8,128)(2,1)S(1)}, bf16[1,4,16,32,128]{4,3,2,1,0:T(8,128)(2,1)}, u32[]{:S(2)}) copy-start(bf16[1,4,16,32,128]{4,3,2,1,0:T(8,128)(2,1)} %param.11) | copy-start | bytes 1572868
  23.3 37.6 %copy-start.9 = (f32[128]{0:T(128)S(1)}, f32[128]{0:T(128)}, u32[]{:S(2)}) copy-start(f32[128]{0:T(128)} %param.9) | copy-start | bytes 1540
  23.3 37.6 %copy-start.10 = (f32[128]{0:T(128)S(1)}, f32[128]{0:T(128)}, u32[]{:S(2)}) copy-start(f32[128]{0:T(128)} %param.10) | copy-start | bytes 1540
  25.7 37.4 %copy-start = (f32[4,18,32,128]{3,2,1,0:T(8,128)}, f32[4,18,32,128]{3,2,1,0:T(8,128)S(1)}, u32[]{:S(2)}) copy-start(f32[4,18,32,128]{3,2,1,0:T(8,128)S(1)} %get-tuple-element.22.mixed_ref.mixed_hbm) | copy-start | bytes 3538948
  25.7 35.2 %all-to-all-start = ((f32[128,2,128]{2,1,0:T(2,128)}), f32[128,2,128]{2,1,0:T(2,128)S(1)}, u32[]{:S(2)}, u32[]{:S(2)}) async-start(f32[128,2,128]{2,1,0:T(2,128)} %bitcast.3), calls=%async_computation | async-start | bytes 262144 | tf_op jit(solution)/shard_map/all_to_all | solution.py:642
  45.8 28.8 %collective-permute-start.3 = (bf16[4,20,32,128]{3,2,1,0:T(8,128)(2,1)}, bf16[4,20,32,128]{3,2,1,0:T(8,128)(2,1)}, u32[]{:S(2)}, u32[]{:S(2)}) collective-permute-start(bf16[4,20,32,128]{3,2,1,0:T(8,128)(2,1)} %maximum_maximum_fusion), channel_id=1, source_target_pairs={{8,0},{16,8},{24,16},{32,24},{40,32},{48,40},{56,48},{64,56},{72,6... | collective-permute-start | bytes 1966088 | tf_op jit(solution)/shard_map/ppermute | solution.py:615
  63.1 23.4 %all-to-all-start.1 = ((f32[128,2,128]{2,1,0:T(2,128)}), f32[128,2,128]{2,1,0:T(2,128)S(1)}, u32[]{:S(2)}, u32[]{:S(2)}) async-start(f32[128,2,128]{2,1,0:T(2,128)} %bitcast.8), calls=%async_computation.1 | async-start | bytes 262144 | tf_op jit(solution)/shard_map/all_to_all | solution.py:676
  77.8 8.7 %copy-start.6 = (bf16[3,128,128]{2,1,0:T(8,128)(2,1)S(1)}, bf16[3,128,128]{2,1,0:T(8,128)(2,1)}, u32[]{:S(2)}) copy-start(bf16[3,128,128]{2,1,0:T(8,128)(2,1)} %temporal_hbm.3) | copy-start | bytes 294916
  109.1 28.4 %copy-start.3 = (bf16[1,4,16,32,128]{4,3,2,1,0:T(8,128)(2,1)S(1)}, bf16[1,4,16,32,128]{4,3,2,1,0:T(8,128)(2,1)}, u32[]{:S(2)}) copy-start(bf16[1,4,16,32,128]{4,3,2,1,0:T(8,128)(2,1)} %param.6) | copy-start | bytes 1572868
  130.2 9.9 %copy-start.8 = (bf16[3,3,128,128]{3,2,1,0:T(8,128)(2,1)S(1)}, bf16[3,3,128,128]{3,2,1,0:T(8,128)(2,1)}, u32[]{:S(2)}) copy-start(bf16[3,3,128,128]{3,2,1,0:T(8,128)(2,1)} %spatial_ref.7) | copy-start | bytes 884740
  130.2 18.4 %all-to-all-start.4 = ((bf16[32,56,128]{2,1,0:T(8,128)(2,1)}), bf16[32,56,128]{2,1,0:T(8,128)(2,1)S(1)}, u32[]{:S(2)}, u32[]{:S(2)}) async-start(bf16[32,56,128]{2,1,0:T(8,128)(2,1)} %shard_map.119), calls=%async_computation.4 | async-start | bytes 917504 | tf_op jit(solution)/shard_map/all_to_all | solution.py:734

commit v7 on v6

--- a/solution.py
+++ b/solution.py
@@ -282,7 +282,7 @@
         def some(i, sums, f=f, mean=mean, inv_std=inv_std):
             normed = (flat(mixed_ref[f, pl.ds(1 + i * step, step)]) - mean) * inv_std
             pre = normed * gain + shift
-            sigma = 1.0 / (1.0 + jnp.exp(-pre))
+            sigma = sigmoid(pre)
             cot = flat(cot_ref[f, pl.ds(i * step, step)]).astype(jnp.float32)
             grad = cot * (sigma * (1.0 + pre * (1.0 - sigma)))
             split = (-1, 8, TILE)
@@ -301,9 +301,13 @@
     stats_ref[at : at + 16] = jnp.where(iota((16, TILE), 0) < 8, total_b, total_a)
 
 
+def sigmoid(value):
+    return 0.5 + 0.5 * jnp.tanh(0.5 * value)
+
+
 def normalised(mixed, mean, inv_std, gain, shift):
     pre = (mixed - mean) * inv_std * gain + shift
-    return pre, 1.0 / (1.0 + jnp.exp(-pre))
+    return pre, sigmoid(pre)
 
 
 def write_outputs(time_devices, stats_ref, mixed_ref, x_ref, gain_ref, shift_ref, outputs_ref):
@@ -429,15 +433,16 @@
     rows = ext - 2
     copies = fetch(
         [
-            (mixed_hbm, mixed_ref.at[pl.ds(0, frames)]),
-            (mixed_next_hbm, mixed_ref.at[pl.ds(frames, 2)]),
-            (scaled_hbm, scaled_ref),
-            (temporal_hbm, temporal_ref),
-            (xt_hbm, xt_ref),
-            (ft_hbm, ft_ref),
-        ],
+            (mixed_hbm.at[f] if f < frames else mixed_next_hbm.at[f - frames], mixed_ref.at[f])
+            if kind
+            else (scaled_hbm.at[f], scaled_ref.at[f])
+            for f in range(frames + 2)
+            for kind in range(2)
+        ]
+        + [(temporal_hbm, temporal_ref), (ft_hbm, ft_ref), (xt_hbm, xt_ref)],
         sems,
     )
+    last = 2 * (frames + 2)
     me, level = lax.axis_index("tm"), lax.axis_index("height")
     following = jnp.minimum(me + 1, time_devices - 1)
     here = per_device_sums(got_ref[...], time_devices, height_devices, False)
@@ -461,14 +466,14 @@
             run = run + values[f]
             at = (2 * f + kind) * time_devices
             carry_ref[at : at + time_devices] = run
-    for copy in copies[:3]:
-        copy.wait()
     exists = (me < time_devices - 1).astype(jnp.float32)
     for f in range(frames + 2):
         own = f < frames
         at, g = (me, f) if own else (following, f - frames)
         first = carry_ref[pl.ds(2 * g * time_devices + at, 1)]
         second = 2.0 * carry_ref[pl.ds((2 * g + 1) * time_devices + at, 1)]
+        copies[2 * f].wait()
+        copies[2 * f + 1].wait()
 
         def some(i, _, f=f, own=own, first=first, second=second):
             at = pl.ds(i * 3, 3)
@@ -479,7 +484,7 @@
             return 0
 
         lax.fori_loop(0, ext // 3, some, 0, unroll=3)
-    copies[3].wait()
+    copies[last].wait()
     back = jnp.concatenate([temporal_ref[k] for k in range(3)], axis=1)
     leaving = []
     place = iota((ext * columns, TILE), 0) // columns
@@ -505,7 +510,7 @@
             ],
             axis=1,
         )
-    for copy in copies[4:]:
+    for copy in copies[last + 1 :]:
         copy.wait()
     inner = flat(mixed_grad_ref[:frames, 1 : rows + 1])
     temporal = [dot(ft_ref[:, k * size : (k + frames) * size], inner) for k in range(3)]
@@ -712,7 +717,7 @@
             held(turned_features),
             held(temporal_kernel),
             pltpu.VMEM((frames * rows * columns, 3 * channels), bf16),
-            dma(6),
+            dma(2 * frames + 7),
             dma(frames),
         ],
         conv * frames * rows * 2,

time: 150 us -> 150 us (level)
  no operation moved by 1% of the time
where the time goes in v7:
time: 150 us; the launch traced here: 149 us
  starting transfers between devices  47.3 us (32%)
  blocking collectives  38.4 us (26%)
  waiting for transfers between devices  29.6 us (20%)
  Pallas kernels  29.2 us (19%)
  local copies, waits for them, and re-layouts  3 us (2%)
    pallas_call x12, Pallas kernels, call(): pl.pallas_call(body, out_shape=[*outs, *far_outs], in_specs=[near] * len(...  29.2 us
    all_to_all x2, starting transfers between devices, shards(): got = lax.all_to_all(payload, share, 0, 0, tiled=True)  26.6 us
    all_to_all x1, blocking collectives, shards(): partial = lax.all_to_all(partial, 'tm', 0, 0, tiled=True)  20.2 us
    all_to_all x2, waiting for transfers between devices, shards(): got = lax.all_to_all(payload, share, 0, 0, tiled=True)  19.2 us
    all_to_all x1, blocking collectives, shards(): partial = lax.all_to_all(partial, ends, 0, 0, tiled=True)  18.2 us
    ppermute x1, starting transfers between devices, shards(): lax.ppermute(jnp.concatenate([x[:, :2], cot[:, :2]], 0), 'height', down)  8.88 us
    all_to_all x1, starting transfers between devices, shards(): sums = lax.all_to_all(partial, ends, 0, 0, tiled=True)  7.31 us
    all_to_all x1, waiting for transfers between devices, shards(): sums = lax.all_to_all(partial, ends, 0, 0, tiled=True)  4.88 us
  transfers between devices with their start and end apart: 7, of which 5 were waited for; matrix products, arithmetic and copies ran while one was open for 1% of the time, Pallas kernels for 14%

profile of v7, /device:TPU:1, one launch (start us, length us, event | category | flops | bytes accessed | tf_op | source)
XLA Modules:
  0.0 149.3 jit_solution(15139573220906093887)
XLA Ops:
  0.6 1.0 fusion
  1.6 0.0 copy-start.2
  1.6 0.0 copy-start.7
  1.6 8.9 %collective-permute-start.1 = (bf16[8,2,32,128]{3,2,1,0:T(8,128)(2,1)S(1)}, bf16[8,2,32,128]{3,2,1,0:T(8,128)(2,1)S(1)}, u32[]{:S(2)}, u32[]{:S(2)}) collective-permute-start(bf16[8,2,32,128]{3,2,1,0:T(8,128)(2,1)S(1)} %pad_maximum_fusion.2), channel_id=1, source_target_pairs={{1,0},{2,1},{3,2},{4,3},{5,4},{6,5},{7,6},{9,8},{10,9},{11,10},{12... | collective-permute-start | bytes 393224 | tf_op jit(solution)/shard_map/ppermute | solution.py:607
  10.6 1.9 %collective-permute-start = (bf16[8,2,32,128]{3,2,1,0:T(8,128)(2,1)S(1)}, bf16[8,2,32,128]{3,2,1,0:T(8,128)(2,1)S(1)}, u32[]{:S(2)}, u32[]{:S(2)}) collective-permute-start(bf16[8,2,32,128]{3,2,1,0:T(8,128)(2,1)S(1)} %pad_maximum_fusion.1), channel_id=1, source_target_pairs={{0,1},{1,2},{2,3},{3,4},{4,5},{5,6},{6,7},{8,9},{9,10},{10,11},{11... | collective-permute-start | bytes 393224 | tf_op jit(solution)/shard_map/ppermute | solution.py:606
  12.5 1.2 slice_bitcast_fusion.1
  13.7 0.0 collective-permute-done.1.after_ref.after_hbm
  13.7 0.7 collective-permute-done.before_ref.before_hbm
  14.4 0.0 copy-start.5
  14.5 1.3 collective-permute-start.2
  15.8 0.0 copy-done.2
  15.8 0.0 copy-done.7
  15.8 1.9 %shard_map.109 = (bf16[4,18,32,128]{3,2,1,0:T(8,128)(2,1)S(1)}, bf16[4,18,32,128]{3,2,1,0:T(8,128)(2,1)S(1)}) custom-call(bf16[4,16,32,128]{3,2,1,0:T(8,128)(2,1)S(1)} %bitcast.24, bf16[8,2,32,128]{3,2,1,0:T(8,128)(2,1)S(1)} %collective-permute-done.before_ref.before_hbm, bf16[8,2,32,128]{3,2,1,0:T(8,128)(2,1)S(1)} %collective-permute-done.1.after_ref.after_hbm, ...), custom_call_target="tpu_custom_call" | custom-call | flops 679477248 | bytes 2260992 | tf_op jit(solution)/shard_map/pallas_call | solution.py:578
  17.7 0.0 copy-start.4
  17.7 0.8 copy-done.4
  18.5 4.8 %collective-permute-done.2.prev_ref = bf16[2,20,32,128]{3,2,1,0:T(8,128)(2,1)S(1)} collective-permute-done((bf16[2,20,32,128]{3,2,1,0:T(8,128)(2,1)S(1)}, bf16[2,20,32,128]{3,2,1,0:T(8,128)(2,1)S(1)}, u32[]{:S(2)}, u32[]{:S(2)}) %collective-permute-start.2) | collective-permute-done | bytes 327712 | tf_op jit(solution)/shard_map/ppermute | solution.py:611
  23.3 0.0 copy-done.5
  23.3 0.0 copy-start.1
  23.3 0.0 copy-start.9
  23.3 0.0 copy-start.10
  23.3 2.4 %shard_map.110 = (f32[4,18,32,128]{3,2,1,0:T(8,128)S(1)}, f32[256,128]{1,0:T(8,128)}) custom-call(bf16[4,18,32,128]{3,2,1,0:T(8,128)(2,1)S(1)} %get-tuple-element.20.feature_ref, bf16[2,20,32,128]{3,2,1,0:T(8,128)(2,1)S(1)} %collective-permute-done.2.prev_ref, bf16[3,3,128,128]{3,2,1,0:T(8,128)(2,1)S(1)} %copy-done.7, bf16[3,128,128]{2,1,0:T(8,128)(2,1)S(1)} %copy-done.5), custom_call_target="tpu_custom_call" | custom-call | flops 679477248 | bytes 2621440 | tf_op jit(solution)/shard_map/pallas_call | solution.py:578
  25.7 0.0 copy-start
  25.7 19.2 %all-to-all-start = ((f32[128,2,128]{2,1,0:T(2,128)}), f32[128,2,128]{2,1,0:T(2,128)S(1)}, u32[]{:S(2)}, u32[]{:S(2)}) async-start(f32[128,2,128]{2,1,0:T(2,128)} %bitcast.3), calls=%async_computation | async-start | bytes 262144 | tf_op jit(solution)/shard_map/all_to_all | solution.py:647
  44.9 0.9 maximum_maximum_fusion
  45.8 1.3 collective-permute-start.3
  47.1 13.8 %all-to-all-done = f32[128,2,128]{2,1,0:T(2,128)S(1)} async-done(((f32[128,2,128]{2,1,0:T(2,128)}), f32[128,2,128]{2,1,0:T(2,128)S(1)}, u32[]{:S(2)}, u32[]{:S(2)}) %all-to-all-start) | async-done | bytes 131104 | tf_op jit(solution)/shard_map/all_to_all | solution.py:647
  60.9 0.0 copy-done.1
  60.9 0.0 copy-done.9
  60.9 0.0 copy-done.10
  60.9 2.1 %shard_map.111 = (f32[144,128]{1,0:T(8,128)S(1)}, f32[256,128]{1,0:T(8,128)}) custom-call(f32[256,128]{1,0:T(8,128)S(1)} %bitcast.27, f32[4,18,32,128]{3,2,1,0:T(8,128)S(1)} %get-tuple-element.22.mixed_ref.mixed_hbm, bf16[4,16,32,128]{3,2,1,0:T(8,128)(2,1)S(1)} %bitcast.19, f32[1,128]{1,0:T(1,128)S(1)} %bitcast.28, f32[1,128]{1,0:T(1,128)S(1)} %bitcast.31), custom_call_target="tpu_custom_call" | custom-call | bytes 2040832 | tf_op jit(solution)/shard_map/pallas_call | solution.py:578
  63.1 0.0 copy-done
  63.1 7.4 %all-to-all-start.1 = ((f32[128,2,128]{2,1,0:T(2,128)}), f32[128,2,128]{2,1,0:T(2,128)S(1)}, u32[]{:S(2)}, u32[]{:S(2)}) async-start(f32[128,2,128]{2,1,0:T(2,128)} %bitcast.8), calls=%async_computation.1 | async-start | bytes 262144 | tf_op jit(solution)/shard_map/all_to_all | solution.py:681
  70.4 4.2 %shard_map.115 = (bf16[384,2048]{1,0:T(8,128)(2,1)}, bf16[128,3072]{1,0:T(8,128)(2,1)}) custom-call(bf16[4,16,32,128]{3,2,1,0:T(8,128)(2,1)} %bitcast.23, bf16[8,2,32,128]{3,2,1,0:T(8,128)(2,1)S(1)} %collective-permute-done.before_ref.before_hbm, bf16[8,2,32,128]{3,2,1,0:T(8,128)(2,1)S(1)} %collective-permute-done.1.after_ref.after_hbm, ...), custom_call_target="tpu_custom_call" | custom-call | flops 679477248 | bytes 4358144 | tf_op jit(solution)/shard_map/pallas_call | solution.py:578
  74.6 0.0 collective-permute-done.3.next_hbm
  74.6 3.2 %shard_map.113.mixed_next_hbm = f32[2,18,32,128]{3,2,1,0:T(8,128)} custom-call(bf16[4,20,32,128]{3,2,1,0:T(8,128)(2,1)} %collective-permute-done.3.next_hbm, bf16[4,18,32,128]{3,2,1,0:T(8,128)(2,1)} %copy-done.4, bf16[3,3,128,128]{3,2,1,0:T(8,128)(2,1)} %spatial_ref.7, bf16[3,128,128]{2,1,0:T(8,128)(2,1)} %temporal_hbm.3), custom_call_target="tpu_custom_call" | custom-call | flops 339738624 | bytes 2228224 | tf_op jit(solution)/shard_map/pallas_call | solution.py:578
  77.8 0.0 copy-start.6
  77.8 3.2 %shard_map.114.scaled_hbm = f32[6,18,32,128]{3,2,1,0:T(8,128)} custom-call(f32[144,128]{1,0:T(8,128)S(1)} %get-tuple-element.23.stats_ref, f32[1,128]{1,0:T(1,128)S(1)} %bitcast.29, f32[1,128]{1,0:T(1,128)S(1)} %bitcast.32, f32[4,18,32,128]{3,2,1,0:T(8,128)} %copy-done, f32[2,18,32,128]{3,2,1,0:T(8,128)} %shard_map.113.mixed_next_hbm, ...), custom_call_target="tpu_custom_call" | custom-call | bytes 5055488 | tf_op jit(solution)/shard_map/pallas_call | solution.py:578
  81.0 5.4 %all-to-all-done.1 = f32[128,2,128]{2,1,0:T(2,128)S(1)} async-done(((f32[128,2,128]{2,1,0:T(2,128)}), f32[128,2,128]{2,1,0:T(2,128)S(1)}, u32[]{:S(2)}, u32[]{:S(2)}) %all-to-all-start.1) | async-done | bytes 131104 | tf_op jit(solution)/shard_map/all_to_all | solution.py:681
  86.4 0.0 copy-done.6
  86.4 4.3 %shard_map.116 = (bf16[32,56,128]{2,1,0:T(8,128)(2,1)S(1)}, bf16[4,18,32,128]{3,2,1,0:T(8,128)(2,1)}) custom-call(f32[256,128]{1,0:T(8,128)S(1)} %bitcast.26, f32[144,128]{1,0:T(8,128)S(1)} %get-tuple-element.23.stats_ref, f32[4,18,32,128]{3,2,1,0:T(8,128)} %copy-done, f32[2,18,32,128]{3,2,1,0:T(8,128)} %shard_map.113.mixed_next_hbm, ...), custom_call_target="tpu_custom_call" | custom-call | flops 1207959552 | bytes 7249920 | tf_op jit(solution)/shard_map/pallas_call | solution.py:578
  90.8 18.2 %all_to_all.37.got_ref = bf16[32,56,128]{2,1,0:T(8,128)(2,1)S(1)} all-to-all(bf16[32,56,128]{2,1,0:T(8,128)(2,1)S(1)} %get-tuple-element.29), channel_id=1, replica_groups=mesh['rep'=4,'tm'=16,'height'=8] {'rep','height'}, dimensions={0} | all-to-all | bytes 917504 | tf_op jit(solution)/shard_map/all_to_all | solution.py:727
  108.9 0.0 copy-start.3
  108.9 0.1 shard_map.118
  109.0 20.2 %all_to_all.38.got_ref = bf16[16,56,128]{2,1,0:T(8,128)(2,1)S(1)} all-to-all(bf16[16,56,128]{2,1,0:T(8,128)(2,1)S(1)} %shard_map.118), channel_id=1, replica_groups=mesh['rep'=4,'tm'=16,'height'=8] {'tm'}, dimensions={0} | all-to-all | bytes 458752 | tf_op jit(solution)/shard_map/all_to_all | solution.py:737
  129.2 0.8 shard_map.119
  130.0 0.0 copy-start.8
  130.0 7.3 %all-to-all-start.4 = ((bf16[32,56,128]{2,1,0:T(8,128)(2,1)}), bf16[32,56,128]{2,1,0:T(8,128)(2,1)S(1)}, u32[]{:S(2)}, u32[]{:S(2)}) async-start(bf16[32,56,128]{2,1,0:T(8,128)(2,1)} %shard_map.119), calls=%async_computation.4 | async-start | bytes 917504 | tf_op jit(solution)/shard_map/all_to_all | solution.py:739
  137.3 0.0 copy-done.3
  137.3 2.5 %shard_map.112 = bf16[4,16,32,128]{3,2,1,0:T(8,128)(2,1)} custom-call(f32[144,128]{1,0:T(8,128)S(1)} %get-tuple-element.23.stats_ref, f32[4,18,32,128]{3,2,1,0:T(8,128)} %copy-done, bf16[4,16,32,128]{3,2,1,0:T(8,128)(2,1)S(1)} %bitcast.25, f32[1,128]{1,0:T(1,128)S(1)} %bitcast.30, f32[1,128]{1,0:T(1,128)S(1)} %bitcast.33), custom_call_target="tpu_custom_call" | custom-call | bytes 2302976 | tf_op jit(solution)/shard_map/pallas_call | solution.py:578
  139.9 0.0 copy-done.8
  139.9 3.6 %shard_map.117 = bf16[4,16,32,128]{3,2,1,0:T(8,128)(2,1)} custom-call(bf16[4,18,32,128]{3,2,1,0:T(8,128)(2,1)} %get-tuple-element.28.grad_ref, bf16[4,16,32,128]{3,2,1,0:T(8,128)(2,1)S(1)} %bitcast.21, bf16[3,3,128,128]{3,2,1,0:T(8,128)(2,1)S(1)} %copy-done.8), custom_call_target="tpu_custom_call" | custom-call | flops 603979776 | bytes 1933312 | tf_op jit(solution)/shard_map/pallas_call | solution.py:578
  143.5 4.9 %all-to-all-done.4.got_ref = bf16[32,56,128]{2,1,0:T(8,128)(2,1)S(1)} async-done(((bf16[32,56,128]{2,1,0:T(8,128)(2,1)}), bf16[32,56,128]{2,1,0:T(8,128)(2,1)S(1)}, u32[]{:S(2)}, u32[]{:S(2)}) %all-to-all-start.4) | async-done | bytes 458784 | tf_op jit(solution)/shard_map/all_to_all | solution.py:739
  148.4 0.9 shard_map.120
  (5 shorter events, 0.1 us)
Async XLA Ops:
  1.6 14.2 %copy-start.2 = (bf16[1,4,16,32,128]{4,3,2,1,0:T(8,128)(2,1)S(1)}, bf16[1,4,16,32,128]{4,3,2,1,0:T(8,128)(2,1)}, u32[]{:S(2)}) copy-start(bf16[1,4,16,32,128]{4,3,2,1,0:T(8,128)(2,1)} %param.6) | copy-start | bytes 1572868
  1.6 14.2 %copy-start.7 = (bf16[3,3,128,128]{3,2,1,0:T(8,128)(2,1)S(1)}, bf16[3,3,128,128]{3,2,1,0:T(8,128)(2,1)}, u32[]{:S(2)}) copy-start(bf16[3,3,128,128]{3,2,1,0:T(8,128)(2,1)} %spatial_ref.7) | copy-start | bytes 884740
  1.6 12.0 %collective-permute-start.1 = (bf16[8,2,32,128]{3,2,1,0:T(8,128)(2,1)S(1)}, bf16[8,2,32,128]{3,2,1,0:T(8,128)(2,1)S(1)}, u32[]{:S(2)}, u32[]{:S(2)}) collective-permute-start(bf16[8,2,32,128]{3,2,1,0:T(8,128)(2,1)S(1)} %pad_maximum_fusion.2), channel_id=1, source_target_pairs={{1,0},{2,1},{3,2},{4,3},{5,4},{6,5},{7,6},{9,8},{10,9},{11,10},{12... | collective-permute-start | bytes 393224 | tf_op jit(solution)/shard_map/ppermute | solution.py:607
  10.6 3.9 %collective-permute-start = (bf16[8,2,32,128]{3,2,1,0:T(8,128)(2,1)S(1)}, bf16[8,2,32,128]{3,2,1,0:T(8,128)(2,1)S(1)}, u32[]{:S(2)}, u32[]{:S(2)}) collective-permute-start(bf16[8,2,32,128]{3,2,1,0:T(8,128)(2,1)S(1)} %pad_maximum_fusion.1), channel_id=1, source_target_pairs={{0,1},{1,2},{2,3},{3,4},{4,5},{5,6},{6,7},{8,9},{9,10},{10,11},{11... | collective-permute-start | bytes 393224 | tf_op jit(solution)/shard_map/ppermute | solution.py:606
  14.4 8.9 %copy-start.5 = (bf16[3,128,128]{2,1,0:T(8,128)(2,1)S(1)}, bf16[3,128,128]{2,1,0:T(8,128)(2,1)}, u32[]{:S(2)}) copy-start(bf16[3,128,128]{2,1,0:T(8,128)(2,1)} %temporal_hbm.3) | copy-start | bytes 294916
  14.5 8.8 %collective-permute-start.2 = (bf16[2,20,32,128]{3,2,1,0:T(8,128)(2,1)S(1)}, bf16[2,20,32,128]{3,2,1,0:T(8,128)(2,1)S(1)}, u32[]{:S(2)}, u32[]{:S(2)}) collective-permute-start(bf16[2,20,32,128]{3,2,1,0:T(8,128)(2,1)S(1)} %pad_maximum_fusion), channel_id=1, source_target_pairs={{0,8},{8,16},{16,24},{24,32},{32,40},{40,48},{48,56},{56,64},{64,7... | collective-permute-start | bytes 983048 | tf_op jit(solution)/shard_map/ppermute | solution.py:611
  17.7 0.8 copy-start.4
  23.3 37.6 %copy-start.1 = (bf16[1,4,16,32,128]{4,3,2,1,0:T(8,128)(2,1)S(1)}, bf16[1,4,16,32,128]{4,3,2,1,0:T(8,128)(2,1)}, u32[]{:S(2)}) copy-start(bf16[1,4,16,32,128]{4,3,2,1,0:T(8,128)(2,1)} %param.11) | copy-start | bytes 1572868
  23.3 37.6 %copy-start.9 = (f32[128]{0:T(128)S(1)}, f32[128]{0:T(128)}, u32[]{:S(2)}) copy-start(f32[128]{0:T(128)} %param.9) | copy-start | bytes 1540
  23.3 37.6 %copy-start.10 = (f32[128]{0:T(128)S(1)}, f32[128]{0:T(128)}, u32[]{:S(2)}) copy-start(f32[128]{0:T(128)} %param.10) | copy-start | bytes 1540
  25.7 37.3 %copy-start = (f32[4,18,32,128]{3,2,1,0:T(8,128)}, f32[4,18,32,128]{3,2,1,0:T(8,128)S(1)}, u32[]{:S(2)}) copy-start(f32[4,18,32,128]{3,2,1,0:T(8,128)S(1)} %get-tuple-element.22.mixed_ref.mixed_hbm) | copy-start | bytes 3538948
  25.7 35.2 %all-to-all-start = ((f32[128,2,128]{2,1,0:T(2,128)}), f32[128,2,128]{2,1,0:T(2,128)S(1)}, u32[]{:S(2)}, u32[]{:S(2)}) async-start(f32[128,2,128]{2,1,0:T(2,128)} %bitcast.3), calls=%async_computation | async-start | bytes 262144 | tf_op jit(solution)/shard_map/all_to_all | solution.py:647
  45.8 28.8 %collective-permute-start.3 = (bf16[4,20,32,128]{3,2,1,0:T(8,128)(2,1)}, bf16[4,20,32,128]{3,2,1,0:T(8,128)(2,1)}, u32[]{:S(2)}, u32[]{:S(2)}) collective-permute-start(bf16[4,20,32,128]{3,2,1,0:T(8,128)(2,1)} %maximum_maximum_fusion), channel_id=1, source_target_pairs={{8,0},{16,8},{24,16},{32,24},{40,32},{48,40},{56,48},{64,56},{72,6... | collective-permute-start | bytes 1966088 | tf_op jit(solution)/shard_map/ppermute | solution.py:620
  63.1 23.4 %all-to-all-start.1 = ((f32[128,2,128]{2,1,0:T(2,128)}), f32[128,2,128]{2,1,0:T(2,128)S(1)}, u32[]{:S(2)}, u32[]{:S(2)}) async-start(f32[128,2,128]{2,1,0:T(2,128)} %bitcast.8), calls=%async_computation.1 | async-start | bytes 262144 | tf_op jit(solution)/shard_map/all_to_all | solution.py:681
  77.8 8.7 %copy-start.6 = (bf16[3,128,128]{2,1,0:T(8,128)(2,1)S(1)}, bf16[3,128,128]{2,1,0:T(8,128)(2,1)}, u32[]{:S(2)}) copy-start(bf16[3,128,128]{2,1,0:T(8,128)(2,1)} %temporal_hbm.3) | copy-start | bytes 294916
  108.9 28.4 %copy-start.3 = (bf16[1,4,16,32,128]{4,3,2,1,0:T(8,128)(2,1)S(1)}, bf16[1,4,16,32,128]{4,3,2,1,0:T(8,128)(2,1)}, u32[]{:S(2)}) copy-start(bf16[1,4,16,32,128]{4,3,2,1,0:T(8,128)(2,1)} %param.6) | copy-start | bytes 1572868
  130.0 9.9 %copy-start.8 = (bf16[3,3,128,128]{3,2,1,0:T(8,128)(2,1)S(1)}, bf16[3,3,128,128]{3,2,1,0:T(8,128)(2,1)}, u32[]{:S(2)}) copy-start(bf16[3,3,128,128]{3,2,1,0:T(8,128)(2,1)} %spatial_ref.7) | copy-start | bytes 884740
  130.0 18.4 %all-to-all-start.4 = ((bf16[32,56,128]{2,1,0:T(8,128)(2,1)}), bf16[32,56,128]{2,1,0:T(8,128)(2,1)S(1)}, u32[]{:S(2)}, u32[]{:S(2)}) async-start(bf16[32,56,128]{2,1,0:T(8,128)(2,1)} %shard_map.119), calls=%async_computation.4 | async-start | bytes 917504 | tf_op jit(solution)/shard_map/all_to_all | solution.py:739

commit v8 on v7

--- a/solution.py
+++ b/solution.py
@@ -292,7 +292,7 @@
             )
 
         zero = jnp.zeros((8, TILE), jnp.float32)
-        a, b = lax.fori_loop(0, rows // step, some, (zero, zero), unroll=2)
+        a, b = lax.fori_loop(0, rows // step, some, (zero, zero), unroll=4)
         firsts.append(a.sum(0, keepdims=True))
         seconds.append(b.sum(0, keepdims=True))
     put_payload(out_ref, [a * gain for a in firsts], [b * gain for b in seconds])
@@ -302,7 +302,7 @@
 
 
 def sigmoid(value):
-    return 0.5 + 0.5 * jnp.tanh(0.5 * value)
+    return 1.0 / (1.0 + jnp.exp(-value))
 
 
 def normalised(mixed, mean, inv_std, gain, shift):
@@ -483,7 +483,7 @@
             mixed_grad_ref[f, at] = grad.astype(jnp.bfloat16).reshape(3, columns, TILE)
             return 0
 
-        lax.fori_loop(0, ext // 3, some, 0, unroll=3)
+        lax.fori_loop(0, ext // 3, some, 0, unroll=6)
     copies[last].wait()
     back = jnp.concatenate([temporal_ref[k] for k in range(3)], axis=1)
     leaving = []

time: 150 us -> 150 us (level)
  no operation moved by 1% of the time
where the time goes in v8:
time: 150 us; the launch traced here: 149 us
  starting transfers between devices  47.3 us (32%)
  blocking collectives  38.4 us (26%)
  waiting for transfers between devices  29.5 us (20%)
  Pallas kernels  29.3 us (20%)
  local copies, waits for them, and re-layouts  3 us (2%)
    pallas_call x12, Pallas kernels, call(): pl.pallas_call(body, out_shape=[*outs, *far_outs], in_specs=[near] * len(...  29.3 us
    all_to_all x2, starting transfers between devices, shards(): got = lax.all_to_all(payload, share, 0, 0, tiled=True)  26.6 us
    all_to_all x1, blocking collectives, shards(): partial = lax.all_to_all(partial, 'tm', 0, 0, tiled=True)  20.2 us
    all_to_all x2, waiting for transfers between devices, shards(): got = lax.all_to_all(payload, share, 0, 0, tiled=True)  19.2 us
    all_to_all x1, blocking collectives, shards(): partial = lax.all_to_all(partial, ends, 0, 0, tiled=True)  18.1 us
    ppermute x1, starting transfers between devices, shards(): lax.ppermute(jnp.concatenate([x[:, :2], cot[:, :2]], 0), 'height', down)  8.88 us
    all_to_all x1, starting transfers between devices, shards(): sums = lax.all_to_all(partial, ends, 0, 0, tiled=True)  7.31 us
    all_to_all x1, waiting for transfers between devices, shards(): sums = lax.all_to_all(partial, ends, 0, 0, tiled=True)  4.8 us
  transfers between devices with their start and end apart: 7, of which 5 were waited for; matrix products, arithmetic and copies ran while one was open for 1% of the time, Pallas kernels for 14%

profile of v8, /device:TPU:1, one launch (start us, length us, event | category | flops | bytes accessed | tf_op | source)
XLA Modules:
  0.0 149.3 jit_solution(1305552388171487031)
XLA Ops:
  0.6 1.0 fusion
  1.6 0.0 copy-start.2
  1.6 0.0 copy-start.7
  1.6 8.9 %collective-permute-start.1 = (bf16[8,2,32,128]{3,2,1,0:T(8,128)(2,1)S(1)}, bf16[8,2,32,128]{3,2,1,0:T(8,128)(2,1)S(1)}, u32[]{:S(2)}, u32[]{:S(2)}) collective-permute-start(bf16[8,2,32,128]{3,2,1,0:T(8,128)(2,1)S(1)} %pad_maximum_fusion.2), channel_id=1, source_target_pairs={{1,0},{2,1},{3,2},{4,3},{5,4},{6,5},{7,6},{9,8},{10,9},{11,10},{12... | collective-permute-start | bytes 393224 | tf_op jit(solution)/shard_map/ppermute | solution.py:607
  10.6 1.9 %collective-permute-start = (bf16[8,2,32,128]{3,2,1,0:T(8,128)(2,1)S(1)}, bf16[8,2,32,128]{3,2,1,0:T(8,128)(2,1)S(1)}, u32[]{:S(2)}, u32[]{:S(2)}) collective-permute-start(bf16[8,2,32,128]{3,2,1,0:T(8,128)(2,1)S(1)} %pad_maximum_fusion.1), channel_id=1, source_target_pairs={{0,1},{1,2},{2,3},{3,4},{4,5},{5,6},{6,7},{8,9},{9,10},{10,11},{11... | collective-permute-start | bytes 393224 | tf_op jit(solution)/shard_map/ppermute | solution.py:606
  12.5 1.2 slice_bitcast_fusion.1
  13.7 0.0 collective-permute-done.1.after_ref.after_hbm
  13.7 0.7 collective-permute-done.before_ref.before_hbm
  14.4 0.0 copy-start.5
  14.5 1.3 collective-permute-start.2
  15.8 0.0 copy-done.2
  15.8 0.0 copy-done.7
  15.8 1.9 %shard_map.109 = (bf16[4,18,32,128]{3,2,1,0:T(8,128)(2,1)S(1)}, bf16[4,18,32,128]{3,2,1,0:T(8,128)(2,1)S(1)}) custom-call(bf16[4,16,32,128]{3,2,1,0:T(8,128)(2,1)S(1)} %bitcast.24, bf16[8,2,32,128]{3,2,1,0:T(8,128)(2,1)S(1)} %collective-permute-done.before_ref.before_hbm, bf16[8,2,32,128]{3,2,1,0:T(8,128)(2,1)S(1)} %collective-permute-done.1.after_ref.after_hbm, ...), custom_call_target="tpu_custom_call" | custom-call | flops 679477248 | bytes 2260992 | tf_op jit(solution)/shard_map/pallas_call | solution.py:578
  17.7 0.0 copy-start.4
  17.7 0.8 copy-done.4
  18.5 4.8 %collective-permute-done.2.prev_ref = bf16[2,20,32,128]{3,2,1,0:T(8,128)(2,1)S(1)} collective-permute-done((bf16[2,20,32,128]{3,2,1,0:T(8,128)(2,1)S(1)}, bf16[2,20,32,128]{3,2,1,0:T(8,128)(2,1)S(1)}, u32[]{:S(2)}, u32[]{:S(2)}) %collective-permute-start.2) | collective-permute-done | bytes 327712 | tf_op jit(solution)/shard_map/ppermute | solution.py:611
  23.3 0.0 copy-done.5
  23.3 0.0 copy-start.1
  23.3 0.0 copy-start.9
  23.3 0.0 copy-start.10
  23.3 2.4 %shard_map.110 = (f32[4,18,32,128]{3,2,1,0:T(8,128)S(1)}, f32[256,128]{1,0:T(8,128)}) custom-call(bf16[4,18,32,128]{3,2,1,0:T(8,128)(2,1)S(1)} %get-tuple-element.20.feature_ref, bf16[2,20,32,128]{3,2,1,0:T(8,128)(2,1)S(1)} %collective-permute-done.2.prev_ref, bf16[3,3,128,128]{3,2,1,0:T(8,128)(2,1)S(1)} %copy-done.7, bf16[3,128,128]{2,1,0:T(8,128)(2,1)S(1)} %copy-done.5), custom_call_target="tpu_custom_call" | custom-call | flops 679477248 | bytes 2621440 | tf_op jit(solution)/shard_map/pallas_call | solution.py:578
  25.7 0.0 copy-start
  25.7 19.2 %all-to-all-start = ((f32[128,2,128]{2,1,0:T(2,128)}), f32[128,2,128]{2,1,0:T(2,128)S(1)}, u32[]{:S(2)}, u32[]{:S(2)}) async-start(f32[128,2,128]{2,1,0:T(2,128)} %bitcast.3), calls=%async_computation | async-start | bytes 262144 | tf_op jit(solution)/shard_map/all_to_all | solution.py:647
  44.9 0.9 maximum_maximum_fusion
  45.8 1.3 collective-permute-start.3
  47.1 13.8 %all-to-all-done = f32[128,2,128]{2,1,0:T(2,128)S(1)} async-done(((f32[128,2,128]{2,1,0:T(2,128)}), f32[128,2,128]{2,1,0:T(2,128)S(1)}, u32[]{:S(2)}, u32[]{:S(2)}) %all-to-all-start) | async-done | bytes 131104 | tf_op jit(solution)/shard_map/all_to_all | solution.py:647
  60.9 0.0 copy-done.1
  60.9 0.0 copy-done.9
  60.9 0.0 copy-done.10
  60.9 2.1 %shard_map.111 = (f32[144,128]{1,0:T(8,128)S(1)}, f32[256,128]{1,0:T(8,128)}) custom-call(f32[256,128]{1,0:T(8,128)S(1)} %bitcast.27, f32[4,18,32,128]{3,2,1,0:T(8,128)S(1)} %get-tuple-element.22.mixed_ref.mixed_hbm, bf16[4,16,32,128]{3,2,1,0:T(8,128)(2,1)S(1)} %bitcast.19, f32[1,128]{1,0:T(1,128)S(1)} %bitcast.28, f32[1,128]{1,0:T(1,128)S(1)} %bitcast.31), custom_call_target="tpu_custom_call" | custom-call | bytes 2040832 | tf_op jit(solution)/shard_map/pallas_call | solution.py:578
  63.0 0.0 copy-done
  63.0 7.4 %all-to-all-start.1 = ((f32[128,2,128]{2,1,0:T(2,128)}), f32[128,2,128]{2,1,0:T(2,128)S(1)}, u32[]{:S(2)}, u32[]{:S(2)}) async-start(f32[128,2,128]{2,1,0:T(2,128)} %bitcast.8), calls=%async_computation.1 | async-start | bytes 262144 | tf_op jit(solution)/shard_map/all_to_all | solution.py:681
  70.4 4.2 %shard_map.115 = (bf16[384,2048]{1,0:T(8,128)(2,1)}, bf16[128,3072]{1,0:T(8,128)(2,1)}) custom-call(bf16[4,16,32,128]{3,2,1,0:T(8,128)(2,1)} %bitcast.23, bf16[8,2,32,128]{3,2,1,0:T(8,128)(2,1)S(1)} %collective-permute-done.before_ref.before_hbm, bf16[8,2,32,128]{3,2,1,0:T(8,128)(2,1)S(1)} %collective-permute-done.1.after_ref.after_hbm, ...), custom_call_target="tpu_custom_call" | custom-call | flops 679477248 | bytes 4358144 | tf_op jit(solution)/shard_map/pallas_call | solution.py:578
  74.6 0.0 collective-permute-done.3.next_hbm
  74.6 3.2 %shard_map.113.mixed_next_hbm = f32[2,18,32,128]{3,2,1,0:T(8,128)} custom-call(bf16[4,20,32,128]{3,2,1,0:T(8,128)(2,1)} %collective-permute-done.3.next_hbm, bf16[4,18,32,128]{3,2,1,0:T(8,128)(2,1)} %copy-done.4, bf16[3,3,128,128]{3,2,1,0:T(8,128)(2,1)} %spatial_ref.7, bf16[3,128,128]{2,1,0:T(8,128)(2,1)} %temporal_hbm.3), custom_call_target="tpu_custom_call" | custom-call | flops 339738624 | bytes 2228224 | tf_op jit(solution)/shard_map/pallas_call | solution.py:578
  77.7 0.0 copy-start.6
  77.7 3.2 %shard_map.114.scaled_hbm = f32[6,18,32,128]{3,2,1,0:T(8,128)} custom-call(f32[144,128]{1,0:T(8,128)S(1)} %get-tuple-element.23.stats_ref, f32[1,128]{1,0:T(1,128)S(1)} %bitcast.29, f32[1,128]{1,0:T(1,128)S(1)} %bitcast.32, f32[4,18,32,128]{3,2,1,0:T(8,128)} %copy-done, f32[2,18,32,128]{3,2,1,0:T(8,128)} %shard_map.113.mixed_next_hbm, ...), custom_call_target="tpu_custom_call" | custom-call | bytes 5055488 | tf_op jit(solution)/shard_map/pallas_call | solution.py:578
  81.0 5.4 %all-to-all-done.1 = f32[128,2,128]{2,1,0:T(2,128)S(1)} async-done(((f32[128,2,128]{2,1,0:T(2,128)}), f32[128,2,128]{2,1,0:T(2,128)S(1)}, u32[]{:S(2)}, u32[]{:S(2)}) %all-to-all-start.1) | async-done | bytes 131104 | tf_op jit(solution)/shard_map/all_to_all | solution.py:681
  86.4 0.0 copy-done.6
  86.4 4.3 %shard_map.116 = (bf16[32,56,128]{2,1,0:T(8,128)(2,1)S(1)}, bf16[4,18,32,128]{3,2,1,0:T(8,128)(2,1)}) custom-call(f32[256,128]{1,0:T(8,128)S(1)} %bitcast.26, f32[144,128]{1,0:T(8,128)S(1)} %get-tuple-element.23.stats_ref, f32[4,18,32,128]{3,2,1,0:T(8,128)} %copy-done, f32[2,18,32,128]{3,2,1,0:T(8,128)} %shard_map.113.mixed_next_hbm, ...), custom_call_target="tpu_custom_call" | custom-call | flops 1207959552 | bytes 7249920 | tf_op jit(solution)/shard_map/pallas_call | solution.py:578
  90.7 18.1 %all_to_all.37.got_ref = bf16[32,56,128]{2,1,0:T(8,128)(2,1)S(1)} all-to-all(bf16[32,56,128]{2,1,0:T(8,128)(2,1)S(1)} %get-tuple-element.29), channel_id=1, replica_groups=mesh['rep'=4,'tm'=16,'height'=8] {'rep','height'}, dimensions={0} | all-to-all | bytes 917504 | tf_op jit(solution)/shard_map/all_to_all | solution.py:727
  108.9 0.0 copy-start.3
  108.9 0.1 shard_map.118
  109.0 20.2 %all_to_all.38.got_ref = bf16[16,56,128]{2,1,0:T(8,128)(2,1)S(1)} all-to-all(bf16[16,56,128]{2,1,0:T(8,128)(2,1)S(1)} %shard_map.118), channel_id=1, replica_groups=mesh['rep'=4,'tm'=16,'height'=8] {'tm'}, dimensions={0} | all-to-all | bytes 458752 | tf_op jit(solution)/shard_map/all_to_all | solution.py:737
  129.2 0.8 shard_map.119
  130.0 0.0 copy-start.8
  130.0 7.3 %all-to-all-start.4 = ((bf16[32,56,128]{2,1,0:T(8,128)(2,1)}), bf16[32,56,128]{2,1,0:T(8,128)(2,1)S(1)}, u32[]{:S(2)}, u32[]{:S(2)}) async-start(bf16[32,56,128]{2,1,0:T(8,128)(2,1)} %shard_map.119), calls=%async_computation.4 | async-start | bytes 917504 | tf_op jit(solution)/shard_map/all_to_all | solution.py:739
  137.3 0.0 copy-done.3
  137.3 2.6 %shard_map.112 = bf16[4,16,32,128]{3,2,1,0:T(8,128)(2,1)} custom-call(f32[144,128]{1,0:T(8,128)S(1)} %get-tuple-element.23.stats_ref, f32[4,18,32,128]{3,2,1,0:T(8,128)} %copy-done, bf16[4,16,32,128]{3,2,1,0:T(8,128)(2,1)S(1)} %bitcast.25, f32[1,128]{1,0:T(1,128)S(1)} %bitcast.30, f32[1,128]{1,0:T(1,128)S(1)} %bitcast.33), custom_call_target="tpu_custom_call" | custom-call | bytes 2302976 | tf_op jit(solution)/shard_map/pallas_call | solution.py:578
  140.0 0.0 copy-done.8
  140.0 3.6 %shard_map.117 = bf16[4,16,32,128]{3,2,1,0:T(8,128)(2,1)} custom-call(bf16[4,18,32,128]{3,2,1,0:T(8,128)(2,1)} %get-tuple-element.28.grad_ref, bf16[4,16,32,128]{3,2,1,0:T(8,128)(2,1)S(1)} %bitcast.21, bf16[3,3,128,128]{3,2,1,0:T(8,128)(2,1)S(1)} %copy-done.8), custom_call_target="tpu_custom_call" | custom-call | flops 603979776 | bytes 1933312 | tf_op jit(solution)/shard_map/pallas_call | solution.py:578
  143.6 4.8 %all-to-all-done.4.got_ref = bf16[32,56,128]{2,1,0:T(8,128)(2,1)S(1)} async-done(((bf16[32,56,128]{2,1,0:T(8,128)(2,1)}), bf16[32,56,128]{2,1,0:T(8,128)(2,1)S(1)}, u32[]{:S(2)}, u32[]{:S(2)}) %all-to-all-start.4) | async-done | bytes 458784 | tf_op jit(solution)/shard_map/all_to_all | solution.py:739
  148.4 0.9 shard_map.120
  (5 shorter events, 0.1 us)
Async XLA Ops:
  1.6 14.2 %copy-start.2 = (bf16[1,4,16,32,128]{4,3,2,1,0:T(8,128)(2,1)S(1)}, bf16[1,4,16,32,128]{4,3,2,1,0:T(8,128)(2,1)}, u32[]{:S(2)}) copy-start(bf16[1,4,16,32,128]{4,3,2,1,0:T(8,128)(2,1)} %param.6) | copy-start | bytes 1572868
  1.6 14.2 %copy-start.7 = (bf16[3,3,128,128]{3,2,1,0:T(8,128)(2,1)S(1)}, bf16[3,3,128,128]{3,2,1,0:T(8,128)(2,1)}, u32[]{:S(2)}) copy-start(bf16[3,3,128,128]{3,2,1,0:T(8,128)(2,1)} %spatial_ref.7) | copy-start | bytes 884740
  1.6 12.0 %collective-permute-start.1 = (bf16[8,2,32,128]{3,2,1,0:T(8,128)(2,1)S(1)}, bf16[8,2,32,128]{3,2,1,0:T(8,128)(2,1)S(1)}, u32[]{:S(2)}, u32[]{:S(2)}) collective-permute-start(bf16[8,2,32,128]{3,2,1,0:T(8,128)(2,1)S(1)} %pad_maximum_fusion.2), channel_id=1, source_target_pairs={{1,0},{2,1},{3,2},{4,3},{5,4},{6,5},{7,6},{9,8},{10,9},{11,10},{12... | collective-permute-start | bytes 393224 | tf_op jit(solution)/shard_map/ppermute | solution.py:607
  10.6 3.9 %collective-permute-start = (bf16[8,2,32,128]{3,2,1,0:T(8,128)(2,1)S(1)}, bf16[8,2,32,128]{3,2,1,0:T(8,128)(2,1)S(1)}, u32[]{:S(2)}, u32[]{:S(2)}) collective-permute-start(bf16[8,2,32,128]{3,2,1,0:T(8,128)(2,1)S(1)} %pad_maximum_fusion.1), channel_id=1, source_target_pairs={{0,1},{1,2},{2,3},{3,4},{4,5},{5,6},{6,7},{8,9},{9,10},{10,11},{11... | collective-permute-start | bytes 393224 | tf_op jit(solution)/shard_map/ppermute | solution.py:606
  14.4 8.9 %copy-start.5 = (bf16[3,128,128]{2,1,0:T(8,128)(2,1)S(1)}, bf16[3,128,128]{2,1,0:T(8,128)(2,1)}, u32[]{:S(2)}) copy-start(bf16[3,128,128]{2,1,0:T(8,128)(2,1)} %temporal_hbm.3) | copy-start | bytes 294916
  14.5 8.8 %collective-permute-start.2 = (bf16[2,20,32,128]{3,2,1,0:T(8,128)(2,1)S(1)}, bf16[2,20,32,128]{3,2,1,0:T(8,128)(2,1)S(1)}, u32[]{:S(2)}, u32[]{:S(2)}) collective-permute-start(bf16[2,20,32,128]{3,2,1,0:T(8,128)(2,1)S(1)} %pad_maximum_fusion), channel_id=1, source_target_pairs={{0,8},{8,16},{16,24},{24,32},{32,40},{40,48},{48,56},{56,64},{64,7... | collective-permute-start | bytes 983048 | tf_op jit(solution)/shard_map/ppermute | solution.py:611
  17.7 0.8 copy-start.4
  23.3 37.6 %copy-start.1 = (bf16[1,4,16,32,128]{4,3,2,1,0:T(8,128)(2,1)S(1)}, bf16[1,4,16,32,128]{4,3,2,1,0:T(8,128)(2,1)}, u32[]{:S(2)}) copy-start(bf16[1,4,16,32,128]{4,3,2,1,0:T(8,128)(2,1)} %param.11) | copy-start | bytes 1572868
  23.3 37.6 %copy-start.9 = (f32[128]{0:T(128)S(1)}, f32[128]{0:T(128)}, u32[]{:S(2)}) copy-start(f32[128]{0:T(128)} %param.9) | copy-start | bytes 1540
  23.3 37.6 %copy-start.10 = (f32[128]{0:T(128)S(1)}, f32[128]{0:T(128)}, u32[]{:S(2)}) copy-start(f32[128]{0:T(128)} %param.10) | copy-start | bytes 1540
  25.7 37.3 %copy-start = (f32[4,18,32,128]{3,2,1,0:T(8,128)}, f32[4,18,32,128]{3,2,1,0:T(8,128)S(1)}, u32[]{:S(2)}) copy-start(f32[4,18,32,128]{3,2,1,0:T(8,128)S(1)} %get-tuple-element.22.mixed_ref.mixed_hbm) | copy-start | bytes 3538948
  25.7 35.2 %all-to-all-start = ((f32[128,2,128]{2,1,0:T(2,128)}), f32[128,2,128]{2,1,0:T(2,128)S(1)}, u32[]{:S(2)}, u32[]{:S(2)}) async-start(f32[128,2,128]{2,1,0:T(2,128)} %bitcast.3), calls=%async_computation | async-start | bytes 262144 | tf_op jit(solution)/shard_map/all_to_all | solution.py:647
  45.8 28.7 %collective-permute-start.3 = (bf16[4,20,32,128]{3,2,1,0:T(8,128)(2,1)}, bf16[4,20,32,128]{3,2,1,0:T(8,128)(2,1)}, u32[]{:S(2)}, u32[]{:S(2)}) collective-permute-start(bf16[4,20,32,128]{3,2,1,0:T(8,128)(2,1)} %maximum_maximum_fusion), channel_id=1, source_target_pairs={{8,0},{16,8},{24,16},{32,24},{40,32},{48,40},{56,48},{64,56},{72,6... | collective-permute-start | bytes 1966088 | tf_op jit(solution)/shard_map/ppermute | solution.py:620
  63.0 23.4 %all-to-all-start.1 = ((f32[128,2,128]{2,1,0:T(2,128)}), f32[128,2,128]{2,1,0:T(2,128)S(1)}, u32[]{:S(2)}, u32[]{:S(2)}) async-start(f32[128,2,128]{2,1,0:T(2,128)} %bitcast.8), calls=%async_computation.1 | async-start | bytes 262144 | tf_op jit(solution)/shard_map/all_to_all | solution.py:681
  77.7 8.7 %copy-start.6 = (bf16[3,128,128]{2,1,0:T(8,128)(2,1)S(1)}, bf16[3,128,128]{2,1,0:T(8,128)(2,1)}, u32[]{:S(2)}) copy-start(bf16[3,128,128]{2,1,0:T(8,128)(2,1)} %temporal_hbm.3) | copy-start | bytes 294916
  108.9 28.4 %copy-start.3 = (bf16[1,4,16,32,128]{4,3,2,1,0:T(8,128)(2,1)S(1)}, bf16[1,4,16,32,128]{4,3,2,1,0:T(8,128)(2,1)}, u32[]{:S(2)}) copy-start(bf16[1,4,16,32,128]{4,3,2,1,0:T(8,128)(2,1)} %param.6) | copy-start | bytes 1572868
  130.0 9.9 %copy-start.8 = (bf16[3,3,128,128]{3,2,1,0:T(8,128)(2,1)S(1)}, bf16[3,3,128,128]{3,2,1,0:T(8,128)(2,1)}, u32[]{:S(2)}) copy-start(bf16[3,3,128,128]{3,2,1,0:T(8,128)(2,1)} %spatial_ref.7) | copy-start | bytes 884740
  130.0 18.4 %all-to-all-start.4 = ((bf16[32,56,128]{2,1,0:T(8,128)(2,1)}), bf16[32,56,128]{2,1,0:T(8,128)(2,1)S(1)}, u32[]{:S(2)}, u32[]{:S(2)}) async-start(bf16[32,56,128]{2,1,0:T(8,128)(2,1)} %shard_map.119), calls=%async_computation.4 | async-start | bytes 917504 | tf_op jit(solution)/shard_map/all_to_all | solution.py:739
